TPU v7x, 128 devices: a whole 4x4x4 slice. The times are simulated.
128 devices in a mesh: lat: 8 (over z_hi, x), lon: 16 (over y, z_lo, core).
Axes of the slice: x: 4, y: 4, z: 4 (z_hi: 2, z_lo: 2; z = z_hi * 2 + z_lo), core: 2. Of those that a mesh axis runs over, the one named last changes fastest.
Arguments:
- features: bfloat16 [128, 3072, 128], P('lat', 'lon'), may hold values from -6 to 6
- cotangent: bfloat16 [128, 3072, 128], P('lat', 'lon'), may hold values from -6 to 6
- w_first: bfloat16 [1152, 128], P(('lat', 'lon')), may hold values from -0.1875 to 0.1875
- w_second: bfloat16 [1152, 128], P(('lat', 'lon')), may hold values from -0.1875 to 0.1875
Outputs:
- grad_features: bfloat16 [128, 3072, 128], P('lat', 'lon')
- grad_first: float32 [1152, 128], P(('lat', 'lon'))
- grad_second: float32 [1152, 128], P(('lat', 'lon'))
All inputs are finite; a program needn't handle non-finite values.
Results may differ from a plain program's by a relative error of at most 0.0033.
Values may be sent and summed in bfloat16 or wider, within the bound.
No kernel may reach another device: no remote copies, remote signals or barrier semaphores. Data moves between devices by JAX's collectives and lax.ppermute only.
A program may use at most 64 MiB of HBM per device.

v0:
```python
import jax
import jax.numpy as jnp
from jax import lax
from jax.sharding import PartitionSpec as P


def padded_2(block, sides, width, periodic):
    for axis, dim in sides:
        count = lax.axis_size(axis)
        forward = [(i, i + 1) for i in range(count - 1)]
        if periodic:
            forward.append((count - 1, 0))
        backward = [(target, source) for source, target in forward]
        low = lax.ppermute(
            lax.slice_in_dim(block, block.shape[dim] - width, None, axis=dim), axis, forward
        )
        high = lax.ppermute(lax.slice_in_dim(block, 0, width, axis=dim), axis, backward)
        block = jnp.concatenate([low, block, high], axis=dim)
    return block


def add_rims(field, width):
    field = padded_2(field, (("lon", 1),), width, True)
    return padded_2(field, (("lat", 0),), width, False)


def forward_conv(padded, weight, rows, cols):
    chans = padded.shape[2]
    total = jnp.zeros((rows * cols, weight.shape[1]), jnp.float32)
    for tap in range(9):
        shift_r, shift_c = divmod(tap, 3)
        piece = padded[shift_r : shift_r + rows, shift_c : shift_c + cols].reshape(-1, chans)
        total = total + jnp.dot(
            piece, weight[tap * chans : (tap + 1) * chans], preferred_element_type=jnp.float32
        )
    return total.reshape(rows, cols, -1)


def transpose_conv(padded, weight, rows, cols):
    chans = weight.shape[1]
    inner = weight.shape[0] // 9
    total = jnp.zeros((rows * cols, inner), jnp.float32)
    for tap in range(9):
        shift_r, shift_c = divmod(tap, 3)
        piece = padded[2 - shift_r : 2 - shift_r + rows, 2 - shift_c : 2 - shift_c + cols].reshape(
            -1, chans
        )
        block = weight[tap * inner : (tap + 1) * inner]
        total = total + lax.dot_general(
            piece, block, (((1,), (1,)), ((), ())), preferred_element_type=jnp.float32
        )
    return total.reshape(rows, cols, -1)


def weight_grad(padded, grad_out, rows, cols):
    chans = padded.shape[2]
    flat_grad = grad_out.reshape(-1, grad_out.shape[2])
    blocks = []
    for tap in range(9):
        shift_r, shift_c = divmod(tap, 3)
        piece = padded[shift_r : shift_r + rows, shift_c : shift_c + cols].reshape(-1, chans)
        blocks.append(
            lax.dot_general(
                piece, flat_grad, (((0,), (0,)), ((), ())), preferred_element_type=jnp.float32
            )
        )
    return jnp.concatenate(blocks, 0)


def local(features, cotangent, w_first, w_second):
    rows, cols, chans = (features.shape[0], features.shape[1], features.shape[2])
    kernel_one, kernel_two = (
        lax.all_gather(w_first, ("lat", "lon"), axis=0, tiled=True),
        lax.all_gather(w_second, ("lat", "lon"), axis=0, tiled=True),
    )
    feat_pad = add_rims(features, 1)
    grad_pad = add_rims(cotangent, 1)
    pre = forward_conv(feat_pad, kernel_one, rows, cols)
    act_pad = add_rims(jax.nn.silu(pre).astype(jnp.bfloat16), 1)
    second_terms = weight_grad(act_pad, cotangent, rows, cols)
    back_act = transpose_conv(grad_pad, kernel_two, rows, cols)
    sigma = jax.nn.sigmoid(pre)
    back_pre = (back_act * sigma * (1.0 + pre * (1.0 - sigma))).astype(jnp.bfloat16)
    first_terms = weight_grad(feat_pad, back_pre, rows, cols)
    back_pad = add_rims(back_pre, 1)
    grad_features = (
        cotangent.astype(jnp.float32) + transpose_conv(back_pad, kernel_one, rows, cols)
    ).astype(jnp.bfloat16)
    grad_first, grad_second = (
        lax.psum_scatter(first_terms, ("lat", "lon"), scatter_dimension=0, tiled=True),
        lax.psum_scatter(second_terms, ("lat", "lon"), scatter_dimension=0, tiled=True),
    )
    return (grad_features, grad_first, grad_second)


def solution(mesh):
    in_specs = (
        P("lat", "lon", None),
        P("lat", "lon", None),
        P(("lat", "lon"), None),
        P(("lat", "lon"), None),
    )
    out_specs = (P("lat", "lon", None), P(("lat", "lon"), None), P(("lat", "lon"), None))
    return jax.shard_map(local, mesh=mesh, in_specs=in_specs, out_specs=out_specs, check_vma=False)
```

profile of v0, /device:TPU:6, one launch (start us, length us, event | category | flops | bytes accessed | tf_op | source)
XLA Modules:
  0.0 588.0 jit_solution(9573633949376731134)
XLA Ops:
  7.2 0.9 fusion.85
  8.2 3.9 collective-permute-start.1
  12.0 0.8 fusion.86
  12.9 3.8 collective-permute-start.5
  16.8 138.9 %all-gather = bf16[128,9,128]{2,1,0:T(8,128)(2,1)S(1)} all-gather(bf16[1,9,128]{2,1,0:T(8,128)(2,1)} %bitcast.182), channel_id=1, replica_groups=mesh['lat'=8,'lon'=16] {'lat','lon'}, dimensions={0}, use_global_device_ids=true | all-gather | bytes 297216 | tf_op jit(solution)/shard_map/all_gather | solution.py:74
  155.8 153.8 %all-gather.1 = bf16[128,9,128]{2,1,0:T(8,128)(2,1)S(1)} all-gather(bf16[1,9,128]{2,1,0:T(8,128)(2,1)} %bitcast.183), channel_id=1, replica_groups=mesh['lat'=8,'lon'=16] {'lat','lon'}, dimensions={0}, use_global_device_ids=true | all-gather | bytes 297216 | tf_op jit(solution)/shard_map/all_gather | solution.py:73
  309.8 1.5 fusion.38
  311.3 1.5 fusion.56
  312.9 19.6 %collective-permute-start.2 = (bf16[1,194,128]{2,1,0:T(8,128)(2,1)S(1)}, bf16[1,194,128]{2,1,0:T(8,128)(2,1)S(1)}, u32[]{:S(2)}, u32[]{:S(2)}) collective-permute-start(bf16[1,194,128]{2,1,0:T(8,128)(2,1)S(1)} %get-tuple-element.35), channel_id=1, source_target_pairs={{16,0},{32,16},{48,32},{64,48},{80,64},{96,80},{112,96},{17,1},{33... | collective-permute-start | bytes 149000 | tf_op jit(solution)/shard_map/ppermute | solution.py:17
  332.5 2.0 collective-permute-start.3
  334.5 3.9 collective-permute-start.6
  338.5 19.9 %collective-permute-start.7 = (bf16[1,194,128]{2,1,0:T(8,128)(2,1)S(1)}, bf16[1,194,128]{2,1,0:T(8,128)(2,1)S(1)}, u32[]{:S(2)}, u32[]{:S(2)}) collective-permute-start(bf16[1,194,128]{2,1,0:T(8,128)(2,1)S(1)} %get-tuple-element.40), channel_id=1, source_target_pairs={{16,0},{32,16},{48,32},{64,48},{80,64},{96,80},{112,96},{17,1},{33... | collective-permute-start | bytes 149000 | tf_op jit(solution)/shard_map/ppermute | solution.py:17
  358.4 0.4 pad_maximum_fusion.12
  358.8 0.5 pad_maximum_fusion.10
  359.7 1.0 fusion.79
  361.8 1.1 fusion.81
  364.3 1.0 copy-done.3
  367.7 1.0 copy-done.2
  370.2 1.9 fusion.32
  372.1 0.8 multiply_convert_fusion
  373.0 3.8 collective-permute-start.13
  380.7 3.8 collective-permute-start.9
  384.6 18.0 %collective-permute-start.14 = (bf16[1,194,128]{2,1,0:T(8,128)(2,1)S(1)}, bf16[1,194,128]{2,1,0:T(8,128)(2,1)S(1)}, u32[]{:S(2)}, u32[]{:S(2)}) collective-permute-start(bf16[1,194,128]{2,1,0:T(8,128)(2,1)S(1)} %get-tuple-element.28), channel_id=1, source_target_pairs={{0,16},{16,32},{32,48},{48,64},{64,80},{80,96},{96,112},{1,17},{17... | collective-permute-start | bytes 149000 | tf_op jit(solution)/shard_map/ppermute | solution.py:14
  402.6 5.7 collective-permute-start.15
  408.3 3.9 collective-permute-start.10
  412.3 5.5 collective-permute-start.11
  417.8 1.6 pad_maximum_fusion.8
  419.9 1.0 fusion.14
  420.9 1.0 fusion.13
  421.9 1.0 fusion.12
  423.0 1.1 fusion.11
  424.0 1.0 fusion.10
  425.1 1.0 fusion.9
  426.1 1.0 fusion.8
  427.2 1.0 fusion.7
  428.2 1.0 fusion.6
  429.7 1.6 fusion.78
  431.3 1.5 fusion.62
  432.8 1.4 fusion.77
  434.5 2.1 convolution_add_fusion.5
  437.0 0.7 copy-done.7
  437.8 0.5 copy-done.8
  438.7 0.8 copy-done.6
  439.8 0.8 copy-done.4
  441.3 1.1 add_convert_fusion
  442.4 136.1 %all-reduce.5.cloned.1.call-done = (f32[1152,128]{1,0:T(8,128)}, f32[1152,128]{1,0:T(8,128)}) async-done(((f32[1152,128]{1,0:T(8,128)}, f32[1152,128]{1,0:T(8,128)}), (f32[1152,128]{1,0:T(8,128)}, f32[1152,128]{1,0:T(8,128)})) %all-reduce.5.cloned.1.call-update) | async-done | bytes 1179664
  578.6 1.3 constant_dynamic-slice_fusion
  579.9 1.3 constant_dynamic-slice_fusion.1
  (79 shorter events, 14.2 us)
Async XLA Ops:
  7.2 302.6 %copy-start = (bf16[16,192,128]{2,1,0:T(8,128)(2,1)S(1)}, bf16[16,192,128]{2,1,0:T(8,128)(2,1)}, u32[]{:S(2)}) copy-start(bf16[16,192,128]{2,1,0:T(8,128)(2,1)} %param.5) | copy-start | bytes 2359300
  7.2 571.4 %all-reduce.5.cloned.1.call-start = ((), (), s32[]{:S(2)}) async-start(), calls=%async_computation | async-start | bytes 2359296
  8.1 304.8 %collective-permute-start = (bf16[16,1,128]{2,1,0:T(2,128)(2,1)S(1)}, bf16[16,1,128]{2,1,0:T(2,128)(2,1)S(1)}, u32[]{:S(2)}, u32[]{:S(2)}) collective-permute-start(bf16[16,1,128]{2,1,0:T(2,128)(2,1)S(1)} %get-tuple-element.49), channel_id=1, source_target_pairs={{0,1},{1,2},{2,3},{3,4},{4,5},{5,6},{6,7},{7,8},{8,9},{9,10},{10,1... | collective-permute-start | bytes 12296 | tf_op jit(solution)/shard_map/ppermute | solution.py:14
  8.2 304.7 %collective-permute-start.1 = (bf16[16,1,128]{2,1,0:T(2,128)(2,1)S(1)}, bf16[16,1,128]{2,1,0:T(2,128)(2,1)S(1)}, u32[]{:S(2)}, u32[]{:S(2)}) collective-permute-start(bf16[16,1,128]{2,1,0:T(2,128)(2,1)S(1)} %get-tuple-element.50), channel_id=1, source_target_pairs={{1,0},{2,1},{3,2},{4,3},{5,4},{6,5},{7,6},{8,7},{9,8},{10,9},{11,1... | collective-permute-start | bytes 12296 | tf_op jit(solution)/shard_map/ppermute | solution.py:17
  12.8 321.7 %collective-permute-start.4 = (bf16[16,1,128]{2,1,0:T(2,128)(2,1)S(1)}, bf16[16,1,128]{2,1,0:T(2,128)(2,1)S(1)}, u32[]{:S(2)}, u32[]{:S(2)}) collective-permute-start(bf16[16,1,128]{2,1,0:T(2,128)(2,1)S(1)} %get-tuple-element.53), channel_id=1, source_target_pairs={{0,1},{1,2},{2,3},{3,4},{4,5},{5,6},{6,7},{7,8},{8,9},{9,10},{10,1... | collective-permute-start | bytes 12296 | tf_op jit(solution)/shard_map/ppermute | solution.py:14
  12.9 321.6 %collective-permute-start.5 = (bf16[16,1,128]{2,1,0:T(2,128)(2,1)S(1)}, bf16[16,1,128]{2,1,0:T(2,128)(2,1)S(1)}, u32[]{:S(2)}, u32[]{:S(2)}) collective-permute-start(bf16[16,1,128]{2,1,0:T(2,128)(2,1)S(1)} %get-tuple-element.54), channel_id=1, source_target_pairs={{1,0},{2,1},{3,2},{4,3},{5,4},{6,5},{7,6},{8,7},{9,8},{10,9},{11,1... | collective-permute-start | bytes 12296 | tf_op jit(solution)/shard_map/ppermute | solution.py:17
  309.6 1.7 copy-start.1
  312.9 46.4 %collective-permute-start.2 = (bf16[1,194,128]{2,1,0:T(8,128)(2,1)S(1)}, bf16[1,194,128]{2,1,0:T(8,128)(2,1)S(1)}, u32[]{:S(2)}, u32[]{:S(2)}) collective-permute-start(bf16[1,194,128]{2,1,0:T(8,128)(2,1)S(1)} %get-tuple-element.35), channel_id=1, source_target_pairs={{16,0},{32,16},{48,32},{64,48},{80,64},{96,80},{112,96},{17,1},{33... | collective-permute-start | bytes 149000 | tf_op jit(solution)/shard_map/ppermute | solution.py:17
  332.5 26.9 %collective-permute-start.3 = (bf16[1,194,128]{2,1,0:T(8,128)(2,1)S(1)}, bf16[1,194,128]{2,1,0:T(8,128)(2,1)S(1)}, u32[]{:S(2)}, u32[]{:S(2)}) collective-permute-start(bf16[1,194,128]{2,1,0:T(8,128)(2,1)S(1)} %get-tuple-element.36), channel_id=1, source_target_pairs={{0,16},{16,32},{32,48},{48,64},{64,80},{80,96},{96,112},{1,17},{17... | collective-permute-start | bytes 149000 | tf_op jit(solution)/shard_map/ppermute | solution.py:14
  334.5 26.9 %collective-permute-start.6 = (bf16[1,194,128]{2,1,0:T(8,128)(2,1)S(1)}, bf16[1,194,128]{2,1,0:T(8,128)(2,1)S(1)}, u32[]{:S(2)}, u32[]{:S(2)}) collective-permute-start(bf16[1,194,128]{2,1,0:T(8,128)(2,1)S(1)} %get-tuple-element.39), channel_id=1, source_target_pairs={{0,16},{16,32},{32,48},{48,64},{64,80},{80,96},{96,112},{1,17},{17... | collective-permute-start | bytes 149000 | tf_op jit(solution)/shard_map/ppermute | solution.py:14
  338.5 23.0 %collective-permute-start.7 = (bf16[1,194,128]{2,1,0:T(8,128)(2,1)S(1)}, bf16[1,194,128]{2,1,0:T(8,128)(2,1)S(1)}, u32[]{:S(2)}, u32[]{:S(2)}) collective-permute-start(bf16[1,194,128]{2,1,0:T(8,128)(2,1)S(1)} %get-tuple-element.40), channel_id=1, source_target_pairs={{16,0},{32,16},{48,32},{64,48},{80,64},{96,80},{112,96},{17,1},{33... | collective-permute-start | bytes 149000 | tf_op jit(solution)/shard_map/ppermute | solution.py:17
  364.0 1.4 copy-start.3
  367.3 1.4 copy-start.2
  372.9 11.7 %collective-permute-start.12 = (bf16[16,1,128]{2,1,0:T(2,128)(2,1)S(1)}, bf16[16,1,128]{2,1,0:T(2,128)(2,1)S(1)}, u32[]{:S(2)}, u32[]{:S(2)}) collective-permute-start(bf16[16,1,128]{2,1,0:T(2,128)(2,1)S(1)} %get-tuple-element.41), channel_id=1, source_target_pairs={{0,1},{1,2},{2,3},{3,4},{4,5},{5,6},{6,7},{7,8},{8,9},{9,10},{10,1... | collective-permute-start | bytes 12296 | tf_op jit(solution)/shard_map/ppermute | solution.py:14
  373.0 11.6 %collective-permute-start.13 = (bf16[16,1,128]{2,1,0:T(2,128)(2,1)S(1)}, bf16[16,1,128]{2,1,0:T(2,128)(2,1)S(1)}, u32[]{:S(2)}, u32[]{:S(2)}) collective-permute-start(bf16[16,1,128]{2,1,0:T(2,128)(2,1)S(1)} %get-tuple-element.42), channel_id=1, source_target_pairs={{1,0},{2,1},{3,2},{4,3},{5,4},{6,5},{7,6},{8,7},{9,8},{10,9},{11,1... | collective-permute-start | bytes 12296 | tf_op jit(solution)/shard_map/ppermute | solution.py:17
  380.6 38.9 %copy-start.9 = (f32[1152,128]{1,0:T(8,128)}, f32[1152,128]{1,0:T(8,128)S(1)}, u32[]{:S(2)}) copy-start(f32[1152,128]{1,0:T(8,128)S(1)} %fusion.15) | copy-start | bytes 1769476
  380.6 27.7 %collective-permute-start.8 = (bf16[16,1,128]{2,1,0:T(2,128)(2,1)S(1)}, bf16[16,1,128]{2,1,0:T(2,128)(2,1)S(1)}, u32[]{:S(2)}, u32[]{:S(2)}) collective-permute-start(bf16[16,1,128]{2,1,0:T(2,128)(2,1)S(1)} %get-tuple-element.45), channel_id=1, source_target_pairs={{0,1},{1,2},{2,3},{3,4},{4,5},{5,6},{6,7},{7,8},{8,9},{9,10},{10,1... | collective-permute-start | bytes 12296 | tf_op jit(solution)/shard_map/ppermute | solution.py:14
  380.7 27.6 %collective-permute-start.9 = (bf16[16,1,128]{2,1,0:T(2,128)(2,1)S(1)}, bf16[16,1,128]{2,1,0:T(2,128)(2,1)S(1)}, u32[]{:S(2)}, u32[]{:S(2)}) collective-permute-start(bf16[16,1,128]{2,1,0:T(2,128)(2,1)S(1)} %get-tuple-element.46), channel_id=1, source_target_pairs={{1,0},{2,1},{3,2},{4,3},{5,4},{6,5},{7,6},{8,7},{9,8},{10,9},{11,1... | collective-permute-start | bytes 12296 | tf_op jit(solution)/shard_map/ppermute | solution.py:17
  384.6 34.9 %collective-permute-start.14 = (bf16[1,194,128]{2,1,0:T(8,128)(2,1)S(1)}, bf16[1,194,128]{2,1,0:T(8,128)(2,1)S(1)}, u32[]{:S(2)}, u32[]{:S(2)}) collective-permute-start(bf16[1,194,128]{2,1,0:T(8,128)(2,1)S(1)} %get-tuple-element.28), channel_id=1, source_target_pairs={{0,16},{16,32},{32,48},{48,64},{64,80},{80,96},{96,112},{1,17},{17... | collective-permute-start | bytes 149000 | tf_op jit(solution)/shard_map/ppermute | solution.py:14
  402.6 16.9 %collective-permute-start.15 = (bf16[1,194,128]{2,1,0:T(8,128)(2,1)S(1)}, bf16[1,194,128]{2,1,0:T(8,128)(2,1)S(1)}, u32[]{:S(2)}, u32[]{:S(2)}) collective-permute-start(bf16[1,194,128]{2,1,0:T(8,128)(2,1)S(1)} %get-tuple-element.27), channel_id=1, source_target_pairs={{16,0},{32,16},{48,32},{64,48},{80,64},{96,80},{112,96},{17,1},{33... | collective-permute-start | bytes 149000 | tf_op jit(solution)/shard_map/ppermute | solution.py:17
  408.3 20.9 %collective-permute-start.10 = (bf16[1,194,128]{2,1,0:T(8,128)(2,1)S(1)}, bf16[1,194,128]{2,1,0:T(8,128)(2,1)S(1)}, u32[]{:S(2)}, u32[]{:S(2)}) collective-permute-start(bf16[1,194,128]{2,1,0:T(8,128)(2,1)S(1)} %get-tuple-element.31), channel_id=1, source_target_pairs={{16,0},{32,16},{48,32},{64,48},{80,64},{96,80},{112,96},{17,1},{33... | collective-permute-start | bytes 149000 | tf_op jit(solution)/shard_map/ppermute | solution.py:17
  412.3 17.0 %collective-permute-start.11 = (bf16[1,194,128]{2,1,0:T(8,128)(2,1)S(1)}, bf16[1,194,128]{2,1,0:T(8,128)(2,1)S(1)}, u32[]{:S(2)}, u32[]{:S(2)}) collective-permute-start(bf16[1,194,128]{2,1,0:T(8,128)(2,1)S(1)} %get-tuple-element.32), channel_id=1, source_target_pairs={{0,16},{16,32},{32,48},{48,64},{64,80},{80,96},{96,112},{1,17},{17... | collective-permute-start | bytes 149000 | tf_op jit(solution)/shard_map/ppermute | solution.py:14
  434.5 2.1 copy-start.5
  436.6 1.1 copy-start.7
  436.7 1.6 copy-start.8
  438.3 1.2 copy-start.6
  439.5 1.1 copy-start.4
Sparse Core Ops, SparseCore 0:
  434.7 143.8 all-reduce.4
where the time goes:
time: 590 us; the launch traced here: 588 us
  blocking collectives  293 us (50%)
  waiting for transfers between devices  136 us (23%)
  starting transfers between devices  94.3 us (16%)
  matrix products  29.7 us (5%)
  between operations  14.6 us (2%)
  local copies, waits for them, and re-layouts  14.5 us (2%)
  other arithmetic  6.06 us (1%)
    all_gather x1, blocking collectives, local(): lax.all_gather(w_first, ('lat', 'lon'), axis=0, tiled=True)  154 us
    all_gather x1, blocking collectives, local(): lax.all_gather(w_second, ('lat', 'lon'), axis=0, tiled=True)  139 us
    unnamed x2, waiting for transfers between devices  136 us
    ppermute x8, starting transfers between devices, padded_2(): lax.ppermute(lax.slice_in_dim(block, 0, width, axis=dim), axis, backward)  64.5 us
    ppermute x8, starting transfers between devices, padded_2(): lax.ppermute(lax.slice_in_dim(block, block.shape[dim] - width, None, axis...  29.8 us
    dot_general x18, matrix products, weight_grad(): lax.dot_general(piece, flat_grad, (((0,), (0,)), ((), ())), preferred_ele...  13.2 us
    dot_general x18, matrix products, transpose_conv(): lax.dot_general(piece, block, (((1,), (1,)), ((), ())), preferred_element...  12.2 us
  transfers between devices with their start and end apart: 17, of which 1 were waited for; matrix products, arithmetic and copies ran while one was open for 5% of the time, Pallas kernels for 0%

commit v1 on v0

v1 whole, which is shorter than its diff:
```python
import jax
import jax.numpy as jnp
from jax import lax
from jax.sharding import PartitionSpec as P

AXES = ("lat", "lon")


def ring(axis, step, periodic):
    count = lax.axis_size(axis)
    pairs = [(i, (i + step) % count) for i in range(count)]
    if not periodic:
        pairs = [(i, j) for i, j in pairs if j == i + step]
    return pairs


def add_rims(fields, width):
    low = lax.ppermute(fields[:, :, -width:], "lon", ring("lon", 1, True))
    high = lax.ppermute(fields[:, :, :width], "lon", ring("lon", -1, True))
    fields = jnp.concatenate([low, fields, high], axis=2)
    low = lax.ppermute(fields[:, -width:], "lat", ring("lat", 1, False))
    high = lax.ppermute(fields[:, :width], "lat", ring("lat", -1, False))
    return jnp.concatenate([low, fields, high], axis=1)


def gather_kernels(w_first, w_second):
    count = lax.axis_size(AXES)
    rows, chans = w_first.shape
    mine = jnp.concatenate([w_first, w_second], 0).reshape(1, rows, 2, chans)
    sent = jnp.broadcast_to(mine, (count, rows, 2, chans))
    got = lax.all_to_all(sent, AXES, 0, 0, tiled=True).reshape(count, 2, rows, chans)
    return got[:, 0].reshape(-1, chans), got[:, 1].reshape(-1, chans)


def scatter_sums(first, second):
    count = lax.axis_size(AXES)
    chans = first.shape[1]
    rows = first.shape[0] // count
    core = lax.axis_index(AXES) % 2
    both = jnp.concatenate(
        [first.reshape(count, rows, chans), second.reshape(count, rows, chans)], 1
    ).reshape(count // 2, 2, rows * 2, chans)
    keep = jnp.where(core == 0, both[:, 0], both[:, 1])
    send = jnp.where(core == 0, both[:, 1], both[:, 0])
    got = lax.ppermute(send, AXES, [(i, i ^ 1) for i in range(count)])
    part = (keep + got).reshape(count // 2, rows, 2, chans)
    groups = [list(range(parity, count, 2)) for parity in range(2)]
    parts = lax.all_to_all(part, AXES, 0, 0, tiled=True, axis_index_groups=groups)
    total = parts.sum(0).reshape(2, rows, chans)
    return total[0], total[1]


def local(features, cotangent, w_first, w_second):
    rows, cols, chans = features.shape
    kernel_one, kernel_two = gather_kernels(w_first, w_second)
    fields = add_rims(jnp.stack([features, cotangent]), 2)
    feat_pad, grad_pad = fields[0], fields[1]

    def conv(padded, weight, flip, height, width):
        total = jnp.zeros((height * width, chans), jnp.float32)
        for tap in range(9):
            a, b = divmod(tap, 3)
            if flip:
                a, b = 2 - a, 2 - b
            piece = padded[a : a + height, b : b + width].reshape(-1, chans)
            block = weight[tap * chans : (tap + 1) * chans]
            total = total + lax.dot_general(
                piece,
                block,
                (((1,), (1 if flip else 0,)), ((), ())),
                preferred_element_type=jnp.float32,
            )
        return total.reshape(height, width, chans)

    pre = conv(feat_pad, kernel_one, False, rows + 2, cols + 2)
    back_act = conv(grad_pad, kernel_two, True, rows + 2, cols + 2)
    sigma = jax.nn.sigmoid(pre)
    act = (pre * sigma).astype(jnp.bfloat16)[1:-1, 1:-1].reshape(-1, chans)
    back_pre = back_act * sigma * (1.0 + pre * (1.0 - sigma))
    place = lax.axis_index("lat") * rows - 1 + lax.broadcasted_iota(
        jnp.int32, (rows + 2, 1, 1), 0
    )
    inside = (place >= 0) & (place < rows * lax.axis_size("lat"))
    back_pre = jnp.where(inside, back_pre, 0.0).astype(jnp.bfloat16)
    back_own = back_pre[1:-1, 1:-1].reshape(-1, chans)
    firsts, seconds = [], []
    for tap in range(9):
        a, b = divmod(tap, 3)
        piece = feat_pad[a + 1 : a + 1 + rows, b + 1 : b + 1 + cols].reshape(-1, chans)
        firsts.append(
            lax.dot_general(
                piece, back_own, (((0,), (0,)), ((), ())), preferred_element_type=jnp.float32
            )
        )
        piece = grad_pad[3 - a : 3 - a + rows, 3 - b : 3 - b + cols].reshape(-1, chans)
        seconds.append(
            lax.dot_general(
                act, piece, (((0,), (0,)), ((), ())), preferred_element_type=jnp.float32
            )
        )
    grad_first, grad_second = scatter_sums(
        jnp.concatenate(firsts, 0), jnp.concatenate(seconds, 0)
    )
    grad_features = (
        cotangent.astype(jnp.float32) + conv(back_pre, kernel_one, True, rows, cols)
    ).astype(jnp.bfloat16)
    return grad_features, grad_first, grad_second


def solution(mesh):
    in_specs = (
        P("lat", "lon", None),
        P("lat", "lon", None),
        P(("lat", "lon"), None),
        P(("lat", "lon"), None),
    )
    out_specs = (P("lat", "lon", None), P(("lat", "lon"), None), P(("lat", "lon"), None))
    return jax.shard_map(local, mesh=mesh, in_specs=in_specs, out_specs=out_specs, check_vma=False)
```

time: 590 us -> 173 us (0.29)
  blocking collectives: 293 us -> 0 us
  waiting for transfers between devices: 136 us -> 12 us
  local copies, waits for them, and re-layouts: 14.5 us -> 80.5 us
  starting transfers between devices: 94.3 us -> 32.1 us
  between operations: 14.6 us -> 1.11 us
  matrix products: 29.7 us -> 37.3 us
    all_gather x2 -> x0, blocking collectives: 293 us -> none  [the longest x1 154 us: local(): lax.all_gather(w_first, ('lat', 'lon'), axis=0, tiled=True)]
    unnamed x2 -> x0, waiting for transfers between devices: 136 us -> none
    ppermute x16 -> x5, starting transfers between devices: 94.2 us -> 12 us  [the longest x1 5.67 us: add_rims(): low = lax.ppermute(fields[:, -width:], 'lat', ring('lat', 1, False))]
    reshape x0 -> x22, local copies, waits for them, and re-layouts: none -> 44.8 us  [the longest x18 38.2 us: conv(): piece = padded[a:a + height, b:b + width].reshape(-1, chans)]
    all_to_all x0 -> x2, starting transfers between devices: none -> 20.1 us  [the longest x1 10.8 us: scatter_sums(): lax.all_to_all(part, AXES, 0, 0, tiled=True, axis_index_groups=groups)]
    all_to_all x0 -> x2, waiting for transfers between devices: none -> 10.6 us  [the longest x1 10.6 us: scatter_sums(): lax.all_to_all(part, AXES, 0, 0, tiled=True, axis_index_groups=groups)]
    dot_general x45, matrix products: 29.7 us -> 37.3 us  [the longest x27 17.6 us: conv(): lax.dot_general(piece, block, (((1,), (1 if flip else 0,)), ((), ())), pr...]
    unnamed x24 -> x71, local copies, waits for them, and re-layouts: 7.81 us -> 14.3 us
  transfers between devices with their start and end apart: 17 -> 7, of which waited for: 1 -> 3; matrix products, arithmetic and copies ran while one was open for 5% -> 30% of each run, Pallas kernels for 0% -> 0%
where the time goes in v1:
time: 173 us; the launch traced here: 170 us
  local copies, waits for them, and re-layouts  80.5 us (47%)
  matrix products  37.3 us (22%)
  starting transfers between devices  32.1 us (19%)
  waiting for transfers between devices  12 us (7%)
  other arithmetic  7.37 us (4%)
    reshape x18, local copies, waits for them, and re-layouts, conv(): piece = padded[a:a + height, b:b + width].reshape(-1, chans)  38.2 us
    dot_general x27, matrix products, conv(): lax.dot_general(piece, block, (((1,), (1 if flip else 0,)), ((), ())), pr...  17.6 us
    unnamed x71, local copies, waits for them, and re-layouts  14.3 us
    all_to_all x1, starting transfers between devices, scatter_sums(): lax.all_to_all(part, AXES, 0, 0, tiled=True, axis_index_groups=groups)  10.8 us
    all_to_all x1, waiting for transfers between devices, scatter_sums(): lax.all_to_all(part, AXES, 0, 0, tiled=True, axis_index_groups=groups)  10.6 us
    dot_general x9, matrix products, local(): lax.dot_general(piece, back_own, (((0,), (0,)), ((), ())), preferred_elem...  10.4 us
    slice x2, local copies, waits for them, and re-layouts, conv(): piece = padded[a:a + height, b:b + width].reshape(-1, chans)  9.7 us
    all_to_all x1, starting transfers between devices, gather_kernels(): lax.all_to_all(sent, AXES, 0, 0, tiled=True).reshape(count, 2, rows, chans)  9.3 us
  transfers between devices with their start and end apart: 7, of which 3 were waited for; matrix products, arithmetic and copies ran while one was open for 30% of the time, Pallas kernels for 0%

profile of v1, /device:TPU:6, one launch (start us, length us, event | category | flops | bytes accessed | tf_op | source)
XLA Modules:
  0.0 170.4 jit_solution(10648477596092910825)
XLA Ops:
  1.7 3.9 %collective-permute-start.1 = (bf16[2,16,2,128]{3,2,1,0:T(2,128)(2,1)S(1)}, bf16[2,16,2,128]{3,2,1,0:T(2,128)(2,1)S(1)}, u32[]{:S(2)}, u32[]{:S(2)}) collective-permute-start(bf16[2,16,2,128]{3,2,1,0:T(2,128)(2,1)S(1)} %get-tuple-element.10), channel_id=1, source_target_pairs={{0,15},{1,0},{2,1},{3,2},{4,3},{5,4},{6,5},{7,6},{8,7},{9,8},{10,9... | collective-permute-start | bytes 49160 | tf_op jit(solution)/shard_map/ppermute | solution.py:19
  5.6 1.4 collective-permute-done
  7.2 5.7 %collective-permute-start.2 = (bf16[2,2,196,128]{3,2,1,0:T(8,128)(2,1)S(1)}, bf16[2,2,196,128]{3,2,1,0:T(8,128)(2,1)S(1)}, u32[]{:S(2)}, u32[]{:S(2)}) collective-permute-start(bf16[2,2,196,128]{3,2,1,0:T(8,128)(2,1)S(1)} %get-tuple-element.7), channel_id=1, source_target_pairs={{0,16},{16,32},{32,48},{48,64},{64,80},{80,96},{96,112},{1,17},{17... | collective-permute-start | bytes 602120 | tf_op jit(solution)/shard_map/ppermute | solution.py:21
  12.8 1.9 %collective-permute-start.3 = (bf16[2,2,196,128]{3,2,1,0:T(8,128)(2,1)S(1)}, bf16[2,2,196,128]{3,2,1,0:T(8,128)(2,1)S(1)}, u32[]{:S(2)}, u32[]{:S(2)}) collective-permute-start(bf16[2,2,196,128]{3,2,1,0:T(8,128)(2,1)S(1)} %get-tuple-element.8), channel_id=1, source_target_pairs={{16,0},{32,16},{48,32},{64,48},{80,64},{96,80},{112,96},{17,1},{33... | collective-permute-start | bytes 602120 | tf_op jit(solution)/shard_map/ppermute | solution.py:22
  15.9 9.3 %all-to-all-start = ((bf16[128,9,2,128]{3,2,1,0:T(2,128)(2,1)}), bf16[128,9,2,128]{3,2,1,0:T(2,128)(2,1)}, u32[]{:S(2)}, u32[]{:S(2)}) async-start(bf16[128,9,2,128]{3,2,1,0:T(2,128)(2,1)} %broadcast_in_dim.21), calls=%async_computation | async-start | bytes 1179648 | tf_op jit(solution)/shard_map/all_to_all | solution.py:31
  25.3 1.7 pad_maximum_fusion
  27.1 6.4 %fusion.76 = (bf16[18,194,128]{2,1,0:T(8,128)(2,1)}, bf16[18,194,128]{2,1,0:T(8,128)(2,1)}, bf16[18,194,128]{2,1,0:T(8,128)(2,1)}, bf16[18,194,128]{2,1,0:T(8,12...) fusion(bf16[20,196,128]{2,1,0:T(8,128)(2,1)S(1)} %get-tuple-ele, ...), kind=kLoop, calls=%fused_computation.139 | loop fusion | bytes 32182272 | tf_op jit(solution)/shard_map/slice | solution.py:65
  33.6 2.2 %reshape.158 = bf16[3492,128]{1,0:T(8,128)(2,1)} reshape(bf16[18,194,128]{2,1,0:T(8,128)(2,1)} %get-tuple-element.11) | data formatting | bytes 1787904 | tf_op jit(solution)/shard_map/reshape | solution.py:65
  35.7 2.2 %reshape.157 = bf16[3492,128]{1,0:T(8,128)(2,1)} reshape(bf16[18,194,128]{2,1,0:T(8,128)(2,1)} %get-tuple-element.12) | data formatting | bytes 1787904 | tf_op jit(solution)/shard_map/reshape | solution.py:65
  37.9 2.2 %reshape.156 = bf16[3492,128]{1,0:T(8,128)(2,1)} reshape(bf16[18,194,128]{2,1,0:T(8,128)(2,1)} %get-tuple-element.13) | data formatting | bytes 1787904 | tf_op jit(solution)/shard_map/reshape | solution.py:65
  40.1 2.2 %reshape.155 = bf16[3492,128]{1,0:T(8,128)(2,1)} reshape(bf16[18,194,128]{2,1,0:T(8,128)(2,1)} %get-tuple-element.14) | data formatting | bytes 1787904 | tf_op jit(solution)/shard_map/reshape | solution.py:65
  42.2 2.2 %reshape.154 = bf16[3492,128]{1,0:T(8,128)(2,1)} reshape(bf16[18,194,128]{2,1,0:T(8,128)(2,1)} %get-tuple-element.15) | data formatting | bytes 1787904 | tf_op jit(solution)/shard_map/reshape | solution.py:65
  44.5 2.2 %reshape.153 = bf16[3492,128]{1,0:T(8,128)(2,1)} reshape(bf16[18,194,128]{2,1,0:T(8,128)(2,1)} %get-tuple-element.16) | data formatting | bytes 1787904 | tf_op jit(solution)/shard_map/reshape | solution.py:65
  46.7 2.2 %reshape.152 = bf16[3492,128]{1,0:T(8,128)(2,1)} reshape(bf16[18,194,128]{2,1,0:T(8,128)(2,1)} %get-tuple-element.17) | data formatting | bytes 1787904 | tf_op jit(solution)/shard_map/reshape | solution.py:65
  48.8 2.2 %reshape.151 = bf16[3492,128]{1,0:T(8,128)(2,1)} reshape(bf16[18,194,128]{2,1,0:T(8,128)(2,1)} %get-tuple-element.18) | data formatting | bytes 1787904 | tf_op jit(solution)/shard_map/reshape | solution.py:65
  51.0 2.2 %reshape.149 = bf16[3492,128]{1,0:T(8,128)(2,1)} reshape(bf16[18,194,128]{2,1,0:T(8,128)(2,1)} %get-tuple-element.19) | data formatting | bytes 1787904 | tf_op jit(solution)/shard_map/reshape | solution.py:65
  53.2 2.2 %reshape.160 = bf16[3492,128]{1,0:T(8,128)(2,1)} reshape(bf16[18,194,128]{2,1,0:T(8,128)(2,1)} %get-tuple-element.42) | data formatting | bytes 1787904 | tf_op jit(solution)/shard_map/reshape | solution.py:65
  55.4 2.2 %reshape.161 = bf16[3492,128]{1,0:T(8,128)(2,1)} reshape(bf16[18,194,128]{2,1,0:T(8,128)(2,1)} %get-tuple-element.43) | data formatting | bytes 1787904 | tf_op jit(solution)/shard_map/reshape | solution.py:65
  57.6 2.2 %reshape.162 = bf16[3492,128]{1,0:T(8,128)(2,1)} reshape(bf16[18,194,128]{2,1,0:T(8,128)(2,1)} %get-tuple-element.44) | data formatting | bytes 1787904 | tf_op jit(solution)/shard_map/reshape | solution.py:65
  59.7 2.2 %reshape.163 = bf16[3492,128]{1,0:T(8,128)(2,1)} reshape(bf16[18,194,128]{2,1,0:T(8,128)(2,1)} %get-tuple-element.45) | data formatting | bytes 1787904 | tf_op jit(solution)/shard_map/reshape | solution.py:65
  61.9 2.2 %reshape.164 = bf16[3492,128]{1,0:T(8,128)(2,1)} reshape(bf16[18,194,128]{2,1,0:T(8,128)(2,1)} %get-tuple-element.46) | data formatting | bytes 1787904 | tf_op jit(solution)/shard_map/reshape | solution.py:65
  64.1 2.2 %reshape.165 = bf16[3492,128]{1,0:T(8,128)(2,1)} reshape(bf16[18,194,128]{2,1,0:T(8,128)(2,1)} %get-tuple-element.47) | data formatting | bytes 1787904 | tf_op jit(solution)/shard_map/reshape | solution.py:65
  66.2 2.2 %reshape.166 = bf16[3492,128]{1,0:T(8,128)(2,1)} reshape(bf16[18,194,128]{2,1,0:T(8,128)(2,1)} %get-tuple-element.48) | data formatting | bytes 1787904 | tf_op jit(solution)/shard_map/reshape | solution.py:65
  68.4 2.2 %reshape.167 = bf16[3492,128]{1,0:T(8,128)(2,1)} reshape(bf16[18,194,128]{2,1,0:T(8,128)(2,1)} %get-tuple-element.49) | data formatting | bytes 1787904 | tf_op jit(solution)/shard_map/reshape | solution.py:65
  71.7 1.2 copy.25
  74.7 2.0 %copy.27 = bf16[128,1,9,128]{3,2,0,1:T(8,128)(2,1)} copy(bf16[128,1,9,128]{3,0,2,1:T(8,128)(2,1)} %get-tuple-element.39) | data formatting | bytes 589824 | tf_op jit(solution)/shard_map/slice | solution.py:32
  76.7 1.2 reshape_squeeze.7
  77.9 1.5 fusion.45
  87.6 1.9 %convolution_add_fusion.8 = f32[3492,128]{1,0:T(8,128)} fusion(f32[3492,128]{1,0:T(8,128)S(1)} %convolution_add_fusion.9, bf16[3492,128]{1,0:T(8,128)(2,1)S(1)} %copy-done.7, bf16[1152,128]{1,0:T(8,128)(2,1)S(1)} %copy-done.32), kind=kOutput, calls=%fused_computation.8 | convolution fusion | flops 114872832 | bytes 4505600 | tf_op jit(solution)/shard_map/dot_general | solution.py:67
  89.5 2.7 %reshape.159 = f32[18,194,128]{2,1,0:T(8,128)} reshape(f32[3492,128]{1,0:T(8,128)} %convolution_add_fusion.8) | data formatting | bytes 3575808 | tf_op jit(solution)/shard_map/reshape | solution.py:73
  101.6 1.8 %convolution_add_fusion = f32[3492,128]{1,0:T(8,128)} fusion(f32[3492,128]{1,0:T(8,128)S(1)} %convolution_add_fusion.1, bf16[3492,128]{1,0:T(8,128)(2,1)S(1)} %copy-done.10, bf16[1152,128]{1,0:T(8,128)(2,1)S(1)} %reshape_squeeze.7), kind=kOutput, calls=%fused_computation | convolution fusion | flops 114872832 | bytes 4505600 | tf_op jit(solution)/shard_map/dot_general | solution.py:67
  103.4 2.6 %reshape.169 = f32[18,194,128]{2,1,0:T(8,128)} reshape(f32[3492,128]{1,0:T(8,128)} %convolution_add_fusion) | data formatting | bytes 3575808 | tf_op jit(solution)/shard_map/reshape | solution.py:73
  106.0 2.8 %add_divide_fusion = (f32[18,194,128]{2,1,0:T(8,128)S(1)}, bf16[18,194,128]{2,1,0:T(8,128)(2,1)S(1)}) fusion(f32[18,194,128]{2,1,0:T(8,128)} %reshape.169, f32[18,194,128]{2,1,0:T(8,128)} %reshape.159, pred[18]{0:T(512)(128)(4,1)S(1)} %compare_and_fusion), kind=kLoop, calls=%fused_computation.26 | loop fusion | flops 4469760 | bytes 6257682 | tf_op jit(solution)/shard_map/div | solution.py:77
  108.8 1.2 fusion.18
  110.0 3.3 %fusion.78 = (bf16[16,192,128]{2,1,0:T(8,128)(2,1)}, bf16[16,192,128]{2,1,0:T(8,128)(2,1)}, bf16[16,192,128]{2,1,0:T(8,128)(2,1)}, bf16[16,192,128]{2,1,0:T(8,12...) fusion(bf16[18,194,128]{2,1,0:T(8,128)(2,1)S(1)} %get-tuple-ele, ...), kind=kLoop, calls=%fused_computation.141 | loop fusion | bytes 14155776 | tf_op jit(solution)/shard_map/slice | solution.py:65
  122.9 2.1 %concatenate.29 = f32[64,2,9,128]{3,2,1,0:T(8,128)} reshape(f32[1152,128]{1,0:T(8,128)} %fusion.1) | data formatting | bytes 1179648 | tf_op jit(solution)/shard_map/concatenate | solution.py:40
  125.0 1.2 fusion.17
  126.2 1.2 fusion.16
  127.4 1.2 fusion.15
  128.5 1.2 fusion.14
  129.7 1.2 fusion.13
  130.8 1.2 fusion.12
  132.0 1.2 fusion.11
  133.1 1.2 fusion.10
  134.3 1.2 concatenate.27
  144.7 1.3 copy.30
  146.0 10.8 %all-to-all-start.1 = ((f32[64,9,2,128]{3,2,1,0:T(2,128)}), f32[64,9,2,128]{3,2,1,0:T(2,128)S(1)}, u32[]{:S(2)}, u32[]{:S(2)}) async-start(f32[64,9,2,128]{3,2,1,0:T(2,128)} %copy.30), calls=%async_computation.1 | async-start | bytes 1179648 | tf_op jit(solution)/shard_map/all_to_all | solution.py:48
  159.0 10.6 %all-to-all-done.1 = f32[64,9,2,128]{3,2,1,0:T(2,128)S(1)} async-done(((f32[64,9,2,128]{3,2,1,0:T(2,128)}), f32[64,9,2,128]{3,2,1,0:T(2,128)S(1)}, u32[]{:S(2)}, u32[]{:S(2)}) %all-to-all-start.1) | async-done | bytes 589856 | tf_op jit(solution)/shard_map/all_to_all | solution.py:48
  (130 shorter events, 44.7 us)
Async XLA Ops:
  0.6 6.4 %copy-start.1 = (bf16[16,192,128]{2,1,0:T(8,128)(2,1)S(1)}, bf16[16,192,128]{2,1,0:T(8,128)(2,1)}, u32[]{:S(2)}) copy-start(bf16[16,192,128]{2,1,0:T(8,128)(2,1)} %param.5) | copy-start | bytes 2359300
  0.6 6.4 %copy-start.3 = (bf16[16,192,128]{2,1,0:T(8,128)(2,1)S(1)}, bf16[16,192,128]{2,1,0:T(8,128)(2,1)}, u32[]{:S(2)}) copy-start(bf16[16,192,128]{2,1,0:T(8,128)(2,1)} %param.4) | copy-start | bytes 2359300
  0.7 14.1 %copy-start.33 = (bf16[9,128]{1,0:T(8,128)(2,1)S(1)}, bf16[9,128]{1,0:T(8,128)(2,1)}, u32[]{:S(2)}) copy-start(bf16[9,128]{1,0:T(8,128)(2,1)} %param.7) | copy-start | bytes 6916
  0.7 14.1 %copy-start.34 = (bf16[9,128]{1,0:T(8,128)(2,1)S(1)}, bf16[9,128]{1,0:T(8,128)(2,1)}, u32[]{:S(2)}) copy-start(bf16[9,128]{1,0:T(8,128)(2,1)} %param.6) | copy-start | bytes 6916
  1.6 5.3 %collective-permute-start = (bf16[2,16,2,128]{3,2,1,0:T(2,128)(2,1)S(1)}, bf16[2,16,2,128]{3,2,1,0:T(2,128)(2,1)S(1)}, u32[]{:S(2)}, u32[]{:S(2)}) collective-permute-start(bf16[2,16,2,128]{3,2,1,0:T(2,128)(2,1)S(1)} %get-tuple-element.9), channel_id=1, source_target_pairs={{0,1},{1,2},{2,3},{3,4},{4,5},{5,6},{6,7},{7,8},{8,9},{9,10},{10,1... | collective-permute-start | bytes 49160 | tf_op jit(solution)/shard_map/ppermute | solution.py:18
  1.7 5.3 %collective-permute-start.1 = (bf16[2,16,2,128]{3,2,1,0:T(2,128)(2,1)S(1)}, bf16[2,16,2,128]{3,2,1,0:T(2,128)(2,1)S(1)}, u32[]{:S(2)}, u32[]{:S(2)}) collective-permute-start(bf16[2,16,2,128]{3,2,1,0:T(2,128)(2,1)S(1)} %get-tuple-element.10), channel_id=1, source_target_pairs={{0,15},{1,0},{2,1},{3,2},{4,3},{5,4},{6,5},{7,6},{8,7},{9,8},{10,9... | collective-permute-start | bytes 49160 | tf_op jit(solution)/shard_map/ppermute | solution.py:19
  7.2 18.1 %collective-permute-start.2 = (bf16[2,2,196,128]{3,2,1,0:T(8,128)(2,1)S(1)}, bf16[2,2,196,128]{3,2,1,0:T(8,128)(2,1)S(1)}, u32[]{:S(2)}, u32[]{:S(2)}) collective-permute-start(bf16[2,2,196,128]{3,2,1,0:T(8,128)(2,1)S(1)} %get-tuple-element.7), channel_id=1, source_target_pairs={{0,16},{16,32},{32,48},{48,64},{64,80},{80,96},{96,112},{1,17},{17... | collective-permute-start | bytes 602120 | tf_op jit(solution)/shard_map/ppermute | solution.py:21
  12.8 12.4 %collective-permute-start.3 = (bf16[2,2,196,128]{3,2,1,0:T(8,128)(2,1)S(1)}, bf16[2,2,196,128]{3,2,1,0:T(8,128)(2,1)S(1)}, u32[]{:S(2)}, u32[]{:S(2)}) collective-permute-start(bf16[2,2,196,128]{3,2,1,0:T(8,128)(2,1)S(1)} %get-tuple-element.8), channel_id=1, source_target_pairs={{16,0},{32,16},{48,32},{64,48},{80,64},{96,80},{112,96},{17,1},{33... | collective-permute-start | bytes 602120 | tf_op jit(solution)/shard_map/ppermute | solution.py:22
  15.9 55.8 %all-to-all-start = ((bf16[128,9,2,128]{3,2,1,0:T(2,128)(2,1)}), bf16[128,9,2,128]{3,2,1,0:T(2,128)(2,1)}, u32[]{:S(2)}, u32[]{:S(2)}) async-start(bf16[128,9,2,128]{3,2,1,0:T(2,128)(2,1)} %broadcast_in_dim.21), calls=%async_computation | async-start | bytes 1179648 | tf_op jit(solution)/shard_map/all_to_all | solution.py:31
  73.7 4.2 %copy-start.6 = (bf16[3492,128]{1,0:T(8,128)(2,1)S(1)}, bf16[3492,128]{1,0:T(8,128)(2,1)}, u32[]{:S(2)}) copy-start(bf16[3492,128]{1,0:T(8,128)(2,1)} %reshape.149) | copy-start | bytes 2681860
  77.9 1.5 copy-start.22
  77.9 1.5 copy-start.32
  79.4 1.2 copy-start.21
  80.6 1.2 copy-start.20
  81.7 1.2 copy-start.19
  82.9 1.2 copy-start.18
  84.1 1.2 copy-start.14
  85.3 1.2 copy-start.8
  86.4 1.2 copy-start.7
  89.5 2.7 %copy-start.5 = (bf16[3492,128]{1,0:T(8,128)(2,1)S(1)}, bf16[3492,128]{1,0:T(8,128)(2,1)}, u32[]{:S(2)}) copy-start(bf16[3492,128]{1,0:T(8,128)(2,1)} %reshape.160) | copy-start | bytes 2681860
  92.2 1.2 copy-start.17
  93.4 1.2 copy-start.16
  94.6 1.2 copy-start.15
  95.7 1.2 copy-start.13
  96.9 1.2 copy-start.12
  98.1 1.2 copy-start.11
  99.2 1.2 copy-start.9
  100.4 1.2 copy-start.10
  110.0 3.3 %copy-start = (f32[18,194,128]{2,1,0:T(8,128)S(1)}, f32[18,194,128]{2,1,0:T(8,128)}, u32[]{:S(2)}) copy-start(f32[18,194,128]{2,1,0:T(8,128)} %reshape.169) | copy-start | bytes 5363716
  134.3 1.6 copy-start.4
  135.9 1.1 copy-start.23
  136.3 1.2 copy-start.31
  136.3 8.3 %collective-permute-start.4 = (f32[64,18,128]{2,0,1:T(8,128)S(1)}, f32[64,18,128]{2,0,1:T(8,128)S(1)}, u32[]{:S(2)}, u32[]{:S(2)}) collective-permute-start(f32[64,18,128]{2,0,1:T(8,128)S(1)} %select_bitcast_fusion), channel_id=1, source_target_pairs={{0,1},{1,0},{2,3},{3,2},{4,5},{5,4},{6,7},{7,6},{8,9},{9,8},{10,11... | collective-permute-start | bytes 1769480 | tf_op jit(solution)/shard_map/ppermute | solution.py:45
  137.4 1.1 copy-start.30
  138.6 1.1 copy-start.29
  139.7 1.1 copy-start.28
  140.8 1.1 copy-start.27
  142.0 1.1 copy-start.26
  143.1 1.1 copy-start.25
  144.6 12.2 %copy-start.24 = (bf16[16,192,128]{2,1,0:T(8,128)(2,1)S(1)}, bf16[16,192,128]{2,1,0:T(8,128)(2,1)}, u32[]{:S(2)}) copy-start(bf16[16,192,128]{2,1,0:T(8,128)(2,1)} %get-tuple-element.29) | copy-start | bytes 2359300
  146.0 23.6 %all-to-all-start.1 = ((f32[64,9,2,128]{3,2,1,0:T(2,128)}), f32[64,9,2,128]{3,2,1,0:T(2,128)S(1)}, u32[]{:S(2)}, u32[]{:S(2)}) async-start(f32[64,9,2,128]{3,2,1,0:T(2,128)} %copy.30), calls=%async_computation.1 | async-start | bytes 1179648 | tf_op jit(solution)/shard_map/all_to_all | solution.py:48
  156.8 1.1 copy-start.2

commit v2 on v1

v2 whole, which is shorter than its diff:
```python
import jax
import jax.numpy as jnp
from jax import lax
from jax.experimental import pallas as pl
from jax.experimental.pallas import tpu as pltpu
from jax.sharding import PartitionSpec as P

AXES = ("lat", "lon")
BF16 = jnp.bfloat16
F32 = jnp.float32


def ring(axis, step, periodic):
    count = lax.axis_size(axis)
    pairs = [(i, (i + step) % count) for i in range(count)]
    if not periodic:
        pairs = [(i, j) for i, j in pairs if j == i + step]
    return pairs


def exchange(fields):
    count, rows, cols, chans = fields.shape
    left = lax.ppermute(fields[:, :, -2:], "lon", ring("lon", 1, True))
    right = lax.ppermute(fields[:, :, :2], "lon", ring("lon", -1, True))
    gap = jnp.zeros((count, rows, 12, chans), fields.dtype)
    wide = jnp.concatenate([fields, right, gap, left], axis=2)
    above = lax.ppermute(wide[:, -2:], "lat", ring("lat", 1, False))
    below = lax.ppermute(wide[:, :2], "lat", ring("lat", -1, False))
    return wide, above, below


def gather_kernels(w_first, w_second):
    count = lax.axis_size(AXES)
    rows, chans = w_first.shape
    mine = jnp.stack([w_first, w_second], 1)[None]
    sent = jnp.broadcast_to(mine, (count, rows, 2, chans))
    got = lax.all_to_all(sent, AXES, 0, 0, tiled=True).reshape(-1, 2, chans)
    return got[:, 0], got[:, 1]


def scatter_sums(first, second):
    count = lax.axis_size(AXES)
    chans = first.shape[1]
    rows = first.shape[0] // count
    core = lax.axis_index(AXES) % 2
    both = jnp.stack([first, second], 1).reshape(count // 2, 2, rows, 2, chans)
    keep = lax.dynamic_index_in_dim(both, core, 1, keepdims=False)
    send = lax.dynamic_index_in_dim(both, 1 - core, 1, keepdims=False)
    got = lax.ppermute(send, AXES, [(i, i ^ 1) for i in range(count)])
    groups = [list(range(parity, count, 2)) for parity in range(2)]
    parts = lax.all_to_all(keep + got, AXES, 0, 0, tiled=True, axis_index_groups=groups)
    total = parts.sum(0)
    return total[:, 0], total[:, 1]


def prepare_kernel(wide_ref, above_ref, below_ref, taps_ref, cells_ref):
    pairs = taps_ref.shape[1]
    for field in range(2):
        for p in range(pairs):
            if p == 0:
                rows = [above_ref[field, r] for r in range(2)]
            elif p == pairs - 1:
                rows = [below_ref[field, r] for r in range(2)]
            else:
                rows = [wide_ref[field, 2 * p - 2 + r] for r in range(2)]
            centre = jnp.concatenate(rows, 1)
            wide = centre.astype(F32)
            size = wide.shape[0]
            taps = jnp.concatenate(
                [
                    pltpu.roll(wide, 1, 0).astype(BF16),
                    centre,
                    pltpu.roll(wide, size - 1, 0).astype(BF16),
                ],
                1,
            )
            taps_ref[field, p] = taps
            filled = jnp.concatenate([taps, jnp.zeros((256 - size, taps.shape[1]), BF16)], 0)
            cells_ref[field, :, 256 * p : 256 * (p + 1)] = filled.T


def prepare(wide, above, below):
    fields, rows, width, chans = wide.shape
    pairs = rows // 2 + 2
    whole = pl.BlockSpec(memory_space=pltpu.VMEM)
    return pl.pallas_call(
        prepare_kernel,
        out_shape=(
            jax.ShapeDtypeStruct((fields, pairs, width, 6 * chans), BF16),
            jax.ShapeDtypeStruct((fields, 6 * chans, 256 * pairs), BF16),
        ),
        in_specs=[whole] * 3,
        out_specs=(whole, whole),
    )(wide, above, below)


def tap_rows(a, b, chans):
    tap = (a + 1) * 3 + b + 1
    return slice(tap * chans, (tap + 1) * chans)


def fill_plain(weight_ref, table_ref):
    chans = weight_ref.shape[1]
    for half in range(2):
        for b in range(3):
            for source in range(2):
                for target in range(2):
                    a = 2 * half + source - target - 1
                    at = (2 * b + source) * chans
                    if abs(a) <= 1:
                        block = weight_ref[tap_rows(a, b - 1, chans)]
                    else:
                        block = jnp.zeros((chans, chans), BF16)
                    table_ref[half, at : at + chans, target * chans : (target + 1) * chans] = block


def fill_turned(weight_ref, table_ref):
    chans = weight_ref.shape[1]
    for half in range(2):
        for b in range(3):
            for source in range(2):
                for target in range(2):
                    a = 2 * half + source - target - 1
                    at = (2 * b + source) * chans
                    if abs(a) <= 1:
                        block = weight_ref[tap_rows(-a, 1 - b, chans)]
                    else:
                        block = jnp.zeros((chans, chans), BF16)
                    table_ref[half, target * chans : (target + 1) * chans, at : at + chans] = block


def plain(lhs, rhs):
    return lax.dot_general(lhs, rhs, (((1,), (0,)), ((), ())), preferred_element_type=F32)


def turned(lhs, rhs):
    return lax.dot_general(lhs, rhs, (((1,), (1,)), ((), ())), preferred_element_type=F32)


def middle_kernel(
    edge_ref, one_ref, two_ref, taps_ref, cells_ref,
    first_ref, second_ref, back_ref,
    plain_ref, turned_ref, act_ref, own_ref,
):
    pairs = back_ref.shape[0]
    width = back_ref.shape[1]
    chans = one_ref.shape[1]
    fill_plain(one_ref, plain_ref)
    fill_turned(two_ref, turned_ref)
    cols = width - 16
    act_ref[...] = jnp.zeros_like(act_ref)
    own_ref[...] = jnp.zeros_like(own_ref)
    lane = lax.broadcasted_iota(jnp.int32, (1, 2 * chans), 1)
    for p in range(pairs):
        pre = plain(taps_ref[0, p], plain_ref[0]) + plain(taps_ref[0, p + 1], plain_ref[1])
        back = turned(taps_ref[1, p], turned_ref[0]) + turned(taps_ref[1, p + 1], turned_ref[1])
        sigma = jax.nn.sigmoid(pre)
        act = pre * sigma
        back = back * sigma * (1.0 + pre * (1.0 - sigma))
        own = back
        if p == 0:
            rim = lane < chans
            back = jnp.where(rim & (edge_ref[0] == 1), 0.0, back)
        if p == pairs - 1:
            rim = lane >= chans
            back = jnp.where(rim & (edge_ref[1] == 1), 0.0, back)
        if p in (0, pairs - 1):
            act = jnp.where(rim, 0.0, act)
            own = jnp.where(rim, 0.0, own)
        back_ref[p] = back.astype(BF16)
        act_ref[256 * p : 256 * p + cols] = act[:cols].astype(BF16)
        own_ref[256 * p : 256 * p + cols] = own[:cols].astype(BF16)
    span = 256 * pairs
    firsts = [plain(cells_ref[0, :, 256 * d : 256 * d + span], own_ref[...]) for d in range(2)]
    seconds = [plain(cells_ref[1, :, 256 * d : 256 * d + span], act_ref[...]) for d in range(2)]
    for a in range(-1, 2):
        for b in range(3):

            def summed(halves):
                total = None
                for half in range(2):
                    for source in range(2):
                        target = 2 * half + source - 1 - a
                        if target in (0, 1):
                            at = (2 * b + source) * chans
                            block = halves[half][at : at + chans, target * chans : (target + 1) * chans]
                            total = block if total is None else total + block
                return total

            first_ref[tap_rows(a, b - 1, chans)] = summed(firsts)
            second_ref[tap_rows(-a, 1 - b, chans)] = summed(seconds).T


def middle(edges, one, two, taps, cells):
    _, pairs, width, lanes = taps.shape
    pairs -= 1
    chans = one.shape[1]
    whole = pl.BlockSpec(memory_space=pltpu.VMEM)
    sums = jax.ShapeDtypeStruct(one.shape, F32)
    return pl.pallas_call(
        middle_kernel,
        out_shape=(sums, sums, jax.ShapeDtypeStruct((pairs, width, 2 * chans), BF16)),
        in_specs=[pl.BlockSpec(memory_space=pltpu.SMEM)] + [whole] * 4,
        out_specs=(whole,) * 3,
        scratch_shapes=[
            pltpu.VMEM((2, lanes, 2 * chans), BF16),
            pltpu.VMEM((2, 2 * chans, lanes), BF16),
            pltpu.VMEM((256 * pairs, 2 * chans), BF16),
            pltpu.VMEM((256 * pairs, 2 * chans), BF16),
        ],
    )(edges, one, two, taps, cells)


def final_kernel(one_ref, back_ref, cot_ref, out_ref, turned_ref, taps_ref):
    fill_turned(one_ref, turned_ref)
    pairs, width, lanes = back_ref.shape
    rows, cols, chans = cot_ref.shape
    for p in range(pairs):
        centre = back_ref[p]
        wide = centre.astype(F32)
        taps_ref[p] = jnp.concatenate(
            [
                pltpu.roll(wide, 1, 0).astype(BF16),
                centre,
                pltpu.roll(wide, width - 1, 0).astype(BF16),
            ],
            1,
        )
    for p in range(rows // 2):
        total = turned(taps_ref[p, :cols], turned_ref[0]) + turned(
            taps_ref[p + 1, :cols], turned_ref[1]
        )
        for r in range(2):
            out_ref[2 * p + r] = (
                total[:, r * chans : (r + 1) * chans] + cot_ref[2 * p + r].astype(F32)
            ).astype(BF16)


def final(one, back, cotangent):
    pairs, width, lanes = back.shape
    whole = pl.BlockSpec(memory_space=pltpu.VMEM)
    return pl.pallas_call(
        final_kernel,
        out_shape=jax.ShapeDtypeStruct(cotangent.shape, BF16),
        in_specs=[whole] * 3,
        out_specs=whole,
        scratch_shapes=[
            pltpu.VMEM((2, lanes, 3 * lanes), BF16),
            pltpu.VMEM((pairs, width, 3 * lanes), BF16),
        ],
        cost_estimate=pl.CostEstimate(flops=2 * 1152 * 128 * 3072, bytes_accessed=4 << 20, transcendentals=0),
    )(one, back, cotangent)


def local(features, cotangent, w_first, w_second):
    one, two = gather_kernels(w_first, w_second)
    wide, above, below = exchange(jnp.stack([features, cotangent]))
    taps, cells = prepare(wide, above, below)
    place = lax.axis_index("lat")
    edges = jnp.stack([place == 0, place == lax.axis_size("lat") - 1]).astype(jnp.int32)
    first, second, back = middle(edges, one, two, taps, cells)
    grad_first, grad_second = scatter_sums(first, second)
    return final(one, back, cotangent), grad_first, grad_second


def solution(mesh):
    in_specs = (
        P("lat", "lon", None),
        P("lat", "lon", None),
        P(("lat", "lon"), None),
        P(("lat", "lon"), None),
    )
    out_specs = (P("lat", "lon", None), P(("lat", "lon"), None), P(("lat", "lon"), None))
    return jax.shard_map(local, mesh=mesh, in_specs=in_specs, out_specs=out_specs, check_vma=False)
```

time: 173 us -> 91.5 us (0.53)
  local copies, waits for them, and re-layouts: 80.5 us -> 9.71 us
  matrix products: 37.3 us -> 0 us
  Pallas kernels: 0 us -> 27 us
  other arithmetic: 7.37 us -> 4.29 us
  waiting for transfers between devices: 12 us -> 14.5 us
  starting transfers between devices: 32.1 us -> 34.1 us
    reshape x22 -> x0, local copies, waits for them, and re-layouts: 44.8 us -> none  [the longest x18 38.2 us: conv(): piece = padded[a:a + height, b:b + width].reshape(-1, chans)]
    dot_general x45 -> x0, matrix products: 37.3 us -> none  [the longest x27 17.6 us: conv(): lax.dot_general(piece, block, (((1,), (1 if flip else 0,)), ((), ())), pr...]
    pallas_call x0 -> x3, Pallas kernels: none -> 27 us  [the longest x1 13.8 us: middle(): pl.pallas_call(middle_kernel, out_shape=(sums, sums, jax.ShapeDtypeStruct...]
    slice x5 -> x3, local copies, waits for them, and re-layouts: 12.6 us -> 0.88 us  [the longest x1 0.85 us: gather_kernels(): return (got[:, 0], got[:, 1])]
    unnamed x71 -> x11, local copies, waits for them, and re-layouts: 14.3 us -> 2.65 us
    concatenate x3 -> x1, local copies, waits for them, and re-layouts: 3.7 us -> 0.08 us  [exchange(): wide = jnp.concatenate([fields, right, gap, left], axis=2)]
    ppermute x4, waiting for transfers between devices: 1.45 us -> 4.33 us  [the longest x1 4.32 us: exchange(): below = lax.ppermute(wide[:, :2], 'lat', ring('lat', -1, False))]
    div x1 -> x0, other arithmetic: 2.81 us -> none  [local(): sigma = jax.nn.sigmoid(pre)]
  transfers between devices with their start and end apart: 7 -> 7, of which waited for: 3 -> 3; matrix products, arithmetic and copies ran while one was open for 30% -> 5% of each run, Pallas kernels for 0% -> 15%
where the time goes in v2:
time: 91.5 us; the launch traced here: 90.3 us
  starting transfers between devices  34.1 us (37%)
  Pallas kernels  27 us (30%)
  waiting for transfers between devices  14.5 us (16%)
  local copies, waits for them, and re-layouts  9.71 us (11%)
  other arithmetic  4.29 us (5%)
    pallas_call x1, Pallas kernels, middle(): pl.pallas_call(middle_kernel, out_shape=(sums, sums, jax.ShapeDtypeStruct...  13.8 us
    all_to_all x1, starting transfers between devices, scatter_sums(): lax.all_to_all(keep + got, AXES, 0, 0, tiled=True, axis_index_groups=groups)  10.7 us
    all_to_all x1, starting transfers between devices, gather_kernels(): got = lax.all_to_all(sent, AXES, 0, 0, tiled=True).reshape(-1, 2, chans)  9.78 us
    pallas_call x1, Pallas kernels, prepare(): pl.pallas_call(prepare_kernel, out_shape=(jax.ShapeDtypeStruct((fields, p...  8.58 us
    all_to_all x1, waiting for transfers between devices, scatter_sums(): lax.all_to_all(keep + got, AXES, 0, 0, tiled=True, axis_index_groups=groups)  8.17 us
    ppermute x1, starting transfers between devices, exchange(): above = lax.ppermute(wide[:, -2:], 'lat', ring('lat', 1, False))  6.69 us
    pallas_call x1, Pallas kernels, final(): pl.pallas_call(final_kernel, out_shape=jax.ShapeDtypeStruct(cotangent.sha...  4.63 us
    ppermute x1, waiting for transfers between devices, exchange(): below = lax.ppermute(wide[:, :2], 'lat', ring('lat', -1, False))  4.32 us
  transfers between devices with their start and end apart: 7, of which 3 were waited for; matrix products, arithmetic and copies ran while one was open for 5% of the time, Pallas kernels for 15%

profile of v2, /device:TPU:6, one launch (start us, length us, event | category | flops | bytes accessed | tf_op | source)
XLA Modules:
  0.0 90.3 jit_solution(5090584902317860015)
XLA Ops:
  0.6 0.0 copy-start.1
  0.6 0.9 %pad_maximum_fusion.2 = (bf16[2,16,2,128]{3,2,1,0:T(2,128)(2,1)S(1)}, bf16[2,16,2,128]{3,2,1,0:T(2,128)(2,1)S(1)}) fusion(bf16[1,16,192,128]{3,2,1,0:T(8,128)(2,1)} %bitcast.25, bf16[1,16,192,128]{3,2,1,0:T(8,128)(2,1)} %bitcast.23), kind=kLoop, calls=%fused_computation.6 | loop fusion | flops 65536 | bytes 1605632 | tf_op jit(solution)/shard_map/slice | solution.py:24
  1.6 3.9 %collective-permute-start = (bf16[2,16,2,128]{3,2,1,0:T(2,128)(2,1)S(1)}, bf16[2,16,2,128]{3,2,1,0:T(2,128)(2,1)S(1)}, u32[]{:S(2)}, u32[]{:S(2)}) collective-permute-start(bf16[2,16,2,128]{3,2,1,0:T(2,128)(2,1)S(1)} %get-tuple-element.17), channel_id=1, source_target_pairs={{0,15},{1,0},{2,1},{3,2},{4,3},{5,4},{6,5},{7,6},{8,7},{9,8},{10,9... | collective-permute-start | bytes 49160 | tf_op jit(solution)/shard_map/ppermute | solution.py:24
  5.4 0.0 collective-permute-start.1
  5.4 0.7 pad_maximum_fusion.3
  6.2 1.1 %broadcast_in_dim.4 = bf16[128,9,2,128]{3,2,1,0:T(2,128)(2,1)} broadcast(bf16[9,2,128]{2,1,0:T(2,128)(2,1)S(1)} %copy.20), dimensions={1,2,3} | broadcast | bytes 594432 | tf_op jit(solution)/shard_map/broadcast_in_dim | solution.py:36
  7.3 9.8 %all-to-all-start = ((bf16[128,9,2,128]{3,2,1,0:T(2,128)(2,1)}), bf16[128,9,2,128]{3,2,1,0:T(2,128)(2,1)S(1)}, u32[]{:S(2)}, u32[]{:S(2)}) async-start(bf16[128,9,2,128]{3,2,1,0:T(2,128)(2,1)} %broadcast_in_dim.4), calls=%async_computation | async-start | bytes 1179648 | tf_op jit(solution)/shard_map/all_to_all | solution.py:37
  17.1 0.1 pad.3.clone
  17.1 0.0 collective-permute-done
  17.2 0.0 collective-permute-done.1
  17.2 0.0 copy-done.1
  17.2 1.6 %pad_maximum_fusion.wide_ref = bf16[2,16,208,128]{3,2,1,0:T(8,128)(2,1)S(1)} fusion(bf16[2,16,2,128]{3,2,1,0:T(2,128)(2,1)S(1)} %collective-permute-done.1, bf16[2,16,2,128]{3,2,1,0:T(2,128)(2,1)S(1)} %collective-permute-done, bf16[1,16,192,128]{3,2,1,0:T(8,128)(2,1)} %bitcast.26, bf16[1,16,192,128]{3,2,1,0:T(8,128)(2,1)S(1)} %bitcast.24, ...), kind=kLoop, calls=%fused_computation | loop fusion | flops 8519680 | bytes 3309984 | tf_op jit(solution)/shard_map/concatenate | solution.py:26
  18.7 0.0 copy-start
  18.8 2.8 %collective-permute-start.3 = (bf16[2,2,208,128]{3,2,1,0:T(8,128)(2,1)S(1)}, bf16[2,2,208,128]{3,2,1,0:T(8,128)(2,1)S(1)}, u32[]{:S(2)}, u32[]{:S(2)}) collective-permute-start(bf16[2,2,208,128]{3,2,1,0:T(8,128)(2,1)S(1)} %get-tuple-element.15), channel_id=1, source_target_pairs={{16,0},{32,16},{48,32},{64,48},{80,64},{96,80},{112,96},{17,1},{33... | collective-permute-start | bytes 638984 | tf_op jit(solution)/shard_map/ppermute | solution.py:28
  21.5 6.7 %collective-permute-start.2 = (bf16[2,2,208,128]{3,2,1,0:T(8,128)(2,1)S(1)}, bf16[2,2,208,128]{3,2,1,0:T(8,128)(2,1)S(1)}, u32[]{:S(2)}, u32[]{:S(2)}) collective-permute-start(bf16[2,2,208,128]{3,2,1,0:T(8,128)(2,1)S(1)} %get-tuple-element.16), channel_id=1, source_target_pairs={{0,16},{16,32},{32,48},{48,64},{64,80},{80,96},{96,112},{1,17},{17... | collective-permute-start | bytes 638984 | tf_op jit(solution)/shard_map/ppermute | solution.py:27
  28.3 0.7 add_convert_fusion.edge_ref
  28.9 4.3 %collective-permute-done.3.below_ref = bf16[2,2,208,128]{3,2,1,0:T(8,128)(2,1)S(1)} collective-permute-done((bf16[2,2,208,128]{3,2,1,0:T(8,128)(2,1)S(1)}, bf16[2,2,208,128]{3,2,1,0:T(8,128)(2,1)S(1)}, u32[]{:S(2)}, u32[]{:S(2)}) %collective-permute-start.3) | collective-permute-done | bytes 213024 | tf_op jit(solution)/shard_map/ppermute | solution.py:28
  33.2 0.0 copy-start.2
  33.2 0.0 collective-permute-done.2.above_ref
  33.2 0.0 copy-done
  33.3 0.7 copy-done.2
  33.9 0.0 copy-start.3
  33.9 0.7 copy-done.3
  34.6 8.6 %shard_map.67 = (bf16[2,10,208,768]{3,2,1,0:T(8,128)(2,1)}, bf16[2,768,2560]{2,1,0:T(8,128)(2,1)}) custom-call(bf16[2,16,208,128]{3,2,1,0:T(8,128)(2,1)} %copy-done, bf16[2,2,208,128]{3,2,1,0:T(8,128)(2,1)} %copy-done.3, bf16[2,2,208,128]{3,2,1,0:T(8,128)(2,1)} %copy-done.2), custom_call_target="tpu_custom_call" | custom-call | tf_op jit(solution)/shard_map/pallas_call | solution.py:86
  43.2 0.0 all-to-all-done
  43.2 0.8 fusion.1
  44.1 0.9 %copy_bitcast_fusion.1 = (bf16[1152,128]{1,0:T(8,128)(2,1)}, bf16[1152,128]{1,0:T(8,128)(2,1)}) fusion(bf16[1152,1,128]{2,1,0:T(2,128)(2,1)S(1)} %get-tuple-element.19, bf16[1152,1,128]{2,1,0:T(2,128)(2,1)S(1)} %get-tuple-element.20), kind=kLoop, calls=%fused_computation.3 | loop fusion | bytes 1179648 | tf_op jit(solution)/shard_map/squeeze | solution.py:38
  45.0 13.8 %shard_map.68 = (f32[1152,128]{1,0:T(8,128)}, f32[1152,128]{1,0:T(8,128)}, bf16[9,208,256]{2,1,0:T(8,128)(2,1)}) custom-call(s32[2]{0:T(128)} %add_convert_fusion.edge_ref, bf16[1152,128]{1,0:T(8,128)(2,1)} %get-tuple-element.24.one_ref, bf16[1152,128]{1,0:T(8,128)(2,1)} %get-tuple-element.23.two_ref, bf16[2,10,208,768]{3,2,1,0:T(8,128)(2,1)} %get-tuple-element.8.taps_ref, ...), custom_call_target="tpu_custom_call" | custom-call | tf_op jit(solution)/shard_map/pallas_call | solution.py:200
  58.7 1.1 %stack.45 = f32[64,2,9,1,128]{4,2,1,0,3:T(8,128)S(1)} reshape(f32[1152,128]{1,0:T(8,128)} %get-tuple-element.11) | data formatting | bytes 1179648 | tf_op jit(solution)/shard_map/stack | solution.py:46
  59.9 0.1 constant_dynamic-update-slice_fusion.1
  60.0 1.1 %stack.46 = f32[64,2,9,1,128]{4,2,1,0,3:T(8,128)S(1)} reshape(f32[1152,128]{1,0:T(8,128)} %get-tuple-element.12) | data formatting | bytes 1179648 | tf_op jit(solution)/shard_map/stack | solution.py:46
  61.1 0.1 constant_dynamic-update-slice_fusion
  61.2 0.2 constant_dynamic-slice_fusion.1
  61.4 0.2 copy.36
  61.6 0.3 collective-permute-start.4
  61.9 2.0 %collective-permute-done.4 = f32[64,9,2,128]{3,0,2,1:T(8,128)S(1)} collective-permute-done((f32[64,9,2,128]{3,0,2,1:T(8,128)S(1)}, f32[64,9,2,128]{3,0,2,1:T(8,128)S(1)}, u32[]{:S(2)}, u32[]{:S(2)}) %collective-permute-start.4) | collective-permute-done | bytes 589856 | tf_op jit(solution)/shard_map/ppermute | solution.py:49
  63.9 0.3 bitcast_add_fusion
  64.2 1.3 %copy.25 = f32[64,9,2,128]{3,2,1,0:T(2,128)} copy(f32[64,9,2,128]{3,0,2,1:T(8,128)S(1)} %bitcast_add_fusion) | data formatting | bytes 1179648 | tf_op jit(solution)/shard_map/add | solution.py:51
  65.4 10.7 %all-to-all-start.1 = ((f32[64,9,2,128]{3,2,1,0:T(2,128)}), f32[64,9,2,128]{3,2,1,0:T(2,128)S(1)}, u32[]{:S(2)}, u32[]{:S(2)}) async-start(f32[64,9,2,128]{3,2,1,0:T(2,128)} %copy.25), calls=%async_computation.1 | async-start | bytes 1179648 | tf_op jit(solution)/shard_map/all_to_all | solution.py:51
  76.1 4.6 %shard_map.69 = bf16[16,192,128]{2,1,0:T(8,128)(2,1)} custom-call(bf16[1152,128]{1,0:T(8,128)(2,1)} %get-tuple-element.24.one_ref, bf16[9,208,256]{2,1,0:T(8,128)(2,1)} %get-tuple-element.10.back_ref, bf16[16,192,128]{2,1,0:T(8,128)(2,1)} %cot_ref.1), custom_call_target="tpu_custom_call" | custom-call | flops 905969664 | bytes 4194304 | tf_op jit(solution)/shard_map/pallas_call | solution.py:242
  80.7 8.2 %all-to-all-done.1 = f32[64,9,2,128]{3,2,1,0:T(2,128)S(1)} async-done(((f32[64,9,2,128]{3,2,1,0:T(2,128)}), f32[64,9,2,128]{3,2,1,0:T(2,128)S(1)}, u32[]{:S(2)}, u32[]{:S(2)}) %all-to-all-start.1) | async-done | bytes 589856 | tf_op jit(solution)/shard_map/all_to_all | solution.py:51
  88.9 0.2 reduce_sum.9
  89.1 0.6 copy.37
  89.7 0.6 copy.38
  (4 shorter events, 0.0 us)
Async XLA Ops:
  0.6 16.5 %copy-start.1 = (bf16[16,192,128]{2,1,0:T(8,128)(2,1)S(1)}, bf16[16,192,128]{2,1,0:T(8,128)(2,1)}, u32[]{:S(2)}) copy-start(bf16[16,192,128]{2,1,0:T(8,128)(2,1)} %param.4) | copy-start | bytes 2359300
  1.6 15.6 %collective-permute-start = (bf16[2,16,2,128]{3,2,1,0:T(2,128)(2,1)S(1)}, bf16[2,16,2,128]{3,2,1,0:T(2,128)(2,1)S(1)}, u32[]{:S(2)}, u32[]{:S(2)}) collective-permute-start(bf16[2,16,2,128]{3,2,1,0:T(2,128)(2,1)S(1)} %get-tuple-element.17), channel_id=1, source_target_pairs={{0,15},{1,0},{2,1},{3,2},{4,3},{5,4},{6,5},{7,6},{8,7},{9,8},{10,9... | collective-permute-start | bytes 49160 | tf_op jit(solution)/shard_map/ppermute | solution.py:24
  5.4 11.7 %collective-permute-start.1 = (bf16[2,16,2,128]{3,2,1,0:T(2,128)(2,1)S(1)}, bf16[2,16,2,128]{3,2,1,0:T(2,128)(2,1)S(1)}, u32[]{:S(2)}, u32[]{:S(2)}) collective-permute-start(bf16[2,16,2,128]{3,2,1,0:T(2,128)(2,1)S(1)} %get-tuple-element.18), channel_id=1, source_target_pairs={{0,1},{1,2},{2,3},{3,4},{4,5},{5,6},{6,7},{7,8},{8,9},{9,10},{10,1... | collective-permute-start | bytes 49160 | tf_op jit(solution)/shard_map/ppermute | solution.py:23
  7.3 35.9 %all-to-all-start = ((bf16[128,9,2,128]{3,2,1,0:T(2,128)(2,1)}), bf16[128,9,2,128]{3,2,1,0:T(2,128)(2,1)S(1)}, u32[]{:S(2)}, u32[]{:S(2)}) async-start(bf16[128,9,2,128]{3,2,1,0:T(2,128)(2,1)} %broadcast_in_dim.4), calls=%async_computation | async-start | bytes 1179648 | tf_op jit(solution)/shard_map/all_to_all | solution.py:37
  18.7 14.5 %copy-start = (bf16[2,16,208,128]{3,2,1,0:T(8,128)(2,1)}, bf16[2,16,208,128]{3,2,1,0:T(8,128)(2,1)S(1)}, u32[]{:S(2)}) copy-start(bf16[2,16,208,128]{3,2,1,0:T(8,128)(2,1)S(1)} %pad_maximum_fusion.wide_ref) | copy-start | bytes 5111812
  18.8 14.5 %collective-permute-start.3 = (bf16[2,2,208,128]{3,2,1,0:T(8,128)(2,1)S(1)}, bf16[2,2,208,128]{3,2,1,0:T(8,128)(2,1)S(1)}, u32[]{:S(2)}, u32[]{:S(2)}) collective-permute-start(bf16[2,2,208,128]{3,2,1,0:T(8,128)(2,1)S(1)} %get-tuple-element.15), channel_id=1, source_target_pairs={{16,0},{32,16},{48,32},{64,48},{80,64},{96,80},{112,96},{17,1},{33... | collective-permute-start | bytes 638984 | tf_op jit(solution)/shard_map/ppermute | solution.py:28
  21.5 11.7 %collective-permute-start.2 = (bf16[2,2,208,128]{3,2,1,0:T(8,128)(2,1)S(1)}, bf16[2,2,208,128]{3,2,1,0:T(8,128)(2,1)S(1)}, u32[]{:S(2)}, u32[]{:S(2)}) collective-permute-start(bf16[2,2,208,128]{3,2,1,0:T(8,128)(2,1)S(1)} %get-tuple-element.16), channel_id=1, source_target_pairs={{0,16},{16,32},{32,48},{48,64},{64,80},{80,96},{96,112},{1,17},{17... | collective-permute-start | bytes 638984 | tf_op jit(solution)/shard_map/ppermute | solution.py:27
  33.2 0.7 copy-start.2
  33.9 0.7 copy-start.3
  61.6 2.3 %collective-permute-start.4 = (f32[64,9,2,128]{3,0,2,1:T(8,128)S(1)}, f32[64,9,2,128]{3,0,2,1:T(8,128)S(1)}, u32[]{:S(2)}, u32[]{:S(2)}) collective-permute-start(f32[64,9,2,128]{3,0,2,1:T(8,128)S(1)} %bitcast.27), channel_id=1, source_target_pairs={{0,1},{1,0},{2,3},{3,2},{4,5},{5,4},{6,7},{7,6},{8,9},{9,8},{10,11... | collective-permute-start | bytes 1769480 | tf_op jit(solution)/shard_map/ppermute | solution.py:49
  65.4 23.5 %all-to-all-start.1 = ((f32[64,9,2,128]{3,2,1,0:T(2,128)}), f32[64,9,2,128]{3,2,1,0:T(2,128)S(1)}, u32[]{:S(2)}, u32[]{:S(2)}) async-start(f32[64,9,2,128]{3,2,1,0:T(2,128)} %copy.25), calls=%async_computation.1 | async-start | bytes 1179648 | tf_op jit(solution)/shard_map/all_to_all | solution.py:51

commit v3 on v2

v3 whole, which is shorter than its diff:
```python
import jax
import jax.numpy as jnp
from jax import lax
from jax.experimental import pallas as pl
from jax.experimental.pallas import tpu as pltpu
from jax.sharding import PartitionSpec as P

AXES = ("lat", "lon")
BF16 = jnp.bfloat16
F32 = jnp.float32
PREP_LIMIT = 24 << 20
MIDDLE_LIMIT = 60 * 1024 * 1024
FINAL_LIMIT = 16 << 20


def ring(axis, step, periodic):
    count = lax.axis_size(axis)
    pairs = [(i, (i + step) % count) for i in range(count)]
    if not periodic:
        pairs = [(i, j) for i, j in pairs if j == i + step]
    return pairs


def gather_kernels(w_first, w_second):
    count = lax.axis_size(AXES)
    rows, chans = w_first.shape
    mine = jnp.stack([w_first, w_second], 1)[None]
    sent = jnp.broadcast_to(mine, (count, rows, 2, chans))
    return lax.all_to_all(sent, AXES, 0, 0, tiled=True).reshape(-1, chans)


def scatter_sums(sums):
    count = lax.axis_size(AXES)
    chans = sums.shape[1]
    rows = sums.shape[0] // (2 * count)
    core = lax.axis_index(AXES) % 2
    both = sums.reshape(count // 2, 2, rows, 2, chans)
    keep = lax.dynamic_index_in_dim(both, core, 1, keepdims=False)
    send = lax.dynamic_index_in_dim(both, 1 - core, 1, keepdims=False)
    got = lax.ppermute(send, AXES, [(i, i ^ 1) for i in range(count)])
    groups = [list(range(parity, count, 2)) for parity in range(2)]
    parts = lax.all_to_all(keep + got, AXES, 0, 0, tiled=True, axis_index_groups=groups)
    return add_parts(parts.reshape(-1, chans), count // 2, rows)


def add_kernel(parts_ref, first_ref, second_ref):
    rows = first_ref.shape[0]
    groups = parts_ref.shape[0] // (2 * rows)
    for r in range(rows):
        for out_ref, at in ((first_ref, 2 * r), (second_ref, 2 * r + 1)):
            out_ref[r : r + 1] = jnp.sum(
                parts_ref[pl.ds(at, groups, stride=2 * rows)], 0, keepdims=True
            )


def add_parts(parts, groups, rows):
    whole = pl.BlockSpec(memory_space=pltpu.VMEM)
    out = jax.ShapeDtypeStruct((rows, parts.shape[1]), F32)
    return pl.pallas_call(
        add_kernel, out_shape=(out, out), in_specs=[whole], out_specs=(whole, whole),
        compiler_params=pltpu.CompilerParams(vmem_limit_bytes=4 << 20),
    )(parts)


def column_taps(centre):
    wide = centre.astype(F32)
    return jnp.concatenate(
        [
            pltpu.roll(wide, 1, 0).astype(BF16),
            centre,
            pltpu.roll(wide, wide.shape[0] - 1, 0).astype(BF16),
        ],
        1,
    )


def inner_kernel(feat_ref, cot_ref, tail_ref, taps_ref, cells_ref):
    pairs = taps_ref.shape[1]
    cols = feat_ref.shape[1]
    for field, own_ref in enumerate((feat_ref, cot_ref)):
        last = None
        for p in range(pairs):
            rows = [
                jnp.concatenate([own_ref[r], tail_ref[field, r]], 0)
                for r in (2 * p + 1, 2 * p + 2)
            ]
            taps = column_taps(jnp.concatenate(rows, 1))
            taps_ref[field, p] = taps
            own = taps[:cols]
            if p:
                at = 2 * cols * ((p - 1) // 2)
                cells_ref[field, p % 2, :, at : at + 2 * cols] = jnp.concatenate([last, own], 0).T
            last = own


def inner(features, cotangent, tail):
    rows, cols, chans = features.shape
    width = cols + tail.shape[2]
    pairs = rows // 2 - 1
    whole = pl.BlockSpec(memory_space=pltpu.VMEM)
    return pl.pallas_call(
        inner_kernel,
        out_shape=(
            jax.ShapeDtypeStruct((2, pairs, width, 6 * chans), BF16),
            jax.ShapeDtypeStruct((2, 2, 6 * chans, cols * (pairs - 1)), BF16),
        ),
        in_specs=[whole] * 3,
        out_specs=(whole, whole),
        compiler_params=pltpu.CompilerParams(vmem_limit_bytes=PREP_LIMIT),
        cost_estimate=pl.CostEstimate(flops=1 << 32, bytes_accessed=16 << 20, transcendentals=0),
    )(features, cotangent, tail)


def outer_kernel(feat_ref, cot_ref, tail_ref, above_ref, below_ref, near_ref, taps_ref, cells_ref):
    rows, cols, _ = feat_ref.shape
    pairs = near_ref.shape[1]
    for field, own_ref in enumerate((feat_ref, cot_ref)):
        first = jnp.concatenate([own_ref[0], tail_ref[field, 0]], 0)
        taps = column_taps(jnp.concatenate([above_ref[field], first], 1))
        taps_ref[field, 0] = taps
        cells_ref[field, 0] = jnp.concatenate([taps[:cols], near_ref[field, 0, :cols]], 0).T
        last = jnp.concatenate([own_ref[rows - 1], tail_ref[field, rows - 1]], 0)
        taps = column_taps(jnp.concatenate([last, below_ref[field]], 1))
        taps_ref[field, 1] = taps
        cells_ref[field, 1] = jnp.concatenate([near_ref[field, pairs - 1, :cols], taps[:cols]], 0).T


def outer(features, cotangent, tail, above, below, near):
    rows, cols, chans = features.shape
    width = cols + tail.shape[2]
    whole = pl.BlockSpec(memory_space=pltpu.VMEM)
    return pl.pallas_call(
        outer_kernel,
        out_shape=(
            jax.ShapeDtypeStruct((2, 2, width, 6 * chans), BF16),
            jax.ShapeDtypeStruct((2, 2, 6 * chans, 2 * cols), BF16),
        ),
        in_specs=[whole] * 6,
        out_specs=(whole, whole),
        compiler_params=pltpu.CompilerParams(vmem_limit_bytes=PREP_LIMIT),
        cost_estimate=pl.CostEstimate(flops=1 << 30, bytes_accessed=4 << 20, transcendentals=0),
    )(features, cotangent, tail, above, below, near)


def tap_rows(a, b, chans):
    tap = (a + 1) * 3 + b + 1
    return slice(tap * chans, (tap + 1) * chans)


def fill_plain(weight_ref, table_ref):
    chans = weight_ref.shape[1]
    for half in range(2):
        for b in range(3):
            for source in range(2):
                for target in range(2):
                    a = 2 * half + source - target - 1
                    at = (2 * b + source) * chans
                    if abs(a) <= 1:
                        block = weight_ref[tap_rows(a, b - 1, chans)]
                    else:
                        block = jnp.zeros((chans, chans), BF16)
                    table_ref[half, at : at + chans, target * chans : (target + 1) * chans] = block


def fill_turned(weight_ref, table_ref):
    chans = weight_ref.shape[1]
    for half in range(2):
        for b in range(3):
            for source in range(2):
                for target in range(2):
                    a = 2 * half + source - target - 1
                    at = (2 * b + source) * chans
                    if abs(a) <= 1:
                        block = weight_ref[tap_rows(-a, 1 - b, chans)]
                    else:
                        block = jnp.zeros((chans, chans), BF16)
                    table_ref[half, target * chans : (target + 1) * chans, at : at + chans] = block


def plain(lhs, rhs):
    return lax.dot_general(lhs, rhs, (((1,), (0,)), ((), ())), preferred_element_type=F32)


def turned(lhs, rhs):
    return lax.dot_general(lhs, rhs, (((1,), (1,)), ((), ())), preferred_element_type=F32)


def middle_kernel(
    both_ref, inner_taps_ref, inner_cells_ref, outer_taps_ref, outer_cells_ref,
    sums_ref, back_ref,
    wide_ref, one_ref, two_ref, plain_ref, turned_ref, slope_ref, act_ref, own_ref,
    taps_ref, cells_ref, taps_sem, cells_sem,
):
    pairs, width, lanes = back_ref.shape
    inner_cols = inner_cells_ref.shape[3]
    outer_cols = outer_cells_ref.shape[3]
    loads = {}
    for c in range(2):
        for field in range(2):
            loads[c, field] = (
                pltpu.make_async_copy(
                    outer_taps_ref.at[field, c],
                    taps_ref.at[field, pairs * c],
                    taps_sem.at[c, field, 0],
                ),
                pltpu.make_async_copy(
                    inner_taps_ref.at[field, pl.ds(c * pairs // 2, pairs // 2 - c)],
                    taps_ref.at[field, pl.ds(c * pairs // 2 + 1, pairs // 2 - c)],
                    taps_sem.at[c, field, 1],
                ),
            )
            for load in loads[c, field]:
                load.start()
    cell_loads = {}
    for field in (1, 0):
        for shift in range(2):
            cell_loads[field, shift] = (
                pltpu.make_async_copy(
                    outer_cells_ref.at[field, shift],
                    cells_ref.at[field, shift, :, pl.ds(shift * inner_cols, outer_cols)],
                    cells_sem.at[field, shift, 0],
                ),
                pltpu.make_async_copy(
                    inner_cells_ref.at[field, shift],
                    cells_ref.at[field, shift, :, pl.ds((1 - shift) * outer_cols, inner_cols)],
                    cells_sem.at[field, shift, 1],
                ),
            )
            for load in cell_loads[field, shift]:
                load.start()
    chans = lanes // 2
    cols = width - 16
    taps = one_ref.shape[0]
    wide_ref[...] = both_ref[...].astype(F32)
    one_ref[...] = wide_ref[pl.ds(0, taps, stride=2)].astype(BF16)
    two_ref[...] = wide_ref[pl.ds(1, taps, stride=2)].astype(BF16)
    fill_plain(one_ref, plain_ref)
    fill_turned(two_ref, turned_ref)

    def rows_of(field, first, count):
        return taps_ref[field, first : first + count].reshape(count * width, 3 * lanes)

    def cells_of(field, shift):
        for load in cell_loads[field, shift]:
            load.wait()
        return cells_ref[field, shift]

    step = pairs // 2
    for c in range(0, pairs, step):
        for load in loads[c // step, 0]:
            load.wait()
        pre = plain(rows_of(0, c, step), plain_ref[0]) + plain(rows_of(0, c + 1, step), plain_ref[1])
        sigma = jax.nn.sigmoid(pre)
        act = (pre * sigma).astype(BF16)
        slope_ref[...] = sigma * (1.0 + pre * (1.0 - sigma))
        for p in range(step):
            at = cols * (c + p)
            act_ref[at : at + cols] = act[width * p : width * p + cols]
        for load in loads[c // step, 1]:
            load.wait()
        back = turned(rows_of(1, c, step), turned_ref[0]) + turned(
            rows_of(1, c + 1, step), turned_ref[1]
        )
        back = (back * slope_ref[...]).astype(BF16)
        for p in range(step):
            at = cols * (c + p)
            part = back[width * p : width * (p + 1)]
            back_ref[c + p] = part
            own_ref[at : at + cols] = part[:cols]
    seconds = [plain(cells_of(1, d), act_ref[...]) for d in range(2)]
    firsts = [plain(cells_of(0, d), own_ref[...]) for d in range(2)]
    for a in range(-1, 2):
        for b in range(3):

            def summed(halves):
                total = None
                for half in range(2):
                    for source in range(2):
                        target = 2 * half + source - 1 - a
                        if target in (0, 1):
                            at = (2 * b + source) * chans
                            block = halves[half][at : at + chans, target * chans : (target + 1) * chans]
                            total = block if total is None else total + block
                return total

            at = tap_rows(a, b - 1, chans).start
            sums_ref[pl.ds(2 * at, chans, stride=2)] = summed(firsts)
            at = tap_rows(-a, 1 - b, chans).start
            sums_ref[pl.ds(2 * at + 1, chans, stride=2)] = summed(seconds).T


def middle(both, inner_parts, outer_parts):
    inner_taps, inner_cells = inner_parts
    outer_taps, outer_cells = outer_parts
    pairs = inner_taps.shape[1] + 1
    width = inner_taps.shape[2]
    rows, chans = both.shape
    lanes = 2 * chans
    cells = pairs * (width - 16)
    whole = pl.BlockSpec(memory_space=pltpu.VMEM)
    return pl.pallas_call(
        middle_kernel,
        out_shape=(
            jax.ShapeDtypeStruct((rows, chans), F32),
            jax.ShapeDtypeStruct((pairs, width, lanes), BF16),
        ),
        in_specs=[whole] + [pl.BlockSpec(memory_space=pltpu.HBM)] * 4,
        out_specs=(whole,) * 2,
        scratch_shapes=[
            pltpu.VMEM((rows, chans), F32),
            pltpu.VMEM((rows // 2, chans), BF16),
            pltpu.VMEM((rows // 2, chans), BF16),
            pltpu.VMEM((2, 3 * lanes, lanes), BF16),
            pltpu.VMEM((2, lanes, 3 * lanes), BF16),
            pltpu.VMEM((pairs // 2 * width, lanes), F32),
            pltpu.VMEM((cells, lanes), BF16),
            pltpu.VMEM((cells, lanes), BF16),
            pltpu.VMEM((2, pairs + 1, width, 3 * lanes), BF16),
            pltpu.VMEM((2, 2, 3 * lanes, cells), BF16),
            pltpu.SemaphoreType.DMA((2, 2, 2)),
            pltpu.SemaphoreType.DMA((2, 2, 2)),
        ],
        compiler_params=pltpu.CompilerParams(vmem_limit_bytes=MIDDLE_LIMIT),
    )(both, inner_taps, inner_cells, outer_taps, outer_cells)


def final_kernel(
    both_ref, back_ref, above_ref, below_ref, cot_ref, out_ref,
    wide_ref, one_ref, turned_ref, taps_ref,
):
    pairs, width, lanes = back_ref.shape
    rows, cols, chans = cot_ref.shape
    wide_ref[...] = both_ref[...].astype(F32)
    one_ref[...] = wide_ref[pl.ds(0, one_ref.shape[0], stride=2)].astype(BF16)
    fill_turned(one_ref, turned_ref)
    for p in range(pairs + 1):
        low = above_ref[...] if p == 0 else back_ref[p - 1, :, chans:]
        high = below_ref[...] if p == pairs else back_ref[p, :, :chans]
        taps = column_taps(jnp.concatenate([low, high], 1))
        taps_ref[cols * p : cols * (p + 1)] = taps[:cols]
    step = pairs // 2
    for c in range(0, pairs, step):
        total = turned(taps_ref[cols * c : cols * (c + step)], turned_ref[0]) + turned(
            taps_ref[cols * (c + 1) : cols * (c + step + 1)], turned_ref[1]
        )
        for p in range(step):
            for r in range(2):
                row = 2 * (c + p) + r
                part = total[cols * p : cols * (p + 1), r * chans : (r + 1) * chans]
                out_ref[row] = (part + cot_ref[row].astype(F32)).astype(BF16)


def final(both, back, above, below, cotangent):
    pairs, width, lanes = back.shape
    rows, cols, chans = cotangent.shape
    whole = pl.BlockSpec(memory_space=pltpu.VMEM)
    return pl.pallas_call(
        final_kernel,
        out_shape=jax.ShapeDtypeStruct(cotangent.shape, BF16),
        in_specs=[whole] * 5,
        out_specs=whole,
        scratch_shapes=[
            pltpu.VMEM(both.shape, F32),
            pltpu.VMEM((both.shape[0] // 2, chans), BF16),
            pltpu.VMEM((2, lanes, 3 * lanes), BF16),
            pltpu.VMEM(((pairs + 1) * cols, 3 * lanes), BF16),
        ],
        compiler_params=pltpu.CompilerParams(vmem_limit_bytes=FINAL_LIMIT),
        cost_estimate=pl.CostEstimate(flops=1 << 32, bytes_accessed=8 << 20, transcendentals=0),
    )(both, back, above, below, cotangent)


def shift_rows(top, bottom):
    above = lax.ppermute(bottom, "lat", ring("lat", 1, False))
    below = lax.ppermute(top, "lat", ring("lat", -1, False))
    return above, below


def local(features, cotangent, w_first, w_second):
    both = gather_kernels(w_first, w_second)
    rows, cols, chans = features.shape
    left = jnp.stack([features[:, -2:], cotangent[:, -2:]])
    right = jnp.stack([features[:, :2], cotangent[:, :2]])
    left = lax.ppermute(left, "lon", ring("lon", 1, True))
    right = lax.ppermute(right, "lon", ring("lon", -1, True))
    tail = jnp.concatenate([right, jnp.zeros((2, rows, 12, chans), BF16), left], 2)

    def whole_row(r):
        return jnp.concatenate([jnp.stack([features[r], cotangent[r]]), tail[:, r]], 1)

    above, below = shift_rows(whole_row(0), whole_row(rows - 1))
    inner_parts = inner(features, cotangent, tail)
    outer_parts = outer(features, cotangent, tail, above, below, inner_parts[0])
    sums, back = middle(both, inner_parts, outer_parts)
    grads = scatter_sums(sums)
    above, below = shift_rows(back[0, :, :chans], back[-1, :, chans:])
    return final(both, back, above, below, cotangent), *grads


def solution(mesh):
    in_specs = (
        P("lat", "lon", None),
        P("lat", "lon", None),
        P(("lat", "lon"), None),
        P(("lat", "lon"), None),
    )
    out_specs = (P("lat", "lon", None), P(("lat", "lon"), None), P(("lat", "lon"), None))
    return jax.shard_map(local, mesh=mesh, in_specs=in_specs, out_specs=out_specs, check_vma=False)
```

time: 91.5 us -> 86.4 us (0.944)
  Pallas kernels: 27 us -> 21.1 us
  local copies, waits for them, and re-layouts: 9.71 us -> 11.7 us
  starting transfers between devices: 34.1 us -> 35.8 us
  waiting for transfers between devices: 14.5 us -> 13.2 us
  other arithmetic: 4.29 us -> 3.29 us
    all_to_all x1, waiting for transfers between devices: 8.17 us -> 0.01 us  [scatter_sums(): lax.all_to_all(keep + got, AXES, 0, 0, tiled=True, axis_index_groups=groups)]
    ppermute x4 -> x6, waiting for transfers between devices: 4.33 us -> 11.2 us  [the longest x2 9.49 us: shift_rows(): below = lax.ppermute(top, 'lat', ring('lat', -1, False))]
    unnamed x11 -> x18, local copies, waits for them, and re-layouts: 2.65 us -> 8.32 us
    ppermute x4 -> x6, starting transfers between devices: 13.3 us -> 18 us  [the longest x2 10.2 us: shift_rows(): above = lax.ppermute(bottom, 'lat', ring('lat', 1, False))]
    pallas_call x2 -> x4, Pallas kernels: 22.4 us -> 18.6 us  [the longest x1 15.2 us: middle(): pl.pallas_call(middle_kernel, out_shape=(jax.ShapeDtypeStruct((rows, chan...]
    all_to_all x1, starting transfers between devices: 10.7 us -> 7.92 us  [scatter_sums(): lax.all_to_all(keep + got, AXES, 0, 0, tiled=True, axis_index_groups=groups)]
    add x1, other arithmetic: 0.25 us -> 2.4 us  [scatter_sums(): keep + got]
    pallas_call x1, Pallas kernels: 4.63 us -> 2.53 us  [final(): pl.pallas_call(final_kernel, out_shape=jax.ShapeDtypeStruct(cotangent.sha...]
  transfers between devices with their start and end apart: 7 -> 9, of which waited for: 3 -> 4; matrix products, arithmetic and copies ran while one was open for 5% -> 2% of each run, Pallas kernels for 15% -> 6%
where the time goes in v3:
time: 86.4 us; the launch traced here: 86 us
  starting transfers between devices  35.8 us (41%)
  Pallas kernels  21.1 us (24%)
  waiting for transfers between devices  13.2 us (15%)
  local copies, waits for them, and re-layouts  11.7 us (14%)
  other arithmetic  3.29 us (4%)
  between operations  0.9 us (1%)
    pallas_call x1, Pallas kernels, middle(): pl.pallas_call(middle_kernel, out_shape=(jax.ShapeDtypeStruct((rows, chan...  15.2 us
    ppermute x2, starting transfers between devices, shift_rows(): above = lax.ppermute(bottom, 'lat', ring('lat', 1, False))  10.2 us
    all_to_all x1, starting transfers between devices, gather_kernels(): return lax.all_to_all(sent, AXES, 0, 0, tiled=True).reshape(-1, chans)  9.76 us
    ppermute x2, waiting for transfers between devices, shift_rows(): below = lax.ppermute(top, 'lat', ring('lat', -1, False))  9.49 us
    unnamed x18, local copies, waits for them, and re-layouts  8.32 us
    all_to_all x1, starting transfers between devices, scatter_sums(): lax.all_to_all(keep + got, AXES, 0, 0, tiled=True, axis_index_groups=groups)  7.92 us
    ppermute x1, starting transfers between devices, local(): right = lax.ppermute(right, 'lon', ring('lon', -1, True))  3.88 us
    ppermute x2, starting transfers between devices, shift_rows(): below = lax.ppermute(top, 'lat', ring('lat', -1, False))  3.84 us
  transfers between devices with their start and end apart: 9, of which 4 were waited for; matrix products, arithmetic and copies ran while one was open for 2% of the time, Pallas kernels for 6%

profile of v3, /device:TPU:6, one launch (start us, length us, event | category | flops | bytes accessed | tf_op | source)
XLA Modules:
  0.0 86.0 jit_solution(16968731917199734042)
XLA Ops:
  0.6 0.0 copy-start.6
  0.6 0.0 copy-start.7
  0.7 1.0 %slice_bitcast_fusion.6 = (bf16[1,16,2,128]{3,2,0,1:T(2,128)(2,1)S(1)}, bf16[1,16,2,128]{3,2,0,1:T(2,128)(2,1)S(1)}, bf16[1,16,2,128]{3,2,0,1:T(2,128)(2,1)S(1)}, bf16[1,16,2,128]{3,2,0,1:T(2,128)(2,1)S(1)}) fusion(bf16[16,192,128]{2,1,0:T(8,128)(2,1)} %cot_ref.5, bf16[16,192,128]{2,1,0:T(8,128)(2,1)} %feat_ref.3), kind=kLoop, calls=%fused_computation.14 | loop fusion | bytes 65536 | tf_op jit(solution)/shard_map/stack | solution.py:383
  1.6 3.9 %collective-permute-start = (bf16[2,16,2,128]{3,2,0,1:T(2,128)(2,1)S(1)}, bf16[2,16,2,128]{3,2,0,1:T(2,128)(2,1)S(1)}, u32[]{:S(2)}, u32[]{:S(2)}) collective-permute-start(bf16[2,16,2,128]{3,2,0,1:T(2,128)(2,1)S(1)} %pad_maximum_fusion.3), channel_id=1, source_target_pairs={{0,15},{1,0},{2,1},{3,2},{4,3},{5,4},{6,5},{7,6},{8,7},{9,8},{10,9... | collective-permute-start | bytes 49160 | tf_op jit(solution)/shard_map/ppermute | solution.py:385
  5.6 0.1 collective-permute-start.1
  5.6 0.7 pad_maximum_fusion.5
  6.4 1.1 %broadcast_in_dim.4 = bf16[128,9,2,128]{3,2,1,0:T(2,128)(2,1)} broadcast(bf16[9,2,128]{2,1,0:T(2,128)(2,1)S(1)} %copy.7), dimensions={1,2,3} | broadcast | bytes 594432 | tf_op jit(solution)/shard_map/broadcast_in_dim | solution.py:28
  7.5 9.8 %all-to-all-start = ((bf16[128,9,2,128]{3,2,1,0:T(2,128)(2,1)}), bf16[128,9,2,128]{3,2,1,0:T(2,128)(2,1)S(1)}, u32[]{:S(2)}, u32[]{:S(2)}) async-start(bf16[128,9,2,128]{3,2,1,0:T(2,128)(2,1)} %broadcast_in_dim.4), calls=%async_computation | async-start | bytes 1179648 | tf_op jit(solution)/shard_map/all_to_all | solution.py:29
  17.2 0.0 copy-done.6
  17.3 0.0 copy-done.7
  17.3 0.1 pad.7.clone
  17.4 0.0 collective-permute-done
  17.4 0.0 collective-permute-done.1
  17.4 0.1 pad_maximum_fusion
  17.5 5.3 %collective-permute-start.2 = (bf16[2,208,128]{2,1,0:T(8,128)(2,1)S(1)}, bf16[2,208,128]{2,1,0:T(8,128)(2,1)S(1)}, u32[]{:S(2)}, u32[]{:S(2)}) collective-permute-start(bf16[2,208,128]{2,1,0:T(8,128)(2,1)S(1)} %pad_maximum_fusion.1), channel_id=1, source_target_pairs={{0,16},{16,32},{32,48},{48,64},{64,80},{80,96},{96,112},{1,17},{17... | collective-permute-start | bytes 319496 | tf_op jit(solution)/shard_map/ppermute | solution.py:374
  22.8 1.9 %collective-permute-start.3 = (bf16[2,208,128]{2,1,0:T(8,128)(2,1)S(1)}, bf16[2,208,128]{2,1,0:T(8,128)(2,1)S(1)}, u32[]{:S(2)}, u32[]{:S(2)}) collective-permute-start(bf16[2,208,128]{2,1,0:T(8,128)(2,1)S(1)} %pad_maximum_fusion.2), channel_id=1, source_target_pairs={{16,0},{32,16},{48,32},{64,48},{80,64},{96,80},{112,96},{17,1},{33... | collective-permute-start | bytes 319496 | tf_op jit(solution)/shard_map/ppermute | solution.py:375
  24.8 2.0 %shard_map.67 = (bf16[2,7,208,768]{3,2,1,0:T(8,128)(2,1)S(1)}, bf16[2,2,768,1152]{3,2,1,0:T(8,128)(2,1)S(1)}) custom-call(bf16[16,192,128]{2,1,0:T(8,128)(2,1)S(1)} %copy-done.6, bf16[16,192,128]{2,1,0:T(8,128)(2,1)S(1)} %copy-done.7, bf16[2,16,16,128]{3,2,1,0:T(8,128)(2,1)S(1)} %copy.8.tail_ref), custom_call_target="tpu_custom_call" | custom-call | flops 4294967296 | bytes 16777216 | tf_op jit(solution)/shard_map/pallas_call | solution.py:101
  26.8 0.0 copy-start.1
  26.8 2.9 %copy-done.1 = bf16[2,2,768,1152]{3,2,1,0:T(8,128)(2,1)} copy-done((bf16[2,2,768,1152]{3,2,1,0:T(8,128)(2,1)}, bf16[2,2,768,1152]{3,2,1,0:T(8,128)(2,1)S(1)}, u32[]{:S(2)}) %copy-start.1) | copy-done | bytes 7077912
  29.6 0.0 collective-permute-done.2.above_ref
  29.6 3.4 %collective-permute-done.3.below_ref = bf16[2,208,128]{2,1,0:T(8,128)(2,1)S(1)} collective-permute-done((bf16[2,208,128]{2,1,0:T(8,128)(2,1)S(1)}, bf16[2,208,128]{2,1,0:T(8,128)(2,1)S(1)}, u32[]{:S(2)}, u32[]{:S(2)}) %collective-permute-start.3) | collective-permute-done | bytes 106528 | tf_op jit(solution)/shard_map/ppermute | solution.py:375
  33.1 0.7 shard_map.68
  33.8 0.0 copy-start
  33.8 2.1 %copy-done = bf16[2,7,208,768]{3,2,1,0:T(8,128)(2,1)} copy-done((bf16[2,7,208,768]{3,2,1,0:T(8,128)(2,1)}, bf16[2,7,208,768]{3,2,1,0:T(8,128)(2,1)S(1)}, u32[]{:S(2)}) %copy-start) | copy-done | bytes 4472856
  35.9 0.0 copy-start.4
  35.9 1.5 %copy-done.4 = bf16[2,2,768,384]{3,2,1,0:T(8,128)(2,1)} copy-done((bf16[2,2,768,384]{3,2,1,0:T(8,128)(2,1)}, bf16[2,2,768,384]{3,2,1,0:T(8,128)(2,1)S(1)}, u32[]{:S(2)}) %copy-start.4) | copy-done | bytes 2359320
  37.4 0.0 copy-start.5
  37.4 1.0 %copy-done.5 = bf16[2,2,208,768]{3,2,1,0:T(8,128)(2,1)} copy-done((bf16[2,2,208,768]{3,2,1,0:T(8,128)(2,1)}, bf16[2,2,208,768]{3,2,1,0:T(8,128)(2,1)S(1)}, u32[]{:S(2)}) %copy-start.5) | copy-done | bytes 1277976
  38.4 0.0 all-to-all-done
  38.4 0.0 copy-start.2
  38.4 0.8 copy-done.2
  39.2 15.2 %shard_map.69 = (f32[2304,128]{1,0:T(8,128)}, bf16[8,208,256]{2,1,0:T(8,128)(2,1)}) custom-call(bf16[2304,128]{1,0:T(8,128)(2,1)} %bitcast.25, bf16[2,7,208,768]{3,2,1,0:T(8,128)(2,1)} %copy-done, bf16[2,2,768,1152]{3,2,1,0:T(8,128)(2,1)} %copy-done.1, bf16[2,2,208,768]{3,2,1,0:T(8,128)(2,1)} %copy-done.5, bf16[2,2,768,384]{3,2,1,0:T(8,128)(2,1)} %copy-done.4), custom_call_target="tpu_custom_call" | custom-call | tf_op jit(solution)/shard_map/pallas_call | solution.py:301
  54.5 1.1 %dynamic-slice_bitcast_fusion = f32[64,9,2,128]{3,2,1,0:T(2,128)S(1)} fusion(f32[64,2,9,2,128]{4,3,2,1,0:T(2,128)} %bitcast.28, s32[]{:T(128)S(6)} %select_n.16), kind=kLoop, calls=%fused_computation.1 | loop fusion | bytes 1179652 | tf_op jit(solution)/shard_map/jit(dynamic_index_in_dim)/squeeze | solution.py:39
  55.6 0.1 collective-permute-start.6
  55.7 0.0 copy-start.8
  55.7 0.0 copy-start.3
  55.7 2.1 %collective-permute-done.6 = f32[64,9,2,128]{3,2,1,0:T(2,128)} collective-permute-done((f32[64,9,2,128]{3,2,1,0:T(2,128)S(1)}, f32[64,9,2,128]{3,2,1,0:T(2,128)}, u32[]{:S(2)}, u32[]{:S(2)}) %collective-permute-start.6) | collective-permute-done | bytes 589856 | tf_op jit(solution)/shard_map/ppermute | solution.py:40
  57.8 2.4 %bitcast_add_fusion = f32[64,9,2,128]{3,2,1,0:T(2,128)} fusion(f32[64,9,2,128]{3,2,1,0:T(2,128)} %collective-permute-done.6, f32[64,2,9,2,128]{4,3,2,1,0:T(2,128)} %bitcast.29, s32[]{:T(128)S(6)} %select_n.15), kind=kLoop, calls=%fused_computation | loop fusion | flops 147456 | bytes 1769476 | tf_op jit(solution)/shard_map/add | solution.py:42
  60.2 7.9 %all-to-all-start.1 = ((f32[64,9,2,128]{3,2,1,0:T(2,128)}), f32[64,9,2,128]{3,2,1,0:T(2,128)S(1)}, u32[]{:S(2)}, u32[]{:S(2)}) async-start(f32[64,9,2,128]{3,2,1,0:T(2,128)} %bitcast_add_fusion), calls=%async_computation.1 | async-start | bytes 1179648 | tf_op jit(solution)/shard_map/all_to_all | solution.py:42
  68.2 0.0 copy-done.8
  68.2 4.9 %collective-permute-start.4 = (bf16[208,128]{1,0:T(8,128)(2,1)S(1)}, bf16[208,128]{1,0:T(8,128)(2,1)S(1)}, u32[]{:S(2)}, u32[]{:S(2)}) collective-permute-start(bf16[208,128]{1,0:T(8,128)(2,1)S(1)} %get-tuple-element.20), channel_id=1, source_target_pairs={{0,16},{16,32},{32,48},{48,64},{64,80},{80,96},{96,112},{1,17},{17... | collective-permute-start | bytes 159752 | tf_op jit(solution)/shard_map/ppermute | solution.py:374
  73.1 1.9 %collective-permute-start.5 = (bf16[208,128]{1,0:T(8,128)(2,1)S(1)}, bf16[208,128]{1,0:T(8,128)(2,1)S(1)}, u32[]{:S(2)}, u32[]{:S(2)}) collective-permute-start(bf16[208,128]{1,0:T(8,128)(2,1)S(1)} %get-tuple-element.19), channel_id=1, source_target_pairs={{16,0},{32,16},{48,32},{64,48},{80,64},{96,80},{112,96},{17,1},{33... | collective-permute-start | bytes 159752 | tf_op jit(solution)/shard_map/ppermute | solution.py:375
  75.1 1.7 %collective-permute-done.4.above_ref = bf16[208,128]{1,0:T(8,128)(2,1)S(1)} collective-permute-done((bf16[208,128]{1,0:T(8,128)(2,1)S(1)}, bf16[208,128]{1,0:T(8,128)(2,1)S(1)}, u32[]{:S(2)}, u32[]{:S(2)}) %collective-permute-start.4) | collective-permute-done | bytes 53280 | tf_op jit(solution)/shard_map/ppermute | solution.py:374
  76.7 6.1 %collective-permute-done.5.below_ref = bf16[208,128]{1,0:T(8,128)(2,1)S(1)} collective-permute-done((bf16[208,128]{1,0:T(8,128)(2,1)S(1)}, bf16[208,128]{1,0:T(8,128)(2,1)S(1)}, u32[]{:S(2)}, u32[]{:S(2)}) %collective-permute-start.5) | collective-permute-done | bytes 53280 | tf_op jit(solution)/shard_map/ppermute | solution.py:375
  82.8 0.0 copy-done.3
  82.8 2.5 %shard_map.70 = bf16[16,192,128]{2,1,0:T(8,128)(2,1)} custom-call(bf16[2304,128]{1,0:T(8,128)(2,1)S(1)} %bitcast.26, bf16[8,208,256]{2,1,0:T(8,128)(2,1)S(1)} %copy-done.8, bf16[208,128]{1,0:T(8,128)(2,1)S(1)} %collective-permute-done.4.above_ref, bf16[208,128]{1,0:T(8,128)(2,1)S(1)} %collective-permute-done.5.below_ref, bf16[16,192,128]{2,1,0:T(8,128)(2,1)S(1)} %copy-done.7), custom_call_target="tpu_custom_call" | custom-call | flops 4294967296 | bytes 8388608 | tf_op jit(solution)/shard_map/pallas_call | solution.py:357
  85.3 0.0 all-to-all-done.1
  85.3 0.6 shard_map.71
  (10 shorter events, 0.1 us)
Async XLA Ops:
  0.6 16.6 %copy-start.6 = (bf16[16,192,128]{2,1,0:T(8,128)(2,1)S(1)}, bf16[16,192,128]{2,1,0:T(8,128)(2,1)}, u32[]{:S(2)}) copy-start(bf16[16,192,128]{2,1,0:T(8,128)(2,1)} %feat_ref.3) | copy-start | bytes 2359300
  0.6 16.6 %copy-start.7 = (bf16[16,192,128]{2,1,0:T(8,128)(2,1)S(1)}, bf16[16,192,128]{2,1,0:T(8,128)(2,1)}, u32[]{:S(2)}) copy-start(bf16[16,192,128]{2,1,0:T(8,128)(2,1)} %cot_ref.5) | copy-start | bytes 2359300
  1.6 15.8 %collective-permute-start = (bf16[2,16,2,128]{3,2,0,1:T(2,128)(2,1)S(1)}, bf16[2,16,2,128]{3,2,0,1:T(2,128)(2,1)S(1)}, u32[]{:S(2)}, u32[]{:S(2)}) collective-permute-start(bf16[2,16,2,128]{3,2,0,1:T(2,128)(2,1)S(1)} %pad_maximum_fusion.3), channel_id=1, source_target_pairs={{0,15},{1,0},{2,1},{3,2},{4,3},{5,4},{6,5},{7,6},{8,7},{9,8},{10,9... | collective-permute-start | bytes 49160 | tf_op jit(solution)/shard_map/ppermute | solution.py:385
  5.6 11.9 %collective-permute-start.1 = (bf16[2,16,2,128]{3,2,0,1:T(2,128)(2,1)S(1)}, bf16[2,16,2,128]{3,2,0,1:T(2,128)(2,1)S(1)}, u32[]{:S(2)}, u32[]{:S(2)}) collective-permute-start(bf16[2,16,2,128]{3,2,0,1:T(2,128)(2,1)S(1)} %pad_maximum_fusion.4), channel_id=1, source_target_pairs={{0,1},{1,2},{2,3},{3,4},{4,5},{5,6},{6,7},{7,8},{8,9},{9,10},{10,1... | collective-permute-start | bytes 49160 | tf_op jit(solution)/shard_map/ppermute | solution.py:384
  7.5 30.9 %all-to-all-start = ((bf16[128,9,2,128]{3,2,1,0:T(2,128)(2,1)}), bf16[128,9,2,128]{3,2,1,0:T(2,128)(2,1)S(1)}, u32[]{:S(2)}, u32[]{:S(2)}) async-start(bf16[128,9,2,128]{3,2,1,0:T(2,128)(2,1)} %broadcast_in_dim.4), calls=%async_computation | async-start | bytes 1179648 | tf_op jit(solution)/shard_map/all_to_all | solution.py:29
  17.5 12.1 %collective-permute-start.2 = (bf16[2,208,128]{2,1,0:T(8,128)(2,1)S(1)}, bf16[2,208,128]{2,1,0:T(8,128)(2,1)S(1)}, u32[]{:S(2)}, u32[]{:S(2)}) collective-permute-start(bf16[2,208,128]{2,1,0:T(8,128)(2,1)S(1)} %pad_maximum_fusion.1), channel_id=1, source_target_pairs={{0,16},{16,32},{32,48},{48,64},{64,80},{80,96},{96,112},{1,17},{17... | collective-permute-start | bytes 319496 | tf_op jit(solution)/shard_map/ppermute | solution.py:374
  22.8 10.2 %collective-permute-start.3 = (bf16[2,208,128]{2,1,0:T(8,128)(2,1)S(1)}, bf16[2,208,128]{2,1,0:T(8,128)(2,1)S(1)}, u32[]{:S(2)}, u32[]{:S(2)}) collective-permute-start(bf16[2,208,128]{2,1,0:T(8,128)(2,1)S(1)} %pad_maximum_fusion.2), channel_id=1, source_target_pairs={{16,0},{32,16},{48,32},{64,48},{80,64},{96,80},{112,96},{17,1},{33... | collective-permute-start | bytes 319496 | tf_op jit(solution)/shard_map/ppermute | solution.py:375
  26.8 2.9 %copy-start.1 = (bf16[2,2,768,1152]{3,2,1,0:T(8,128)(2,1)}, bf16[2,2,768,1152]{3,2,1,0:T(8,128)(2,1)S(1)}, u32[]{:S(2)}) copy-start(bf16[2,2,768,1152]{3,2,1,0:T(8,128)(2,1)S(1)} %get-tuple-element.12.inner_cells_ref) | copy-start | bytes 21233668
  33.8 2.1 %copy-start = (bf16[2,7,208,768]{3,2,1,0:T(8,128)(2,1)}, bf16[2,7,208,768]{3,2,1,0:T(8,128)(2,1)S(1)}, u32[]{:S(2)}) copy-start(bf16[2,7,208,768]{3,2,1,0:T(8,128)(2,1)S(1)} %get-tuple-element.11.near_ref.inner_taps_ref) | copy-start | bytes 13418500
  35.9 1.5 %copy-start.4 = (bf16[2,2,768,384]{3,2,1,0:T(8,128)(2,1)}, bf16[2,2,768,384]{3,2,1,0:T(8,128)(2,1)S(1)}, u32[]{:S(2)}) copy-start(bf16[2,2,768,384]{3,2,1,0:T(8,128)(2,1)S(1)} %get-tuple-element.14.outer_cells_ref) | copy-start | bytes 7077892
  37.4 1.0 %copy-start.5 = (bf16[2,2,208,768]{3,2,1,0:T(8,128)(2,1)}, bf16[2,2,208,768]{3,2,1,0:T(8,128)(2,1)S(1)}, u32[]{:S(2)}) copy-start(bf16[2,2,208,768]{3,2,1,0:T(8,128)(2,1)S(1)} %get-tuple-element.13.outer_taps_ref) | copy-start | bytes 3833860
  38.4 0.8 copy-start.2
  55.6 2.2 %collective-permute-start.6 = (f32[64,9,2,128]{3,2,1,0:T(2,128)S(1)}, f32[64,9,2,128]{3,2,1,0:T(2,128)}, u32[]{:S(2)}, u32[]{:S(2)}) collective-permute-start(f32[64,9,2,128]{3,2,1,0:T(2,128)S(1)} %dynamic-slice_bitcast_fusion), channel_id=1, source_target_pairs={{0,1},{1,0},{2,3},{3,2},{4,5},{5,4},{6,7},{7,6},{8,9},{9,8},{10,11... | collective-permute-start | bytes 1769480 | tf_op jit(solution)/shard_map/ppermute | solution.py:40
  55.7 12.4 %copy-start.8 = (bf16[8,208,256]{2,1,0:T(8,128)(2,1)S(1)}, bf16[8,208,256]{2,1,0:T(8,128)(2,1)}, u32[]{:S(2)}) copy-start(bf16[8,208,256]{2,1,0:T(8,128)(2,1)} %get-tuple-element.15.back_ref) | copy-start | bytes 2555908
  55.7 27.0 %copy-start.3 = (bf16[128,9,2,128]{3,2,1,0:T(2,128)(2,1)S(1)}, bf16[128,9,2,128]{3,2,1,0:T(2,128)(2,1)}, u32[]{:S(2)}) copy-start(bf16[128,9,2,128]{3,2,1,0:T(2,128)(2,1)} %copy-done.2) | copy-start | bytes 1769476
  60.2 25.1 %all-to-all-start.1 = ((f32[64,9,2,128]{3,2,1,0:T(2,128)}), f32[64,9,2,128]{3,2,1,0:T(2,128)S(1)}, u32[]{:S(2)}, u32[]{:S(2)}) async-start(f32[64,9,2,128]{3,2,1,0:T(2,128)} %bitcast_add_fusion), calls=%async_computation.1 | async-start | bytes 1179648 | tf_op jit(solution)/shard_map/all_to_all | solution.py:42
  68.2 8.5 %collective-permute-start.4 = (bf16[208,128]{1,0:T(8,128)(2,1)S(1)}, bf16[208,128]{1,0:T(8,128)(2,1)S(1)}, u32[]{:S(2)}, u32[]{:S(2)}) collective-permute-start(bf16[208,128]{1,0:T(8,128)(2,1)S(1)} %get-tuple-element.20), channel_id=1, source_target_pairs={{0,16},{16,32},{32,48},{48,64},{64,80},{80,96},{96,112},{1,17},{17... | collective-permute-start | bytes 159752 | tf_op jit(solution)/shard_map/ppermute | solution.py:374
  73.1 9.6 %collective-permute-start.5 = (bf16[208,128]{1,0:T(8,128)(2,1)S(1)}, bf16[208,128]{1,0:T(8,128)(2,1)S(1)}, u32[]{:S(2)}, u32[]{:S(2)}) collective-permute-start(bf16[208,128]{1,0:T(8,128)(2,1)S(1)} %get-tuple-element.19), channel_id=1, source_target_pairs={{16,0},{32,16},{48,32},{64,48},{80,64},{96,80},{112,96},{17,1},{33... | collective-permute-start | bytes 159752 | tf_op jit(solution)/shard_map/ppermute | solution.py:375

commit v4 on v3

v4 whole, which is shorter than its diff:
```python
import functools

import jax
import jax.numpy as jnp
from jax import lax
from jax.experimental import pallas as pl
from jax.experimental.pallas import tpu as pltpu
from jax.sharding import PartitionSpec as P


AXES = ("lat", "lon")
BF16 = jnp.bfloat16
F32 = jnp.float32
PREP_LIMIT = 4 << 20
MIDDLE_LIMIT = 12 << 20
FINAL_LIMIT = 12 << 20


def ring(axis, step, periodic):
    count = lax.axis_size(axis)
    pairs = [(i, (i + step) % count) for i in range(count)]
    if not periodic:
        pairs = [(i, j) for i, j in pairs if j == i + step]
    return pairs


def gather_kernels(w_first, w_second):
    count = lax.axis_size(AXES)
    rows, chans = w_first.shape
    mine = jnp.stack([w_first, w_second], 1)[None]
    sent = jnp.broadcast_to(mine, (count, rows, 2, chans))
    return lax.all_to_all(sent, AXES, 0, 0, tiled=True).reshape(-1, chans)


def scatter_sums(keep, send):
    count = lax.axis_size(AXES)
    rows, chans = keep.shape
    rows //= count
    got = lax.ppermute(send, AXES, [(i, i ^ 1) for i in range(count)])
    groups = [list(range(parity, count, 2)) for parity in range(2)]
    parts = join(keep, got).reshape(count // 2, rows, 2, chans)
    parts = lax.all_to_all(parts, AXES, 0, 0, tiled=True, axis_index_groups=groups)
    return add_parts(parts.reshape(-1, chans), rows)


def join_kernel(keep_ref, got_ref, out_ref):
    out_ref[...] = keep_ref[...] + got_ref[...]


def join(keep, got):
    whole = pl.BlockSpec(memory_space=pltpu.VMEM)
    return pl.pallas_call(
        join_kernel, out_shape=jax.ShapeDtypeStruct(keep.shape, F32),
        in_specs=[whole] * 2, out_specs=whole,
        compiler_params=pltpu.CompilerParams(vmem_limit_bytes=4 << 20),
    )(keep, got)


def add_kernel(parts_ref, first_ref, second_ref):
    rows = first_ref.shape[0]
    groups = parts_ref.shape[0] // (2 * rows)
    for r in range(rows):
        for out_ref, at in ((first_ref, 2 * r), (second_ref, 2 * r + 1)):
            out_ref[r : r + 1] = jnp.sum(
                parts_ref[pl.ds(at, groups, stride=2 * rows)], 0, keepdims=True
            )


def add_parts(parts, rows):
    whole = pl.BlockSpec(memory_space=pltpu.VMEM)
    out = jax.ShapeDtypeStruct((rows, parts.shape[1]), F32)
    return pl.pallas_call(
        add_kernel, out_shape=(out, out), in_specs=[whole], out_specs=(whole, whole),
        compiler_params=pltpu.CompilerParams(vmem_limit_bytes=4 << 20),
    )(parts)


def shifted(row):
    wide = row.astype(F32)
    left = pltpu.roll(wide, 1, 0).astype(BF16)
    right = pltpu.roll(wide, wide.shape[0] - 1, 0).astype(BF16)
    return left, row, right


def paired(first, second):
    return jnp.concatenate([part for both in zip(first, second) for part in both], 1)


def inner_kernel(feat_ref, cot_ref, tail_ref, taps_ref, cells_ref):
    rows, cols, _ = feat_ref.shape
    for field, own_ref in enumerate((feat_ref, cot_ref)):
        seen = [
            shifted(jnp.concatenate([own_ref[r], tail_ref[field, r]], 0)) for r in range(rows)
        ]
        for p in range(rows // 2):
            taps_ref[field, p] = paired(seen[2 * p], seen[2 * p + 1])
        pairs = [paired(seen[r], seen[r + 1])[:cols] for r in range(1, rows - 2, 2)]
        for p in range(len(pairs) - 1):
            at = 2 * cols * (p // 2)
            cells_ref[field, 1 - p % 2, :, at : at + 2 * cols] = jnp.concatenate(
                pairs[p : p + 2], 0
            ).T


def inner(features, cotangent, tail):
    rows, cols, chans = features.shape
    width = cols + tail.shape[2]
    whole = pl.BlockSpec(memory_space=pltpu.VMEM)
    return pl.pallas_call(
        inner_kernel,
        out_shape=(
            jax.ShapeDtypeStruct((2, rows // 2, width, 6 * chans), BF16),
            jax.ShapeDtypeStruct((2, 2, 6 * chans, cols * (rows // 2 - 2)), BF16),
        ),
        in_specs=[whole] * 3,
        out_specs=(whole, whole),
        compiler_params=pltpu.CompilerParams(vmem_limit_bytes=PREP_LIMIT),
        cost_estimate=pl.CostEstimate(flops=1 << 32, bytes_accessed=16 << 20, transcendentals=0),
    )(features, cotangent, tail)


def outer_kernel(above_ref, below_ref, near_ref, taps_ref, cells_ref):
    pairs = near_ref.shape[1]
    chans = above_ref.shape[3]
    cols = cells_ref.shape[3] // 2
    for field in range(2):

        def near(r):
            p, r = divmod(r % (2 * pairs), 2)
            at = [(2 * b + r) * chans for b in range(3)]
            return [near_ref[field, p, :, i : i + chans] for i in at]

        above = [shifted(above_ref[field, r]) for r in range(2)]
        below = [shifted(below_ref[field, r]) for r in range(2)]
        taps_ref[field, 0] = paired(*above)
        taps_ref[field, 1] = paired(*below)
        cells = [paired(above[1], near(0)), paired(near(1), near(2))]
        cells_ref[field, 0] = jnp.concatenate([cell[:cols] for cell in cells], 0).T
        cells = [paired(near(-3), near(-2)), paired(near(-1), below[0])]
        cells_ref[field, 1] = jnp.concatenate([cell[:cols] for cell in cells], 0).T


def outer(above, below, near, cols):
    _, _, width, chans = above.shape
    whole = pl.BlockSpec(memory_space=pltpu.VMEM)
    return pl.pallas_call(
        outer_kernel,
        out_shape=(
            jax.ShapeDtypeStruct((2, 2, width, 6 * chans), BF16),
            jax.ShapeDtypeStruct((2, 2, 6 * chans, 2 * cols), BF16),
        ),
        in_specs=[whole] * 3,
        out_specs=(whole, whole),
        compiler_params=pltpu.CompilerParams(vmem_limit_bytes=PREP_LIMIT),
        cost_estimate=pl.CostEstimate(flops=1 << 30, bytes_accessed=4 << 20, transcendentals=0),
    )(above, below, near)


def tap_rows(a, b, chans):
    tap = (a + 1) * 3 + b + 1
    return slice(tap * chans, (tap + 1) * chans)


def fill_plain(weight_ref, table_ref):
    chans = weight_ref.shape[1]
    for half in range(2):
        for b in range(3):
            for source in range(2):
                for target in range(2):
                    a = 2 * half + source - target - 1
                    at = (2 * b + source) * chans
                    if abs(a) <= 1:
                        block = weight_ref[tap_rows(a, b - 1, chans)]
                    else:
                        block = jnp.zeros((chans, chans), BF16)
                    table_ref[half, at : at + chans, target * chans : (target + 1) * chans] = block


def fill_turned(weight_ref, table_ref):
    chans = weight_ref.shape[1]
    for half in range(2):
        for b in range(3):
            for source in range(2):
                for target in range(2):
                    a = 2 * half + source - target - 1
                    at = (2 * b + source) * chans
                    if abs(a) <= 1:
                        block = weight_ref[tap_rows(-a, 1 - b, chans)]
                    else:
                        block = jnp.zeros((chans, chans), BF16)
                    table_ref[half, target * chans : (target + 1) * chans, at : at + chans] = block


def plain(lhs, rhs):
    return lax.dot_general(lhs, rhs, (((1,), (0,)), ((), ())), preferred_element_type=F32)


def turned(lhs, rhs):
    return lax.dot_general(lhs, rhs, (((1,), (1,)), ((), ())), preferred_element_type=F32)


def middle_kernel(
    own_rows, place_ref, both_ref, inner_taps_ref, inner_cells_ref, outer_taps_ref, outer_cells_ref,
    keep_ref, send_ref, back_ref,
    wide_ref, sums_ref, one_ref, two_ref, plain_ref, turned_ref, slope_ref, act_ref, own_ref,
):
    pairs, width, lanes = back_ref.shape
    chans = lanes // 2
    cols = width - 16
    taps = one_ref.shape[0]
    wide_ref[...] = both_ref[...].astype(F32)
    one_ref[...] = wide_ref[pl.ds(0, taps, stride=2)].astype(BF16)
    two_ref[...] = wide_ref[pl.ds(1, taps, stride=2)].astype(BF16)
    fill_plain(one_ref, plain_ref)
    fill_turned(two_ref, turned_ref)

    def rows_of(field, first, count):
        parts = []
        for p in range(first, first + count):
            if p == 0:
                parts.append(outer_taps_ref[field, 0])
            elif p == pairs:
                parts.append(outer_taps_ref[field, 1])
            else:
                parts.append(inner_taps_ref[field, p - 1])
        return jnp.concatenate(parts, 0)

    def cells_of(field, shift):
        parts = [outer_cells_ref[field, shift], inner_cells_ref[field, shift]]
        return jnp.concatenate(parts if shift == 0 else parts[::-1], 1)

    lane = lax.broadcasted_iota(jnp.int32, (1, lanes), 1)
    step = pairs // 3
    for c in range(0, pairs, step):
        pre = plain(rows_of(0, c, step), plain_ref[0]) + plain(rows_of(0, c + 1, step), plain_ref[1])
        sigma = jax.nn.sigmoid(pre)
        act = (pre * sigma).astype(BF16)
        slope_ref[...] = sigma * (1.0 + pre * (1.0 - sigma))
        back = turned(rows_of(1, c, step), turned_ref[0]) + turned(
            rows_of(1, c + 1, step), turned_ref[1]
        )
        back = (back * slope_ref[...]).astype(BF16)
        for p in range(step):
            part = back[width * p : width * (p + 1)]
            for out_ref, rows in ((act_ref, act[width * p : width * p + cols]), (own_ref, part[:cols])):
                at = cols * (c + p)
                if c + p < pairs - 1:
                    out_ref[at : at + cols, :chans] = rows[:, chans:]
                if c + p > 0:
                    out_ref[at - cols : at, chans:] = rows[:, :chans]
            if c + p == 0:
                part = jnp.where((lane < chans) & (place_ref[1] == 1), 0.0, part.astype(F32)).astype(BF16)
            if c + p == pairs - 1:
                part = jnp.where((lane >= chans) & (place_ref[2] == 1), 0.0, part.astype(F32)).astype(BF16)
            back_ref[c + p] = part
    seconds = [plain(cells_of(1, d), act_ref[...]) for d in range(2)]
    firsts = [plain(cells_of(0, d), own_ref[...]) for d in range(2)]
    for a in range(-1, 2):
        for b in range(3):

            def summed(halves):
                total = None
                for half in range(2):
                    for source in range(2):
                        target = 2 * half + source - 1 - a
                        if target in (0, 1):
                            at = (2 * b + source) * chans
                            block = halves[half][at : at + chans, target * chans : (target + 1) * chans]
                            total = block if total is None else total + block
                return total

            at = tap_rows(a, b - 1, chans).start
            sums_ref[pl.ds(2 * at, chans, stride=2)] = summed(firsts)
            at = tap_rows(-a, 1 - b, chans).start
            sums_ref[pl.ds(2 * at + 1, chans, stride=2)] = summed(seconds).T
    core = place_ref[0]
    groups = keep_ref.shape[0] // own_rows
    for g in range(groups):
        out = pl.ds(own_rows * g, own_rows)
        keep_ref[out] = sums_ref[pl.ds(own_rows * (2 * g + core), own_rows)]
        send_ref[out] = sums_ref[pl.ds(own_rows * (2 * g + 1 - core), own_rows)]


def middle(place, both, inner_parts, outer_parts, own_rows):
    inner_taps, inner_cells = inner_parts
    outer_taps, outer_cells = outer_parts
    pairs = inner_taps.shape[1] + 1
    width = inner_taps.shape[2]
    rows, chans = both.shape
    lanes = 2 * chans
    cells = (pairs - 1) * (width - 16)
    whole = pl.BlockSpec(memory_space=pltpu.VMEM)
    return pl.pallas_call(
        functools.partial(middle_kernel, own_rows),
        out_shape=(
            jax.ShapeDtypeStruct((rows // 2, chans), F32),
            jax.ShapeDtypeStruct((rows // 2, chans), F32),
            jax.ShapeDtypeStruct((pairs, width, lanes), BF16),
        ),
        in_specs=[pl.BlockSpec(memory_space=pltpu.SMEM)] + [whole] * 5,
        out_specs=(whole,) * 3,
        scratch_shapes=[
            pltpu.VMEM((rows, chans), F32),
            pltpu.VMEM((rows, chans), F32),
            pltpu.VMEM((rows // 2, chans), BF16),
            pltpu.VMEM((rows // 2, chans), BF16),
            pltpu.VMEM((2, 3 * lanes, lanes), BF16),
            pltpu.VMEM((2, lanes, 3 * lanes), BF16),
            pltpu.VMEM((pairs // 3 * width, lanes), F32),
            pltpu.VMEM((cells, lanes), BF16),
            pltpu.VMEM((cells, lanes), BF16),
        ],
        compiler_params=pltpu.CompilerParams(vmem_limit_bytes=MIDDLE_LIMIT),
    )(place, both, inner_taps, inner_cells, outer_taps, outer_cells)


def final_kernel(both_ref, back_ref, cot_ref, out_ref, wide_ref, one_ref, turned_ref, taps_ref):
    pairs, _, _ = back_ref.shape
    _, cols, chans = cot_ref.shape
    wide_ref[...] = both_ref[...].astype(F32)
    one_ref[...] = wide_ref[pl.ds(0, one_ref.shape[0], stride=2)].astype(BF16)
    fill_turned(one_ref, turned_ref)
    for p in range(pairs):
        taps = jnp.concatenate(shifted(back_ref[p]), 1)
        taps_ref[cols * p : cols * (p + 1)] = taps[:cols]
    step = (pairs - 1) // 2
    for c in range(0, pairs - 1, step):
        total = turned(taps_ref[cols * c : cols * (c + step)], turned_ref[0]) + turned(
            taps_ref[cols * (c + 1) : cols * (c + step + 1)], turned_ref[1]
        )
        for p in range(step):
            for r in range(2):
                row = 2 * (c + p) + r
                part = total[cols * p : cols * (p + 1), r * chans : (r + 1) * chans]
                out_ref[row] = (part + cot_ref[row].astype(F32)).astype(BF16)


def final(both, back, cotangent):
    pairs, _, lanes = back.shape
    _, cols, chans = cotangent.shape
    whole = pl.BlockSpec(memory_space=pltpu.VMEM)
    return pl.pallas_call(
        final_kernel,
        out_shape=jax.ShapeDtypeStruct(cotangent.shape, BF16),
        in_specs=[whole] * 3,
        out_specs=whole,
        scratch_shapes=[
            pltpu.VMEM(both.shape, F32),
            pltpu.VMEM((both.shape[0] // 2, chans), BF16),
            pltpu.VMEM((2, lanes, 3 * lanes), BF16),
            pltpu.VMEM((pairs * cols, 3 * lanes), BF16),
        ],
        compiler_params=pltpu.CompilerParams(vmem_limit_bytes=FINAL_LIMIT),
        cost_estimate=pl.CostEstimate(flops=1 << 32, bytes_accessed=8 << 20, transcendentals=0),
    )(both, back, cotangent)


def layer(features, cotangent, w_first, w_second):
    both = gather_kernels(w_first, w_second)
    rows, cols, chans = features.shape
    left = jnp.stack([features[:, -2:], cotangent[:, -2:]])
    right = jnp.stack([features[:, :2], cotangent[:, :2]])
    left = lax.ppermute(left, "lon", ring("lon", 1, True))
    right = lax.ppermute(right, "lon", ring("lon", -1, True))
    tail = jnp.concatenate([right, jnp.zeros((2, rows, 12, chans), BF16), left], 2)

    def whole_rows(at):
        return jnp.concatenate([jnp.stack([features[at], cotangent[at]]), tail[:, at]], 2)

    above = lax.ppermute(whole_rows(slice(rows - 2, rows)), "lat", ring("lat", 1, False))
    below = lax.ppermute(whole_rows(slice(0, 2)), "lat", ring("lat", -1, False))
    at = lax.axis_index("lat")
    place = jnp.stack(
        [
            lax.axis_index(AXES) % 2,
            (at == 0).astype(jnp.int32),
            (at == lax.axis_size("lat") - 1).astype(jnp.int32),
        ]
    )
    both, own_tail = lax.optimization_barrier((both, tail))
    inner_parts = inner(features, cotangent, own_tail)
    outer_parts = outer(above, below, inner_parts[0], cols)
    keep, send, back = middle(place, both, inner_parts, outer_parts, 2 * w_first.shape[0])
    grads = scatter_sums(keep, send)
    return final(both, back, cotangent), *grads


def solution(mesh):
    in_specs = (
        P("lat", "lon", None),
        P("lat", "lon", None),
        P(("lat", "lon"), None),
        P(("lat", "lon"), None),
    )
    out_specs = (P("lat", "lon", None), P(("lat", "lon"), None), P(("lat", "lon"), None))
    return jax.shard_map(layer, mesh=mesh, in_specs=in_specs, out_specs=out_specs, check_vma=False)
```

time: 86.4 us -> 68.4 us (0.79)
  Pallas kernels: 21.1 us -> 13.3 us
  starting transfers between devices: 35.8 us -> 28.3 us
  local copies, waits for them, and re-layouts: 11.7 us -> 5.4 us
  waiting for transfers between devices: 13.2 us -> 18.5 us
  other arithmetic: 3.29 us -> 0.97 us
    all_to_all x1, waiting for transfers between devices: 0.01 us -> 10.3 us  [scatter_sums(): lax.all_to_all(parts, AXES, 0, 0, tiled=True, axis_index_groups=groups)]
    ppermute x6 -> x4, waiting for transfers between devices: 11.2 us -> 2.33 us  [the longest x1 2.32 us: layer(): below = lax.ppermute(whole_rows(slice(0, 2)), 'lat', ring('lat', -1, False))]
    pallas_call x2 -> x3, Pallas kernels: 17.2 us -> 9.46 us  [the longest x1 6.57 us: middle(): pl.pallas_call(functools.partial(middle_kernel, own_rows), out_shape=(jax...]
    ppermute x6 -> x4, starting transfers between devices: 18 us -> 11.2 us  [the longest x1 5.26 us: layer(): lax.ppermute(whole_rows(slice(rows - 2, rows)), 'lat', ring('lat', 1, Fal...]
    unnamed x18 -> x6, local copies, waits for them, and re-layouts: 8.32 us -> 2.27 us
    all_to_all x1, waiting for transfers between devices: 0.01 us -> 3.97 us  [gather_kernels(): return lax.all_to_all(sent, AXES, 0, 0, tiled=True).reshape(-1, chans)]
    add x1 -> x0, other arithmetic: 2.4 us -> none  [scatter_sums(): keep + got]
    squeeze x3 -> x0, local copies, waits for them, and re-layouts: 1.15 us -> none  [the longest x1 1.14 us: scatter_sums(): send = lax.dynamic_index_in_dim(both, 1 - core, 1, keepdims=False)]
  transfers between devices with their start and end apart: 9 -> 7, of which waited for: 4 -> 4; matrix products, arithmetic and copies ran while one was open for 2% -> 5% of each run, Pallas kernels for 6% -> 7%
where the time goes in v4:
time: 68.4 us; the launch traced here: 67.3 us
  starting transfers between devices  28.3 us (41%)
  waiting for transfers between devices  18.5 us (27%)
  Pallas kernels  13.3 us (19%)
  local copies, waits for them, and re-layouts  5.4 us (8%)
  other arithmetic  0.97 us (1%)
  between operations  0.82 us (1%)
    all_to_all x1, waiting for transfers between devices, scatter_sums(): lax.all_to_all(parts, AXES, 0, 0, tiled=True, axis_index_groups=groups)  10.3 us
    all_to_all x1, starting transfers between devices, gather_kernels(): return lax.all_to_all(sent, AXES, 0, 0, tiled=True).reshape(-1, chans)  9.1 us
    all_to_all x1, starting transfers between devices, scatter_sums(): lax.all_to_all(parts, AXES, 0, 0, tiled=True, axis_index_groups=groups)  7.92 us
    pallas_call x1, Pallas kernels, middle(): pl.pallas_call(functools.partial(middle_kernel, own_rows), out_shape=(jax...  6.57 us
    ppermute x1, starting transfers between devices, layer(): lax.ppermute(whole_rows(slice(rows - 2, rows)), 'lat', ring('lat', 1, Fal...  5.26 us
    all_to_all x1, waiting for transfers between devices, gather_kernels(): return lax.all_to_all(sent, AXES, 0, 0, tiled=True).reshape(-1, chans)  3.97 us
    ppermute x1, starting transfers between devices, layer(): right = lax.ppermute(right, 'lon', ring('lon', -1, True))  3.9 us
    pallas_call x1, Pallas kernels, final(): pl.pallas_call(final_kernel, out_shape=jax.ShapeDtypeStruct(cotangent.sha...  2.53 us
  transfers between devices with their start and end apart: 7, of which 4 were waited for; matrix products, arithmetic and copies ran while one was open for 5% of the time, Pallas kernels for 7%

profile of v4, /device:TPU:6, one launch (start us, length us, event | category | flops | bytes accessed | tf_op | source)
XLA Modules:
  0.0 67.3 jit_solution(2522732689842597281)
XLA Ops:
  0.6 0.8 %slice_bitcast_fusion.6 = (bf16[1,16,2,128]{3,2,1,0:T(2,128)(2,1)S(1)}, bf16[1,16,2,128]{3,2,1,0:T(2,128)(2,1)S(1)}, bf16[1,16,2,128]{3,2,1,0:T(2,128)(2,1)S(1)}, bf16[1,16,2,128]{3,2,1,0:T(2,128)(2,1)S(1)}) fusion(bf16[16,192,128]{2,1,0:T(8,128)(2,1)} %cot_ref.3, bf16[16,192,128]{2,1,0:T(8,128)(2,1)} %feat_ref.1), kind=kLoop, calls=%fused_computation.12 | loop fusion | bytes 65536 | tf_op jit(solution)/shard_map/stack | solution.py:362
  1.5 0.1 collective-permute-start.1
  1.6 3.9 %collective-permute-start = (bf16[2,16,2,128]{3,2,1,0:T(2,128)(2,1)S(1)}, bf16[2,16,2,128]{3,2,1,0:T(2,128)(2,1)S(1)}, u32[]{:S(2)}, u32[]{:S(2)}) collective-permute-start(bf16[2,16,2,128]{3,2,1,0:T(2,128)(2,1)S(1)} %pad_maximum_fusion.3), channel_id=1, source_target_pairs={{0,15},{1,0},{2,1},{3,2},{4,3},{5,4},{6,5},{7,6},{8,7},{9,8},{10,9... | collective-permute-start | bytes 49160 | tf_op jit(solution)/shard_map/ppermute | solution.py:364
  5.5 0.7 %pad_maximum_fusion.5 = bf16[9,2,128]{2,0,1:T(8,128)(2,1)S(1)} fusion(bf16[9,1,128]{2,0,1:T(8,128)(2,1)} %bitcast.27, bf16[9,1,128]{2,0,1:T(8,128)(2,1)} %bitcast.28), kind=kLoop, calls=%fused_computation.9 | loop fusion | flops 2304 | bytes 9216 | tf_op jit(solution)/shard_map/stack | solution.py:30
  6.3 1.1 %broadcast_in_dim.4 = bf16[128,9,2,128]{3,2,1,0:T(2,128)(2,1)} broadcast(bf16[9,2,128]{2,1,0:T(2,128)(2,1)S(1)} %copy.7), dimensions={1,2,3} | broadcast | bytes 594432 | tf_op jit(solution)/shard_map/broadcast_in_dim | solution.py:31
  7.4 9.1 %all-to-all-start = ((bf16[128,9,2,128]{3,2,1,0:T(2,128)(2,1)}), bf16[128,9,2,128]{3,2,1,0:T(2,128)(2,1)S(1)}, u32[]{:S(2)}, u32[]{:S(2)}) async-start(bf16[128,9,2,128]{3,2,1,0:T(2,128)(2,1)} %broadcast_in_dim.4), calls=%async_computation | async-start | bytes 1179648 | tf_op jit(solution)/shard_map/all_to_all | solution.py:32
  16.5 1.1 %slice_bitcast_fusion = (bf16[1,2,192,128]{3,2,1,0:T(8,128)(2,1)S(1)}, bf16[1,2,192,128]{3,2,1,0:T(8,128)(2,1)S(1)}, bf16[1,2,192,128]{3,2,1,0:T(8,128)(2,1)S(1)}, bf16[1,2,192,128]{3,2,1,0:T(8,128)(2,1)S(1)}) fusion(bf16[16,192,128]{2,1,0:T(8,128)(2,1)} %cot_ref.3, bf16[16,192,128]{2,1,0:T(8,128)(2,1)} %feat_ref.1), kind=kLoop, calls=%fused_computation.3 | loop fusion | bytes 786432 | tf_op jit(solution)/shard_map/stack | solution.py:368
  17.6 0.1 pad_add_fusion.place_ref
  17.7 0.1 pad.10.clone
  17.7 0.0 collective-permute-done.1
  17.7 0.0 collective-permute-done
  17.8 0.1 pad_maximum_fusion.2.tail_ref
  17.9 5.3 %collective-permute-start.2 = (bf16[2,2,208,128]{3,2,1,0:T(8,128)(2,1)S(1)}, bf16[2,2,208,128]{3,2,1,0:T(8,128)(2,1)S(1)}, u32[]{:S(2)}, u32[]{:S(2)}) collective-permute-start(bf16[2,2,208,128]{3,2,1,0:T(8,128)(2,1)S(1)} %pad_maximum_fusion), channel_id=1, source_target_pairs={{0,16},{16,32},{32,48},{48,64},{64,80},{80,96},{96,112},{1,17},{17... | collective-permute-start | bytes 638984 | tf_op jit(solution)/shard_map/ppermute | solution.py:370
  23.2 1.9 %collective-permute-start.3 = (bf16[2,2,208,128]{3,2,1,0:T(8,128)(2,1)S(1)}, bf16[2,2,208,128]{3,2,1,0:T(8,128)(2,1)S(1)}, u32[]{:S(2)}, u32[]{:S(2)}) collective-permute-start(bf16[2,2,208,128]{3,2,1,0:T(8,128)(2,1)S(1)} %pad_maximum_fusion.1), channel_id=1, source_target_pairs={{16,0},{32,16},{48,32},{64,48},{80,64},{96,80},{112,96},{17,1},{33... | collective-permute-start | bytes 638984 | tf_op jit(solution)/shard_map/ppermute | solution.py:371
  25.1 4.0 %all-to-all-done = bf16[128,9,2,128]{3,2,1,0:T(2,128)(2,1)S(1)} async-done(((bf16[128,9,2,128]{3,2,1,0:T(2,128)(2,1)}), bf16[128,9,2,128]{3,2,1,0:T(2,128)(2,1)S(1)}, u32[]{:S(2)}, u32[]{:S(2)}) %all-to-all-start) | async-done | bytes 589856 | tf_op jit(solution)/shard_map/all_to_all | solution.py:32
  29.1 0.0 copy-start
  29.1 1.1 %copy-done = bf16[16,192,128]{2,1,0:T(8,128)(2,1)S(1)} copy-done((bf16[16,192,128]{2,1,0:T(8,128)(2,1)S(1)}, bf16[16,192,128]{2,1,0:T(8,128)(2,1)}, u32[]{:S(2)}) %copy-start) | copy-done | bytes 786456
  30.2 0.0 copy-start.1
  30.2 1.1 %copy-done.1 = bf16[16,192,128]{2,1,0:T(8,128)(2,1)S(1)} copy-done((bf16[16,192,128]{2,1,0:T(8,128)(2,1)S(1)}, bf16[16,192,128]{2,1,0:T(8,128)(2,1)}, u32[]{:S(2)}) %copy-start.1) | copy-done | bytes 786456
  31.4 2.0 %shard_map.67 = (bf16[2,8,208,768]{3,2,1,0:T(8,128)(2,1)S(1)}, bf16[2,2,768,1152]{3,2,1,0:T(8,128)(2,1)S(1)}) custom-call(bf16[16,192,128]{2,1,0:T(8,128)(2,1)S(1)} %copy-done, bf16[16,192,128]{2,1,0:T(8,128)(2,1)S(1)} %copy-done.1, bf16[2,16,16,128]{3,2,1,0:T(8,128)(2,1)S(1)} %pad_maximum_fusion.2.tail_ref), custom_call_target="tpu_custom_call" | custom-call | flops 4294967296 | bytes 16777216 | tf_op jit(solution)/shard_map/pallas_call | solution.py:109
  33.4 0.0 collective-permute-done.2.above_ref
  33.4 2.3 %collective-permute-done.3.below_ref = bf16[2,2,208,128]{3,2,1,0:T(8,128)(2,1)S(1)} collective-permute-done((bf16[2,2,208,128]{3,2,1,0:T(8,128)(2,1)S(1)}, bf16[2,2,208,128]{3,2,1,0:T(8,128)(2,1)S(1)}, u32[]{:S(2)}, u32[]{:S(2)}) %collective-permute-start.3) | collective-permute-done | bytes 213024 | tf_op jit(solution)/shard_map/ppermute | solution.py:371
  35.7 0.7 %shard_map.68 = (bf16[2,2,208,768]{3,2,1,0:T(8,128)(2,1)S(1)}, bf16[2,2,768,384]{3,2,1,0:T(8,128)(2,1)S(1)}) custom-call(bf16[2,2,208,128]{3,2,1,0:T(8,128)(2,1)S(1)} %collective-permute-done.2.above_ref, bf16[2,2,208,128]{3,2,1,0:T(8,128)(2,1)S(1)} %collective-permute-done.3.below_ref, bf16[2,8,208,768]{3,2,1,0:T(8,128)(2,1)S(1)} %get-tuple-element.16.near_ref.inner_taps_ref), custom_call_target="tpu_custom_call" | custom-call | flops 1073741824 | bytes 4194304 | tf_op jit(solution)/shard_map/pallas_call | solution.py:146
  36.4 0.0 copy-start.2
  36.4 6.6 %shard_map.69 = (f32[1152,128]{1,0:T(8,128)S(1)}, f32[1152,128]{1,0:T(8,128)S(1)}, bf16[9,208,256]{2,1,0:T(8,128)(2,1)S(1)}) custom-call(s32[3]{0:T(128)S(1)} %pad_add_fusion.place_ref, bf16[2304,128]{1,0:T(8,128)(2,1)S(1)} %bitcast.24, bf16[2,8,208,768]{3,2,1,0:T(8,128)(2,1)S(1)} %get-tuple-element.16.near_ref.inner_taps_ref, ...), custom_call_target="tpu_custom_call" | custom-call | tf_op jit(solution)/shard_map/pallas_call | solution.py:293
  43.0 0.1 collective-permute-start.4
  43.1 2.0 %collective-permute-done.4.got_ref = f32[1152,128]{1,0:T(8,128)S(1)} collective-permute-done((f32[1152,128]{1,0:T(8,128)S(1)}, f32[1152,128]{1,0:T(8,128)S(1)}, u32[]{:S(2)}, u32[]{:S(2)}) %collective-permute-start.4) | collective-permute-done | bytes 589856 | tf_op jit(solution)/shard_map/ppermute | solution.py:39
  45.1 0.9 %shard_map.71 = f32[1152,128]{1,0:T(8,128)} custom-call(f32[1152,128]{1,0:T(8,128)S(1)} %get-tuple-element.21.keep_ref, f32[1152,128]{1,0:T(8,128)S(1)} %collective-permute-done.4.got_ref), custom_call_target="tpu_custom_call" | custom-call | tf_op jit(solution)/shard_map/pallas_call | solution.py:52
  46.0 7.9 %all-to-all-start.1 = ((f32[64,9,2,128]{3,2,1,0:T(2,128)}), f32[64,9,2,128]{3,2,1,0:T(2,128)S(1)}, u32[]{:S(2)}, u32[]{:S(2)}) async-start(f32[64,9,2,128]{3,2,1,0:T(2,128)} %bitcast.14), calls=%async_computation.1 | async-start | bytes 1179648 | tf_op jit(solution)/shard_map/all_to_all | solution.py:42
  53.9 0.0 copy-done.2
  53.9 2.5 %shard_map.70 = bf16[16,192,128]{2,1,0:T(8,128)(2,1)} custom-call(bf16[2304,128]{1,0:T(8,128)(2,1)S(1)} %bitcast.25, bf16[9,208,256]{2,1,0:T(8,128)(2,1)S(1)} %get-tuple-element.20.back_ref, bf16[16,192,128]{2,1,0:T(8,128)(2,1)S(1)} %copy-done.2), custom_call_target="tpu_custom_call" | custom-call | flops 4294967296 | bytes 8388608 | tf_op jit(solution)/shard_map/pallas_call | solution.py:342
  56.4 10.3 %all-to-all-done.1 = f32[64,9,2,128]{3,2,1,0:T(2,128)S(1)} async-done(((f32[64,9,2,128]{3,2,1,0:T(2,128)}), f32[64,9,2,128]{3,2,1,0:T(2,128)S(1)}, u32[]{:S(2)}, u32[]{:S(2)}) %all-to-all-start.1) | async-done | bytes 589856 | tf_op jit(solution)/shard_map/all_to_all | solution.py:42
  66.7 0.6 shard_map.72
  (7 shorter events, 0.1 us)
Async XLA Ops:
  1.5 16.2 %collective-permute-start.1 = (bf16[2,16,2,128]{3,2,1,0:T(2,128)(2,1)S(1)}, bf16[2,16,2,128]{3,2,1,0:T(2,128)(2,1)S(1)}, u32[]{:S(2)}, u32[]{:S(2)}) collective-permute-start(bf16[2,16,2,128]{3,2,1,0:T(2,128)(2,1)S(1)} %pad_maximum_fusion.4), channel_id=1, source_target_pairs={{0,1},{1,2},{2,3},{3,4},{4,5},{5,6},{6,7},{7,8},{8,9},{9,10},{10,1... | collective-permute-start | bytes 49160 | tf_op jit(solution)/shard_map/ppermute | solution.py:363
  1.6 16.1 %collective-permute-start = (bf16[2,16,2,128]{3,2,1,0:T(2,128)(2,1)S(1)}, bf16[2,16,2,128]{3,2,1,0:T(2,128)(2,1)S(1)}, u32[]{:S(2)}, u32[]{:S(2)}) collective-permute-start(bf16[2,16,2,128]{3,2,1,0:T(2,128)(2,1)S(1)} %pad_maximum_fusion.3), channel_id=1, source_target_pairs={{0,15},{1,0},{2,1},{3,2},{4,3},{5,4},{6,5},{7,6},{8,7},{9,8},{10,9... | collective-permute-start | bytes 49160 | tf_op jit(solution)/shard_map/ppermute | solution.py:364
  7.4 21.7 %all-to-all-start = ((bf16[128,9,2,128]{3,2,1,0:T(2,128)(2,1)}), bf16[128,9,2,128]{3,2,1,0:T(2,128)(2,1)S(1)}, u32[]{:S(2)}, u32[]{:S(2)}) async-start(bf16[128,9,2,128]{3,2,1,0:T(2,128)(2,1)} %broadcast_in_dim.4), calls=%async_computation | async-start | bytes 1179648 | tf_op jit(solution)/shard_map/all_to_all | solution.py:32
  17.9 15.5 %collective-permute-start.2 = (bf16[2,2,208,128]{3,2,1,0:T(8,128)(2,1)S(1)}, bf16[2,2,208,128]{3,2,1,0:T(8,128)(2,1)S(1)}, u32[]{:S(2)}, u32[]{:S(2)}) collective-permute-start(bf16[2,2,208,128]{3,2,1,0:T(8,128)(2,1)S(1)} %pad_maximum_fusion), channel_id=1, source_target_pairs={{0,16},{16,32},{32,48},{48,64},{64,80},{80,96},{96,112},{1,17},{17... | collective-permute-start | bytes 638984 | tf_op jit(solution)/shard_map/ppermute | solution.py:370
  23.2 12.5 %collective-permute-start.3 = (bf16[2,2,208,128]{3,2,1,0:T(8,128)(2,1)S(1)}, bf16[2,2,208,128]{3,2,1,0:T(8,128)(2,1)S(1)}, u32[]{:S(2)}, u32[]{:S(2)}) collective-permute-start(bf16[2,2,208,128]{3,2,1,0:T(8,128)(2,1)S(1)} %pad_maximum_fusion.1), channel_id=1, source_target_pairs={{16,0},{32,16},{48,32},{64,48},{80,64},{96,80},{112,96},{17,1},{33... | collective-permute-start | bytes 638984 | tf_op jit(solution)/shard_map/ppermute | solution.py:371
  29.1 1.1 %copy-start = (bf16[16,192,128]{2,1,0:T(8,128)(2,1)S(1)}, bf16[16,192,128]{2,1,0:T(8,128)(2,1)}, u32[]{:S(2)}) copy-start(bf16[16,192,128]{2,1,0:T(8,128)(2,1)} %feat_ref.1) | copy-start | bytes 2359300
  30.2 1.1 %copy-start.1 = (bf16[16,192,128]{2,1,0:T(8,128)(2,1)S(1)}, bf16[16,192,128]{2,1,0:T(8,128)(2,1)}, u32[]{:S(2)}) copy-start(bf16[16,192,128]{2,1,0:T(8,128)(2,1)} %cot_ref.3) | copy-start | bytes 2359300
  36.4 17.5 %copy-start.2 = (bf16[16,192,128]{2,1,0:T(8,128)(2,1)S(1)}, bf16[16,192,128]{2,1,0:T(8,128)(2,1)}, u32[]{:S(2)}) copy-start(bf16[16,192,128]{2,1,0:T(8,128)(2,1)} %cot_ref.3) | copy-start | bytes 2359300
  43.0 2.1 %collective-permute-start.4 = (f32[1152,128]{1,0:T(8,128)S(1)}, f32[1152,128]{1,0:T(8,128)S(1)}, u32[]{:S(2)}, u32[]{:S(2)}) collective-permute-start(f32[1152,128]{1,0:T(8,128)S(1)} %get-tuple-element.22), channel_id=1, source_target_pairs={{0,1},{1,0},{2,3},{3,2},{4,5},{5,4},{6,7},{7,6},{8,9},{9,8},{10,11... | collective-permute-start | bytes 1769480 | tf_op jit(solution)/shard_map/ppermute | solution.py:39
  46.0 20.7 %all-to-all-start.1 = ((f32[64,9,2,128]{3,2,1,0:T(2,128)}), f32[64,9,2,128]{3,2,1,0:T(2,128)S(1)}, u32[]{:S(2)}, u32[]{:S(2)}) async-start(f32[64,9,2,128]{3,2,1,0:T(2,128)} %bitcast.14), calls=%async_computation.1 | async-start | bytes 1179648 | tf_op jit(solution)/shard_map/all_to_all | solution.py:42

commit v5 on v4

--- a/solution.py
+++ b/solution.py
@@ -16,20 +16,48 @@
 FINAL_LIMIT = 12 << 20
 
 
-def ring(axis, step, periodic):
+def swap(sent, axis, odd_first, periodic):
     count = lax.axis_size(axis)
-    pairs = [(i, (i + step) % count) for i in range(count)]
+    pairs = [(i, (i + 1) % count) for i in range(odd_first, count, 2)]
     if not periodic:
-        pairs = [(i, j) for i, j in pairs if j == i + step]
-    return pairs
+        pairs = [(i, j) for i, j in pairs if j == i + 1]
+    return lax.ppermute(sent, axis, pairs + [(j, i) for i, j in pairs])
+
+
+def spread_kernel(first_ref, second_ref, out_ref, mixed_ref):
+    rows, _ = first_ref.shape
+    first, second = first_ref[...].astype(F32), second_ref[...].astype(F32)
+    blocks = mixed_ref.shape[0] // (2 * rows)
+    for block in range(blocks):
+        at = 2 * rows * block
+        mixed_ref[pl.ds(at, rows, stride=2)] = first
+        mixed_ref[pl.ds(at + 1, rows, stride=2)] = second
+    mixed = mixed_ref[...].astype(BF16)
+    for at in range(0, out_ref.shape[0], mixed.shape[0]):
+        out_ref[at : at + mixed.shape[0]] = mixed
+
+
+def spread(w_first, w_second, count):
+    rows, chans = w_first.shape
+    whole = pl.BlockSpec(memory_space=pltpu.VMEM)
+    return pl.pallas_call(
+        spread_kernel,
+        out_shape=jax.ShapeDtypeStruct((2 * rows * count, chans), BF16),
+        in_specs=[whole] * 2,
+        out_specs=whole,
+        scratch_shapes=[pltpu.VMEM((2 * rows * min(8, count), chans), F32)],
+        compiler_params=pltpu.CompilerParams(vmem_limit_bytes=4 << 20),
+    )(w_first, w_second)
 
 
 def gather_kernels(w_first, w_second):
     count = lax.axis_size(AXES)
     rows, chans = w_first.shape
-    mine = jnp.stack([w_first, w_second], 1)[None]
-    sent = jnp.broadcast_to(mine, (count, rows, 2, chans))
-    return lax.all_to_all(sent, AXES, 0, 0, tiled=True).reshape(-1, chans)
+    sent = spread(w_first, w_second, count // 2).reshape(count // 2, rows, 2, chans)
+    groups = [list(range(parity, count, 2)) for parity in range(2)]
+    mine = lax.all_to_all(sent, AXES, 0, 0, tiled=True, axis_index_groups=groups)
+    mine = mine.reshape(-1, chans)
+    return mine, lax.ppermute(mine, AXES, [(i, i ^ 1) for i in range(count)])
 
 
 def scatter_sums(keep, send):
@@ -119,10 +147,17 @@
     )(features, cotangent, tail)
 
 
-def outer_kernel(above_ref, below_ref, near_ref, taps_ref, cells_ref):
+def outer_kernel(
+    place_ref, even_ref, odd_ref, near_ref, taps_ref, cells_ref
+):
     pairs = near_ref.shape[1]
-    chans = above_ref.shape[3]
+    chans = even_ref.shape[3]
     cols = cells_ref.shape[3] // 2
+    odd = place_ref[3] == 1
+
+    def whole(first_ref, second_ref, at):
+        return jnp.where(odd, first_ref[at].astype(F32), second_ref[at].astype(F32)).astype(BF16)
+
     for field in range(2):
 
         def near(r):
@@ -130,8 +165,8 @@
             at = [(2 * b + r) * chans for b in range(3)]
             return [near_ref[field, p, :, i : i + chans] for i in at]
 
-        above = [shifted(above_ref[field, r]) for r in range(2)]
-        below = [shifted(below_ref[field, r]) for r in range(2)]
+        above = [shifted(whole(even_ref, odd_ref, (field, r))) for r in range(2)]
+        below = [shifted(whole(odd_ref, even_ref, (field, r))) for r in range(2)]
         taps_ref[field, 0] = paired(*above)
         taps_ref[field, 1] = paired(*below)
         cells = [paired(above[1], near(0)), paired(near(1), near(2))]
@@ -140,8 +175,8 @@
         cells_ref[field, 1] = jnp.concatenate([cell[:cols] for cell in cells], 0).T
 
 
-def outer(above, below, near, cols):
-    _, _, width, chans = above.shape
+def outer(place, rims, near, cols):
+    _, _, width, chans = rims[0].shape
     whole = pl.BlockSpec(memory_space=pltpu.VMEM)
     return pl.pallas_call(
         outer_kernel,
@@ -149,11 +184,11 @@
             jax.ShapeDtypeStruct((2, 2, width, 6 * chans), BF16),
             jax.ShapeDtypeStruct((2, 2, 6 * chans, 2 * cols), BF16),
         ),
-        in_specs=[whole] * 3,
+        in_specs=[pl.BlockSpec(memory_space=pltpu.SMEM)] + [whole] * 3,
         out_specs=(whole, whole),
         compiler_params=pltpu.CompilerParams(vmem_limit_bytes=PREP_LIMIT),
         cost_estimate=pl.CostEstimate(flops=1 << 30, bytes_accessed=4 << 20, transcendentals=0),
-    )(above, below, near)
+    )(place, *rims, near)
 
 
 def tap_rows(a, b, chans):
@@ -200,15 +235,22 @@
 
 
 def middle_kernel(
-    own_rows, place_ref, both_ref, inner_taps_ref, inner_cells_ref, outer_taps_ref, outer_cells_ref,
-    keep_ref, send_ref, back_ref,
-    wide_ref, sums_ref, one_ref, two_ref, plain_ref, turned_ref, slope_ref, act_ref, own_ref,
+    own_rows, place_ref, mine_ref, other_ref, inner_taps_ref, inner_cells_ref, outer_taps_ref, outer_cells_ref,
+    keep_ref, send_ref, back_ref, one_ref,
+    mixed_ref, wide_ref, sums_ref, two_ref, plain_ref, turned_ref, slope_ref, act_ref, own_ref,
 ):
     pairs, width, lanes = back_ref.shape
     chans = lanes // 2
     cols = width - 16
     taps = one_ref.shape[0]
-    wide_ref[...] = both_ref[...].astype(F32)
+    core = place_ref[0]
+    mixed_ref[0] = mine_ref[...].astype(F32)
+    mixed_ref[1] = other_ref[...].astype(F32)
+    for g in range(mine_ref.shape[0] // own_rows):
+        at = own_rows * g
+        mine, other = (mixed_ref[i, at : at + own_rows] for i in range(2))
+        wide_ref[2 * at : 2 * at + own_rows] = jnp.where(core == 0, mine, other)
+        wide_ref[2 * at + own_rows : 2 * at + 2 * own_rows] = jnp.where(core == 0, other, mine)
     one_ref[...] = wide_ref[pl.ds(0, taps, stride=2)].astype(BF16)
     two_ref[...] = wide_ref[pl.ds(1, taps, stride=2)].astype(BF16)
     fill_plain(one_ref, plain_ref)
@@ -273,7 +315,6 @@
             sums_ref[pl.ds(2 * at, chans, stride=2)] = summed(firsts)
             at = tap_rows(-a, 1 - b, chans).start
             sums_ref[pl.ds(2 * at + 1, chans, stride=2)] = summed(seconds).T
-    core = place_ref[0]
     groups = keep_ref.shape[0] // own_rows
     for g in range(groups):
         out = pl.ds(own_rows * g, own_rows)
@@ -286,7 +327,8 @@
     outer_taps, outer_cells = outer_parts
     pairs = inner_taps.shape[1] + 1
     width = inner_taps.shape[2]
-    rows, chans = both.shape
+    rows, chans = both[0].shape
+    rows *= 2
     lanes = 2 * chans
     cells = (pairs - 1) * (width - 16)
     whole = pl.BlockSpec(memory_space=pltpu.VMEM)
@@ -296,13 +338,14 @@
             jax.ShapeDtypeStruct((rows // 2, chans), F32),
             jax.ShapeDtypeStruct((rows // 2, chans), F32),
             jax.ShapeDtypeStruct((pairs, width, lanes), BF16),
+            jax.ShapeDtypeStruct((rows // 2, chans), BF16),
         ),
-        in_specs=[pl.BlockSpec(memory_space=pltpu.SMEM)] + [whole] * 5,
-        out_specs=(whole,) * 3,
+        in_specs=[pl.BlockSpec(memory_space=pltpu.SMEM)] + [whole] * 6,
+        out_specs=(whole,) * 4,
         scratch_shapes=[
+            pltpu.VMEM((2, rows // 2, chans), F32),
             pltpu.VMEM((rows, chans), F32),
             pltpu.VMEM((rows, chans), F32),
-            pltpu.VMEM((rows // 2, chans), BF16),
             pltpu.VMEM((rows // 2, chans), BF16),
             pltpu.VMEM((2, 3 * lanes, lanes), BF16),
             pltpu.VMEM((2, lanes, 3 * lanes), BF16),
@@ -311,14 +354,12 @@
             pltpu.VMEM((cells, lanes), BF16),
         ],
         compiler_params=pltpu.CompilerParams(vmem_limit_bytes=MIDDLE_LIMIT),
-    )(place, both, inner_taps, inner_cells, outer_taps, outer_cells)
-
-
-def final_kernel(both_ref, back_ref, cot_ref, out_ref, wide_ref, one_ref, turned_ref, taps_ref):
+    )(place, *both, inner_taps, inner_cells, outer_taps, outer_cells)
+
+
+def final_kernel(one_ref, back_ref, cot_ref, out_ref, turned_ref, taps_ref):
     pairs, _, _ = back_ref.shape
     _, cols, chans = cot_ref.shape
-    wide_ref[...] = both_ref[...].astype(F32)
-    one_ref[...] = wide_ref[pl.ds(0, one_ref.shape[0], stride=2)].astype(BF16)
     fill_turned(one_ref, turned_ref)
     for p in range(pairs):
         taps = jnp.concatenate(shifted(back_ref[p]), 1)
@@ -335,9 +376,9 @@
                 out_ref[row] = (part + cot_ref[row].astype(F32)).astype(BF16)
 
 
-def final(both, back, cotangent):
+def final(one, back, cotangent):
     pairs, _, lanes = back.shape
-    _, cols, chans = cotangent.shape
+    _, cols, _ = cotangent.shape
     whole = pl.BlockSpec(memory_space=pltpu.VMEM)
     return pl.pallas_call(
         final_kernel,
@@ -345,44 +386,52 @@
         in_specs=[whole] * 3,
         out_specs=whole,
         scratch_shapes=[
-            pltpu.VMEM(both.shape, F32),
-            pltpu.VMEM((both.shape[0] // 2, chans), BF16),
             pltpu.VMEM((2, lanes, 3 * lanes), BF16),
             pltpu.VMEM((pairs * cols, 3 * lanes), BF16),
         ],
         compiler_params=pltpu.CompilerParams(vmem_limit_bytes=FINAL_LIMIT),
         cost_estimate=pl.CostEstimate(flops=1 << 32, bytes_accessed=8 << 20, transcendentals=0),
-    )(both, back, cotangent)
+    )(one, back, cotangent)
 
 
 def layer(features, cotangent, w_first, w_second):
     both = gather_kernels(w_first, w_second)
     rows, cols, chans = features.shape
-    left = jnp.stack([features[:, -2:], cotangent[:, -2:]])
-    right = jnp.stack([features[:, :2], cotangent[:, :2]])
-    left = lax.ppermute(left, "lon", ring("lon", 1, True))
-    right = lax.ppermute(right, "lon", ring("lon", -1, True))
+    lon, lat = lax.axis_index("lon"), lax.axis_index("lat")
+
+    def edge(field, axis, first):
+        size = field.shape[axis]
+        start = jnp.where(first, 0, size - 2)
+        return lax.dynamic_slice_in_dim(field, start, 2, axis)
+
+    def edges(axis, first):
+        return jnp.stack([edge(features, axis, first), edge(cotangent, axis, first)])
+
+    lat_odd, lon_odd = lat % 2 == 1, lon % 2 == 1
+    rims, sides = [None, None], [None, None]
+    for turn in (1, 0):
+        sides[turn] = swap(edges(1, lon_odd ^ (turn == 1)), "lon", turn, True)
+    right = jnp.where(lon_odd, sides[1], sides[0])
+    left = jnp.where(lon_odd, sides[0], sides[1])
     tail = jnp.concatenate([right, jnp.zeros((2, rows, 12, chans), BF16), left], 2)
-
-    def whole_rows(at):
-        return jnp.concatenate([jnp.stack([features[at], cotangent[at]]), tail[:, at]], 2)
-
-    above = lax.ppermute(whole_rows(slice(rows - 2, rows)), "lat", ring("lat", 1, False))
-    below = lax.ppermute(whole_rows(slice(0, 2)), "lat", ring("lat", -1, False))
-    at = lax.axis_index("lat")
+    for turn in (1, 0):
+        first = lat_odd ^ (turn == 1)
+        sent = jnp.concatenate([edges(0, first), edge(tail, 1, first)], 2)
+        rims[turn] = swap(sent, "lat", turn, False)
     place = jnp.stack(
         [
-            lax.axis_index(AXES) % 2,
-            (at == 0).astype(jnp.int32),
-            (at == lax.axis_size("lat") - 1).astype(jnp.int32),
+            (lax.axis_index(AXES) % 2).astype(jnp.int32),
+            (lat == 0).astype(jnp.int32),
+            (lat == lax.axis_size("lat") - 1).astype(jnp.int32),
+            lat_odd.astype(jnp.int32),
         ]
     )
-    both, own_tail = lax.optimization_barrier((both, tail))
+    _, own_tail = lax.optimization_barrier((both[0], tail))
     inner_parts = inner(features, cotangent, own_tail)
-    outer_parts = outer(above, below, inner_parts[0], cols)
-    keep, send, back = middle(place, both, inner_parts, outer_parts, 2 * w_first.shape[0])
+    outer_parts = outer(place, rims, inner_parts[0], cols)
+    keep, send, back, one = middle(place, both, inner_parts, outer_parts, 2 * w_first.shape[0])
     grads = scatter_sums(keep, send)
-    return final(both, back, cotangent), *grads
+    return final(one, back, cotangent), *grads
 
 
 def solution(mesh):

time: 68.4 us -> 65.2 us (0.953)
  waiting for transfers between devices: 18.5 us -> 15 us
  Pallas kernels: 13.3 us -> 14.6 us
  other arithmetic: 0.97 us -> 0.27 us
    ppermute x4 -> x5, waiting for transfers between devices: 2.33 us -> 0.01 us  [the longest x4 0.01 us: swap(): return lax.ppermute(sent, axis, pairs + [(j, i) for i, j in pairs])]
    unnamed x6 -> x10, local copies, waits for them, and re-layouts: 2.27 us -> 3.65 us
    broadcast_in_dim x1 -> x0, local copies, waits for them, and re-layouts: 1.12 us -> none  [gather_kernels(): sent = jnp.broadcast_to(mine, (count, rows, 2, chans))]
    all_to_all x1, waiting for transfers between devices: 3.97 us -> 2.91 us  [gather_kernels(): lax.all_to_all(sent, AXES, 0, 0, tiled=True, axis_index_groups=groups)]
    pallas_call x0 -> x1, Pallas kernels: none -> 0.75 us  [spread(): pl.pallas_call(spread_kernel, out_shape=jax.ShapeDtypeStruct((2 * rows *...]
    another operation x4 -> x3, other arithmetic: 0.84 us -> 0.14 us  [the longest x1 0.08 us: layer(): jnp.stack([(lax.axis_index(AXES) % 2).astype(jnp.int32), (lat == 0).astyp...]
    another operation x3 -> x2, local copies, waits for them, and re-layouts: 1.92 us -> 1.93 us  [edges(): jnp.stack([edge(features, axis, first), edge(cotangent, axis, first)])]
    ppermute x4 -> x5, starting transfers between devices: 11.2 us -> 11.2 us  [the longest x4 11.2 us: swap(): return lax.ppermute(sent, axis, pairs + [(j, i) for i, j in pairs])]
  transfers between devices with their start and end apart: 7 -> 8, of which waited for: 4 -> 3; matrix products, arithmetic and copies ran while one was open for 5% -> 2% of each run, Pallas kernels for 7% -> 10%
where the time goes in v5:
time: 65.2 us; the launch traced here: 64.1 us
  starting transfers between devices  27.8 us (43%)
  waiting for transfers between devices  15 us (23%)
  Pallas kernels  14.6 us (22%)
  local copies, waits for them, and re-layouts  5.67 us (9%)
  between operations  0.84 us (1%)
    ppermute x4, starting transfers between devices, swap(): return lax.ppermute(sent, axis, pairs + [(j, i) for i, j in pairs])  11.2 us
    all_to_all x1, waiting for transfers between devices, scatter_sums(): lax.all_to_all(parts, AXES, 0, 0, tiled=True, axis_index_groups=groups)  10.4 us
    all_to_all x1, starting transfers between devices, gather_kernels(): lax.all_to_all(sent, AXES, 0, 0, tiled=True, axis_index_groups=groups)  8.58 us
    all_to_all x1, starting transfers between devices, scatter_sums(): lax.all_to_all(parts, AXES, 0, 0, tiled=True, axis_index_groups=groups)  7.44 us
    pallas_call x1, Pallas kernels, middle(): pl.pallas_call(functools.partial(middle_kernel, own_rows), out_shape=(jax...  6.68 us
    unnamed x10, local copies, waits for them, and re-layouts  3.65 us
    all_to_all x1, waiting for transfers between devices, gather_kernels(): lax.all_to_all(sent, AXES, 0, 0, tiled=True, axis_index_groups=groups)  2.91 us
    pallas_call x1, Pallas kernels, final(): pl.pallas_call(final_kernel, out_shape=jax.ShapeDtypeStruct(cotangent.sha...  2.37 us
  transfers between devices with their start and end apart: 8, of which 3 were waited for; matrix products, arithmetic and copies ran while one was open for 2% of the time, Pallas kernels for 10%

profile of v5, /device:TPU:6, one launch (start us, length us, event | category | flops | bytes accessed | tf_op | source)
XLA Modules:
  0.0 64.1 jit_solution(1279923262597068545)
XLA Ops:
  0.6 0.9 %dynamic-slice_bitcast_fusion.6 = (bf16[1,16,2,128]{3,2,1,0:T(2,128)(2,1)S(1)}, bf16[1,16,2,128]{3,2,1,0:T(2,128)(2,1)S(1)}, bf16[1,16,2,128]{3,2,1,0:T(2,128)(2,1)S(1)}, bf16[1,16,2,128]{3,2,1,0:T(2,128)(2,1)S(1)}) fusion(bf16[16,192,128]{2,1,0:T(8,128)(2,1)} %cot_ref.3, s32[]{:T(128)S(6)} %select_n.60, s32[]{:T(128)S(6)} %select_n.61, ...), kind=kLoop, calls=%fused_computation.13 | loop fusion | bytes 65544 | tf_op jit(solution)/shard_map/stack | solution.py:408
  1.5 0.1 collective-permute-start.2
  1.7 4.5 %collective-permute-start.1 = (bf16[2,16,2,128]{3,2,1,0:T(2,128)(2,1)S(1)}, bf16[2,16,2,128]{3,2,1,0:T(2,128)(2,1)S(1)}, u32[]{:S(2)}, u32[]{:S(2)}) collective-permute-start(bf16[2,16,2,128]{3,2,1,0:T(2,128)(2,1)S(1)} %pad_maximum_fusion.3), channel_id=1, source_target_pairs={{1,2},{3,4},{5,6},{7,8},{9,10},{11,12},{13,14},{15,0},{2,1},{4,3},... | collective-permute-start | bytes 49160 | tf_op jit(solution)/shard_map/ppermute | solution.py:24
  6.2 0.0 copy-start.3
  6.2 0.7 %copy-done.3 = bf16[9,128]{1,0:T(8,128)(2,1)S(1)} copy-done((bf16[9,128]{1,0:T(8,128)(2,1)S(1)}, bf16[9,128]{1,0:T(8,128)(2,1)}, u32[]{:S(2)}) %copy-start.3) | copy-done | bytes 2328
  6.9 0.0 copy-start.4
  6.9 0.7 %copy-done.4 = bf16[9,128]{1,0:T(8,128)(2,1)S(1)} copy-done((bf16[9,128]{1,0:T(8,128)(2,1)S(1)}, bf16[9,128]{1,0:T(8,128)(2,1)}, u32[]{:S(2)}) %copy-start.4) | copy-done | bytes 2328
  7.6 0.7 %shard_map.67 = bf16[1152,128]{1,0:T(8,128)(2,1)} custom-call(bf16[9,128]{1,0:T(8,128)(2,1)S(1)} %copy-done.3, bf16[9,128]{1,0:T(8,128)(2,1)S(1)} %copy-done.4), custom_call_target="tpu_custom_call" | custom-call | tf_op jit(solution)/shard_map/pallas_call | solution.py:43
  8.3 8.6 %all-to-all-start = ((bf16[64,9,2,128]{3,2,1,0:T(2,128)(2,1)}), bf16[64,9,2,128]{3,2,1,0:T(2,128)(2,1)S(1)}, u32[]{:S(2)}, u32[]{:S(2)}) async-start(bf16[64,9,2,128]{3,2,1,0:T(2,128)(2,1)} %bitcast.4), calls=%async_computation | async-start | bytes 589824 | tf_op jit(solution)/shard_map/all_to_all | solution.py:58
  17.0 1.1 %dynamic-slice_bitcast_fusion = (bf16[1,2,192,128]{3,2,1,0:T(8,128)(2,1)S(1)}, bf16[1,2,192,128]{3,2,1,0:T(8,128)(2,1)S(1)}, bf16[1,2,192,128]{3,2,1,0:T(8,128)(2,1)S(1)}, bf16[1,2,192,128]{3,2,1,0:T(8,128)(2,1)S(1)}) fusion(bf16[16,192,128]{2,1,0:T(8,128)(2,1)} %cot_ref.3, s32[]{:T(128)S(6)} %select_n.65, s32[]{:T(128)S(6)} %select_n.64, ...), kind=kLoop, calls=%fused_computation.3 | loop fusion | bytes 786440 | tf_op jit(solution)/shard_map/stack | solution.py:408
  18.0 0.1 pad_add_fusion.place_ref
  18.1 0.1 pad.7.clone
  18.2 0.0 collective-permute-done.2
  18.2 0.0 collective-permute-done.1
  18.2 0.1 pad_maximum_fusion.2.tail_ref
  18.4 0.9 %collective-permute-start.3 = (bf16[2,2,208,128]{3,2,1,0:T(8,128)(2,1)S(1)}, bf16[2,2,208,128]{3,2,1,0:T(8,128)(2,1)S(1)}, u32[]{:S(2)}, u32[]{:S(2)}) collective-permute-start(bf16[2,2,208,128]{3,2,1,0:T(8,128)(2,1)S(1)} %pad_maximum_fusion), channel_id=1, source_target_pairs={{0,16},{32,48},{64,80},{96,112},{16,0},{48,32},{80,64},{112,96},{1... | collective-permute-start | bytes 638984 | tf_op jit(solution)/shard_map/ppermute | solution.py:24
  19.3 5.6 %collective-permute-start.4 = (bf16[2,2,208,128]{3,2,1,0:T(8,128)(2,1)S(1)}, bf16[2,2,208,128]{3,2,1,0:T(8,128)(2,1)S(1)}, u32[]{:S(2)}, u32[]{:S(2)}) collective-permute-start(bf16[2,2,208,128]{3,2,1,0:T(8,128)(2,1)S(1)} %pad_maximum_fusion.1), channel_id=1, source_target_pairs={{16,32},{48,64},{80,96},{32,16},{64,48},{96,80},{17,33},{49,65},{8... | collective-permute-start | bytes 638984 | tf_op jit(solution)/shard_map/ppermute | solution.py:24
  24.9 2.9 %all-to-all-done = bf16[64,9,2,128]{3,2,1,0:T(2,128)(2,1)S(1)} async-done(((bf16[64,9,2,128]{3,2,1,0:T(2,128)(2,1)}), bf16[64,9,2,128]{3,2,1,0:T(2,128)(2,1)S(1)}, u32[]{:S(2)}, u32[]{:S(2)}) %all-to-all-start) | async-done | bytes 294944 | tf_op jit(solution)/shard_map/all_to_all | solution.py:58
  27.8 0.0 collective-permute-start
  27.8 0.0 copy-start
  27.8 1.1 %copy-done = bf16[16,192,128]{2,1,0:T(8,128)(2,1)S(1)} copy-done((bf16[16,192,128]{2,1,0:T(8,128)(2,1)S(1)}, bf16[16,192,128]{2,1,0:T(8,128)(2,1)}, u32[]{:S(2)}) %copy-start) | copy-done | bytes 786456
  29.0 0.0 copy-start.1
  29.0 1.1 %copy-done.1 = bf16[16,192,128]{2,1,0:T(8,128)(2,1)S(1)} copy-done((bf16[16,192,128]{2,1,0:T(8,128)(2,1)S(1)}, bf16[16,192,128]{2,1,0:T(8,128)(2,1)}, u32[]{:S(2)}) %copy-start.1) | copy-done | bytes 786456
  30.1 2.0 %shard_map.68 = (bf16[2,8,208,768]{3,2,1,0:T(8,128)(2,1)S(1)}, bf16[2,2,768,1152]{3,2,1,0:T(8,128)(2,1)S(1)}) custom-call(bf16[16,192,128]{2,1,0:T(8,128)(2,1)S(1)} %copy-done, bf16[16,192,128]{2,1,0:T(8,128)(2,1)S(1)} %copy-done.1, bf16[2,16,16,128]{3,2,1,0:T(8,128)(2,1)S(1)} %pad_maximum_fusion.2.tail_ref), custom_call_target="tpu_custom_call" | custom-call | flops 4294967296 | bytes 16777216 | tf_op jit(solution)/shard_map/pallas_call | solution.py:137
  32.1 0.0 collective-permute-done.3.even_ref
  32.1 0.0 collective-permute-done.4.odd_ref
  32.1 1.3 %shard_map.69 = (bf16[2,2,208,768]{3,2,1,0:T(8,128)(2,1)S(1)}, bf16[2,2,768,384]{3,2,1,0:T(8,128)(2,1)S(1)}) custom-call(s32[4]{0:T(128)S(1)} %pad_add_fusion.place_ref, bf16[2,2,208,128]{3,2,1,0:T(8,128)(2,1)S(1)} %collective-permute-done.3.even_ref, bf16[2,2,208,128]{3,2,1,0:T(8,128)(2,1)S(1)} %collective-permute-done.4.odd_ref, ...), custom_call_target="tpu_custom_call" | custom-call | flops 1073741824 | bytes 4194304 | tf_op jit(solution)/shard_map/pallas_call | solution.py:181
  33.4 0.0 collective-permute-done.other_ref
  33.4 0.0 copy-start.2
  33.4 6.7 %shard_map.70 = (f32[1152,128]{1,0:T(8,128)S(1)}, f32[1152,128]{1,0:T(8,128)S(1)}, bf16[9,208,256]{2,1,0:T(8,128)(2,1)S(1)}, bf16[1152,128]{1,0:T(8,128)(2,1)S(1)}) custom-call(s32[4]{0:T(128)S(1)} %pad_add_fusion.place_ref, bf16[1152,128]{1,0:T(8,128)(2,1)S(1)} %bitcast.30, bf16[1152,128]{1,0:T(8,128)(2,1)S(1)} %collective-permute-done.other_ref, ...), custom_call_target="tpu_custom_call" | custom-call | tf_op jit(solution)/shard_map/pallas_call | solution.py:335
  40.1 0.6 collective-permute-start.5
  40.7 1.6 %collective-permute-done.5.got_ref = f32[1152,128]{1,0:T(8,128)S(1)} collective-permute-done((f32[1152,128]{1,0:T(8,128)S(1)}, f32[1152,128]{1,0:T(8,128)S(1)}, u32[]{:S(2)}, u32[]{:S(2)}) %collective-permute-start.5) | collective-permute-done | bytes 589856 | tf_op jit(solution)/shard_map/ppermute | solution.py:67
  42.3 0.9 %shard_map.72 = f32[1152,128]{1,0:T(8,128)} custom-call(f32[1152,128]{1,0:T(8,128)S(1)} %get-tuple-element.21.keep_ref, f32[1152,128]{1,0:T(8,128)S(1)} %collective-permute-done.5.got_ref), custom_call_target="tpu_custom_call" | custom-call | tf_op jit(solution)/shard_map/pallas_call | solution.py:80
  43.2 7.4 %all-to-all-start.1 = ((f32[64,9,2,128]{3,2,1,0:T(2,128)}), f32[64,9,2,128]{3,2,1,0:T(2,128)S(1)}, u32[]{:S(2)}, u32[]{:S(2)}) async-start(f32[64,9,2,128]{3,2,1,0:T(2,128)} %bitcast.14), calls=%async_computation.1 | async-start | bytes 1179648 | tf_op jit(solution)/shard_map/all_to_all | solution.py:70
  50.7 0.0 copy-done.2
  50.7 2.4 %shard_map.71 = bf16[16,192,128]{2,1,0:T(8,128)(2,1)} custom-call(bf16[1152,128]{1,0:T(8,128)(2,1)S(1)} %get-tuple-element.19.one_ref, bf16[9,208,256]{2,1,0:T(8,128)(2,1)S(1)} %get-tuple-element.20.back_ref, bf16[16,192,128]{2,1,0:T(8,128)(2,1)S(1)} %copy-done.2), custom_call_target="tpu_custom_call" | custom-call | flops 4294967296 | bytes 8388608 | tf_op jit(solution)/shard_map/pallas_call | solution.py:383
  53.0 10.4 %all-to-all-done.1 = f32[64,9,2,128]{3,2,1,0:T(2,128)S(1)} async-done(((f32[64,9,2,128]{3,2,1,0:T(2,128)}), f32[64,9,2,128]{3,2,1,0:T(2,128)S(1)}, u32[]{:S(2)}, u32[]{:S(2)}) %all-to-all-start.1) | async-done | bytes 589856 | tf_op jit(solution)/shard_map/all_to_all | solution.py:70
  63.5 0.6 %shard_map.73 = (f32[9,128]{1,0:T(8,128)}, f32[9,128]{1,0:T(8,128)}) custom-call(f32[1152,128]{1,0:T(8,128)S(1)} %bitcast.28), custom_call_target="tpu_custom_call" | custom-call | tf_op jit(solution)/shard_map/pallas_call | solution.py:100
  (7 shorter events, 0.1 us)
Async XLA Ops:
  1.5 16.7 %collective-permute-start.2 = (bf16[2,16,2,128]{3,2,1,0:T(2,128)(2,1)S(1)}, bf16[2,16,2,128]{3,2,1,0:T(2,128)(2,1)S(1)}, u32[]{:S(2)}, u32[]{:S(2)}) collective-permute-start(bf16[2,16,2,128]{3,2,1,0:T(2,128)(2,1)S(1)} %pad_maximum_fusion.4), channel_id=1, source_target_pairs={{0,1},{2,3},{4,5},{6,7},{8,9},{10,11},{12,13},{14,15},{1,0},{3,2},... | collective-permute-start | bytes 49160 | tf_op jit(solution)/shard_map/ppermute | solution.py:24
  1.7 16.5 %collective-permute-start.1 = (bf16[2,16,2,128]{3,2,1,0:T(2,128)(2,1)S(1)}, bf16[2,16,2,128]{3,2,1,0:T(2,128)(2,1)S(1)}, u32[]{:S(2)}, u32[]{:S(2)}) collective-permute-start(bf16[2,16,2,128]{3,2,1,0:T(2,128)(2,1)S(1)} %pad_maximum_fusion.3), channel_id=1, source_target_pairs={{1,2},{3,4},{5,6},{7,8},{9,10},{11,12},{13,14},{15,0},{2,1},{4,3},... | collective-permute-start | bytes 49160 | tf_op jit(solution)/shard_map/ppermute | solution.py:24
  6.2 0.7 %copy-start.3 = (bf16[9,128]{1,0:T(8,128)(2,1)S(1)}, bf16[9,128]{1,0:T(8,128)(2,1)}, u32[]{:S(2)}) copy-start(bf16[9,128]{1,0:T(8,128)(2,1)} %first_ref.1) | copy-start | bytes 6916
  6.9 0.7 %copy-start.4 = (bf16[9,128]{1,0:T(8,128)(2,1)S(1)}, bf16[9,128]{1,0:T(8,128)(2,1)}, u32[]{:S(2)}) copy-start(bf16[9,128]{1,0:T(8,128)(2,1)} %second_ref.1) | copy-start | bytes 6916
  8.3 19.5 %all-to-all-start = ((bf16[64,9,2,128]{3,2,1,0:T(2,128)(2,1)}), bf16[64,9,2,128]{3,2,1,0:T(2,128)(2,1)S(1)}, u32[]{:S(2)}, u32[]{:S(2)}) async-start(bf16[64,9,2,128]{3,2,1,0:T(2,128)(2,1)} %bitcast.4), calls=%async_computation | async-start | bytes 589824 | tf_op jit(solution)/shard_map/all_to_all | solution.py:58
  18.4 13.8 %collective-permute-start.3 = (bf16[2,2,208,128]{3,2,1,0:T(8,128)(2,1)S(1)}, bf16[2,2,208,128]{3,2,1,0:T(8,128)(2,1)S(1)}, u32[]{:S(2)}, u32[]{:S(2)}) collective-permute-start(bf16[2,2,208,128]{3,2,1,0:T(8,128)(2,1)S(1)} %pad_maximum_fusion), channel_id=1, source_target_pairs={{0,16},{32,48},{64,80},{96,112},{16,0},{48,32},{80,64},{112,96},{1... | collective-permute-start | bytes 638984 | tf_op jit(solution)/shard_map/ppermute | solution.py:24
  19.3 12.9 %collective-permute-start.4 = (bf16[2,2,208,128]{3,2,1,0:T(8,128)(2,1)S(1)}, bf16[2,2,208,128]{3,2,1,0:T(8,128)(2,1)S(1)}, u32[]{:S(2)}, u32[]{:S(2)}) collective-permute-start(bf16[2,2,208,128]{3,2,1,0:T(8,128)(2,1)S(1)} %pad_maximum_fusion.1), channel_id=1, source_target_pairs={{16,32},{48,64},{80,96},{32,16},{64,48},{96,80},{17,33},{49,65},{8... | collective-permute-start | bytes 638984 | tf_op jit(solution)/shard_map/ppermute | solution.py:24
  27.8 5.6 %collective-permute-start = (bf16[1152,128]{1,0:T(8,128)(2,1)S(1)}, bf16[1152,128]{1,0:T(8,128)(2,1)S(1)}, u32[]{:S(2)}, u32[]{:S(2)}) collective-permute-start(bf16[1152,128]{1,0:T(8,128)(2,1)S(1)} %bitcast.29), channel_id=1, source_target_pairs={{0,1},{1,0},{2,3},{3,2},{4,5},{5,4},{6,7},{7,6},{8,9},{9,8},{10,11... | collective-permute-start | bytes 884744 | tf_op jit(solution)/shard_map/ppermute | solution.py:60
  27.8 1.1 %copy-start = (bf16[16,192,128]{2,1,0:T(8,128)(2,1)S(1)}, bf16[16,192,128]{2,1,0:T(8,128)(2,1)}, u32[]{:S(2)}) copy-start(bf16[16,192,128]{2,1,0:T(8,128)(2,1)} %feat_ref.1) | copy-start | bytes 2359300
  29.0 1.1 %copy-start.1 = (bf16[16,192,128]{2,1,0:T(8,128)(2,1)S(1)}, bf16[16,192,128]{2,1,0:T(8,128)(2,1)}, u32[]{:S(2)}) copy-start(bf16[16,192,128]{2,1,0:T(8,128)(2,1)} %cot_ref.3) | copy-start | bytes 2359300
  33.4 17.2 %copy-start.2 = (bf16[16,192,128]{2,1,0:T(8,128)(2,1)S(1)}, bf16[16,192,128]{2,1,0:T(8,128)(2,1)}, u32[]{:S(2)}) copy-start(bf16[16,192,128]{2,1,0:T(8,128)(2,1)} %cot_ref.3) | copy-start | bytes 2359300
  40.1 2.2 %collective-permute-start.5 = (f32[1152,128]{1,0:T(8,128)S(1)}, f32[1152,128]{1,0:T(8,128)S(1)}, u32[]{:S(2)}, u32[]{:S(2)}) collective-permute-start(f32[1152,128]{1,0:T(8,128)S(1)} %get-tuple-element.22), channel_id=1, source_target_pairs={{0,1},{1,0},{2,3},{3,2},{4,5},{5,4},{6,7},{7,6},{8,9},{9,8},{10,11... | collective-permute-start | bytes 1769480 | tf_op jit(solution)/shard_map/ppermute | solution.py:67
  43.2 20.2 %all-to-all-start.1 = ((f32[64,9,2,128]{3,2,1,0:T(2,128)}), f32[64,9,2,128]{3,2,1,0:T(2,128)S(1)}, u32[]{:S(2)}, u32[]{:S(2)}) async-start(f32[64,9,2,128]{3,2,1,0:T(2,128)} %bitcast.14), calls=%async_computation.1 | async-start | bytes 1179648 | tf_op jit(solution)/shard_map/all_to_all | solution.py:70

commit v6 on v5

--- a/solution.py
+++ b/solution.py
@@ -11,6 +11,7 @@
 AXES = ("lat", "lon")
 BF16 = jnp.bfloat16
 F32 = jnp.float32
+SPREAD_LIMIT = 60 * 1024 * 1024
 PREP_LIMIT = 4 << 20
 MIDDLE_LIMIT = 12 << 20
 FINAL_LIMIT = 12 << 20
@@ -24,9 +25,17 @@
     return lax.ppermute(sent, axis, pairs + [(j, i) for i, j in pairs])
 
 
-def spread_kernel(first_ref, second_ref, out_ref, mixed_ref):
+def spread_kernel(first_ref, second_ref, out_ref, kernel_ref, mixed_ref, sems):
     rows, _ = first_ref.shape
-    first, second = first_ref[...].astype(F32), second_ref[...].astype(F32)
+    loads = [
+        pltpu.make_async_copy(source, kernel_ref.at[i], sems.at[i])
+        for i, source in enumerate((first_ref, second_ref))
+    ]
+    for load in loads:
+        load.start()
+    for load in loads:
+        load.wait()
+    first, second = kernel_ref[0].astype(F32), kernel_ref[1].astype(F32)
     blocks = mixed_ref.shape[0] // (2 * rows)
     for block in range(blocks):
         at = 2 * rows * block
@@ -43,10 +52,14 @@
     return pl.pallas_call(
         spread_kernel,
         out_shape=jax.ShapeDtypeStruct((2 * rows * count, chans), BF16),
-        in_specs=[whole] * 2,
+        in_specs=[pl.BlockSpec(memory_space=pl.ANY)] * 2,
         out_specs=whole,
-        scratch_shapes=[pltpu.VMEM((2 * rows * min(8, count), chans), F32)],
-        compiler_params=pltpu.CompilerParams(vmem_limit_bytes=4 << 20),
+        scratch_shapes=[
+            pltpu.VMEM((2, rows, chans), BF16),
+            pltpu.VMEM((2 * rows * min(8, count), chans), F32),
+            pltpu.SemaphoreType.DMA((2,)),
+        ],
+        compiler_params=pltpu.CompilerParams(vmem_limit_bytes=SPREAD_LIMIT),
     )(w_first, w_second)
 
 
@@ -112,6 +125,24 @@
 
 def paired(first, second):
     return jnp.concatenate([part for both in zip(first, second) for part in both], 1)
+
+
+def stage_kernel(feat_ref, cot_ref, feat_out_ref, cot_out_ref):
+    feat_out_ref[...] = feat_ref[...]
+    cot_out_ref[...] = cot_ref[...]
+
+
+def stage(features, cotangent):
+    whole = pl.BlockSpec(memory_space=pltpu.VMEM)
+    out = jax.ShapeDtypeStruct(features.shape, BF16)
+    return pl.pallas_call(
+        stage_kernel,
+        out_shape=(out, out),
+        in_specs=[whole] * 2,
+        out_specs=(whole, whole),
+        compiler_params=pltpu.CompilerParams(vmem_limit_bytes=PREP_LIMIT),
+        cost_estimate=pl.CostEstimate(flops=1 << 30, bytes_accessed=4 << 20, transcendentals=0),
+    )(features, cotangent)
 
 
 def inner_kernel(feat_ref, cot_ref, tail_ref, taps_ref, cells_ref):
@@ -148,12 +179,12 @@
 
 
 def outer_kernel(
-    place_ref, even_ref, odd_ref, near_ref, taps_ref, cells_ref
+    even_ref, odd_ref, near_ref, taps_ref, cells_ref
 ):
     pairs = near_ref.shape[1]
     chans = even_ref.shape[3]
     cols = cells_ref.shape[3] // 2
-    odd = place_ref[3] == 1
+    odd = lax.axis_index("lat") % 2 == 1
 
     def whole(first_ref, second_ref, at):
         return jnp.where(odd, first_ref[at].astype(F32), second_ref[at].astype(F32)).astype(BF16)
@@ -175,7 +206,7 @@
         cells_ref[field, 1] = jnp.concatenate([cell[:cols] for cell in cells], 0).T
 
 
-def outer(place, rims, near, cols):
+def outer(rims, near, cols):
     _, _, width, chans = rims[0].shape
     whole = pl.BlockSpec(memory_space=pltpu.VMEM)
     return pl.pallas_call(
@@ -184,11 +215,11 @@
             jax.ShapeDtypeStruct((2, 2, width, 6 * chans), BF16),
             jax.ShapeDtypeStruct((2, 2, 6 * chans, 2 * cols), BF16),
         ),
-        in_specs=[pl.BlockSpec(memory_space=pltpu.SMEM)] + [whole] * 3,
+        in_specs=[whole] * 3,
         out_specs=(whole, whole),
         compiler_params=pltpu.CompilerParams(vmem_limit_bytes=PREP_LIMIT),
         cost_estimate=pl.CostEstimate(flops=1 << 30, bytes_accessed=4 << 20, transcendentals=0),
-    )(place, *rims, near)
+    )(*rims, near)
 
 
 def tap_rows(a, b, chans):
@@ -235,7 +266,7 @@
 
 
 def middle_kernel(
-    own_rows, place_ref, mine_ref, other_ref, inner_taps_ref, inner_cells_ref, outer_taps_ref, outer_cells_ref,
+    own_rows, mine_ref, other_ref, inner_taps_ref, inner_cells_ref, outer_taps_ref, outer_cells_ref,
     keep_ref, send_ref, back_ref, one_ref,
     mixed_ref, wide_ref, sums_ref, two_ref, plain_ref, turned_ref, slope_ref, act_ref, own_ref,
 ):
@@ -243,7 +274,8 @@
     chans = lanes // 2
     cols = width - 16
     taps = one_ref.shape[0]
-    core = place_ref[0]
+    core = lax.axis_index(AXES) % 2
+    lat = lax.axis_index("lat")
     mixed_ref[0] = mine_ref[...].astype(F32)
     mixed_ref[1] = other_ref[...].astype(F32)
     for g in range(mine_ref.shape[0] // own_rows):
@@ -291,9 +323,9 @@
                 if c + p > 0:
                     out_ref[at - cols : at, chans:] = rows[:, :chans]
             if c + p == 0:
-                part = jnp.where((lane < chans) & (place_ref[1] == 1), 0.0, part.astype(F32)).astype(BF16)
+                part = jnp.where((lane < chans) & (lat == 0), 0.0, part.astype(F32)).astype(BF16)
             if c + p == pairs - 1:
-                part = jnp.where((lane >= chans) & (place_ref[2] == 1), 0.0, part.astype(F32)).astype(BF16)
+                part = jnp.where((lane >= chans) & (lat == lax.axis_size("lat") - 1), 0.0, part.astype(F32)).astype(BF16)
             back_ref[c + p] = part
     seconds = [plain(cells_of(1, d), act_ref[...]) for d in range(2)]
     firsts = [plain(cells_of(0, d), own_ref[...]) for d in range(2)]
@@ -322,7 +354,7 @@
         send_ref[out] = sums_ref[pl.ds(own_rows * (2 * g + 1 - core), own_rows)]
 
 
-def middle(place, both, inner_parts, outer_parts, own_rows):
+def middle(both, inner_parts, outer_parts, own_rows):
     inner_taps, inner_cells = inner_parts
     outer_taps, outer_cells = outer_parts
     pairs = inner_taps.shape[1] + 1
@@ -340,7 +372,7 @@
             jax.ShapeDtypeStruct((pairs, width, lanes), BF16),
             jax.ShapeDtypeStruct((rows // 2, chans), BF16),
         ),
-        in_specs=[pl.BlockSpec(memory_space=pltpu.SMEM)] + [whole] * 6,
+        in_specs=[whole] * 6,
         out_specs=(whole,) * 4,
         scratch_shapes=[
             pltpu.VMEM((2, rows // 2, chans), F32),
@@ -354,7 +386,7 @@
             pltpu.VMEM((cells, lanes), BF16),
         ],
         compiler_params=pltpu.CompilerParams(vmem_limit_bytes=MIDDLE_LIMIT),
-    )(place, *both, inner_taps, inner_cells, outer_taps, outer_cells)
+    )(*both, inner_taps, inner_cells, outer_taps, outer_cells)
 
 
 def final_kernel(one_ref, back_ref, cot_ref, out_ref, turned_ref, taps_ref):
@@ -418,18 +450,11 @@
         first = lat_odd ^ (turn == 1)
         sent = jnp.concatenate([edges(0, first), edge(tail, 1, first)], 2)
         rims[turn] = swap(sent, "lat", turn, False)
-    place = jnp.stack(
-        [
-            (lax.axis_index(AXES) % 2).astype(jnp.int32),
-            (lat == 0).astype(jnp.int32),
-            (lat == lax.axis_size("lat") - 1).astype(jnp.int32),
-            lat_odd.astype(jnp.int32),
-        ]
-    )
+    staged = stage(features, cotangent)
     _, own_tail = lax.optimization_barrier((both[0], tail))
-    inner_parts = inner(features, cotangent, own_tail)
-    outer_parts = outer(place, rims, inner_parts[0], cols)
-    keep, send, back, one = middle(place, both, inner_parts, outer_parts, 2 * w_first.shape[0])
+    inner_parts = inner(*staged, own_tail)
+    outer_parts = outer(rims, inner_parts[0], cols)
+    keep, send, back, one = middle(both, inner_parts, outer_parts, 2 * w_first.shape[0])
     grads = scatter_sums(keep, send)
     return final(one, back, cotangent), *grads
 

time: 65.2 us -> 65.7 us (level)
  waiting for transfers between devices: 15 us -> 16.5 us
  local copies, waits for them, and re-layouts: 5.67 us -> 4.28 us
  starting transfers between devices: 27.8 us -> 28.5 us
    ppermute x4, waiting for transfers between devices: 0.01 us -> 4.09 us  [swap(): return lax.ppermute(sent, axis, pairs + [(j, i) for i, j in pairs])]
    all_to_all x1, waiting for transfers between devices: 2.91 us -> 0.01 us  [gather_kernels(): lax.all_to_all(sent, AXES, 0, 0, tiled=True, axis_index_groups=groups)]
    unnamed x10 -> x6, local copies, waits for them, and re-layouts: 3.65 us -> 2.27 us
    all_to_all x1, starting transfers between devices: 7.44 us -> 8.59 us  [scatter_sums(): lax.all_to_all(parts, AXES, 0, 0, tiled=True, axis_index_groups=groups)]
    pallas_call x1, Pallas kernels: 0.75 us -> 1.46 us  [spread(): pl.pallas_call(spread_kernel, out_shape=jax.ShapeDtypeStruct((2 * rows *...]
where the time goes in v6:
time: 65.7 us; the launch traced here: 64.6 us
  starting transfers between devices  28.5 us (43%)
  waiting for transfers between devices  16.5 us (25%)
  Pallas kernels  14.3 us (22%)
  local copies, waits for them, and re-layouts  4.28 us (7%)
  between operations  0.85 us (1%)
    ppermute x4, starting transfers between devices, swap(): return lax.ppermute(sent, axis, pairs + [(j, i) for i, j in pairs])  11.2 us
    all_to_all x1, waiting for transfers between devices, scatter_sums(): lax.all_to_all(parts, AXES, 0, 0, tiled=True, axis_index_groups=groups)  10.4 us
    all_to_all x1, starting transfers between devices, scatter_sums(): lax.all_to_all(parts, AXES, 0, 0, tiled=True, axis_index_groups=groups)  8.59 us
    all_to_all x1, starting transfers between devices, gather_kernels(): lax.all_to_all(sent, AXES, 0, 0, tiled=True, axis_index_groups=groups)  8.59 us
    pallas_call x1, Pallas kernels, middle(): pl.pallas_call(functools.partial(middle_kernel, own_rows), out_shape=(jax...  6.1 us
    ppermute x4, waiting for transfers between devices, swap(): return lax.ppermute(sent, axis, pairs + [(j, i) for i, j in pairs])  4.09 us
    pallas_call x1, Pallas kernels, final(): pl.pallas_call(final_kernel, out_shape=jax.ShapeDtypeStruct(cotangent.sha...  2.38 us
    unnamed x6, local copies, waits for them, and re-layouts  2.27 us
  transfers between devices with their start and end apart: 8, of which 3 were waited for; matrix products, arithmetic and copies ran while one was open for 2% of the time, Pallas kernels for 10%

profile of v6, /device:TPU:6, one launch (start us, length us, event | category | flops | bytes accessed | tf_op | source)
XLA Modules:
  0.0 64.6 jit_solution(2351782504052057541)
XLA Ops:
  0.6 0.9 %dynamic-slice_bitcast_fusion.6 = (bf16[1,16,2,128]{3,2,1,0:T(2,128)(2,1)S(1)}, bf16[1,16,2,128]{3,2,1,0:T(2,128)(2,1)S(1)}, bf16[1,16,2,128]{3,2,1,0:T(2,128)(2,1)S(1)}, bf16[1,16,2,128]{3,2,1,0:T(2,128)(2,1)S(1)}) fusion(bf16[16,192,128]{2,1,0:T(8,128)(2,1)} %cot_ref.3, s32[]{:T(128)S(6)} %select_n.54, s32[]{:T(128)S(6)} %select_n.55, ...), kind=kLoop, calls=%fused_computation.13 | loop fusion | bytes 65544 | tf_op jit(solution)/shard_map/stack | solution.py:440
  1.5 0.1 collective-permute-start.2
  1.7 4.5 %collective-permute-start.1 = (bf16[2,16,2,128]{3,2,1,0:T(2,128)(2,1)S(1)}, bf16[2,16,2,128]{3,2,1,0:T(2,128)(2,1)S(1)}, u32[]{:S(2)}, u32[]{:S(2)}) collective-permute-start(bf16[2,16,2,128]{3,2,1,0:T(2,128)(2,1)S(1)} %pad_maximum_fusion.3), channel_id=1, source_target_pairs={{1,2},{3,4},{5,6},{7,8},{9,10},{11,12},{13,14},{15,0},{2,1},{4,3},... | collective-permute-start | bytes 49160 | tf_op jit(solution)/shard_map/ppermute | solution.py:25
  6.2 1.5 %shard_map.67 = bf16[1152,128]{1,0:T(8,128)(2,1)} custom-call(bf16[9,128]{1,0:T(8,128)(2,1)} %first_ref.1, bf16[9,128]{1,0:T(8,128)(2,1)} %second_ref.1), custom_call_target="tpu_custom_call" | custom-call | tf_op jit(solution)/shard_map/pallas_call | solution.py:52
  7.7 8.6 %all-to-all-start = ((bf16[64,9,2,128]{3,2,1,0:T(2,128)(2,1)}), bf16[64,9,2,128]{3,2,1,0:T(2,128)(2,1)S(1)}, u32[]{:S(2)}, u32[]{:S(2)}) async-start(bf16[64,9,2,128]{3,2,1,0:T(2,128)(2,1)} %bitcast.27), calls=%async_computation | async-start | bytes 589824 | tf_op jit(solution)/shard_map/all_to_all | solution.py:71
  16.3 1.1 %dynamic-slice_bitcast_fusion = (bf16[1,2,192,128]{3,2,1,0:T(8,128)(2,1)S(1)}, bf16[1,2,192,128]{3,2,1,0:T(8,128)(2,1)S(1)}, bf16[1,2,192,128]{3,2,1,0:T(8,128)(2,1)S(1)}, bf16[1,2,192,128]{3,2,1,0:T(8,128)(2,1)S(1)}) fusion(bf16[16,192,128]{2,1,0:T(8,128)(2,1)} %cot_ref.3, s32[]{:T(128)S(6)} %select_n.60, s32[]{:T(128)S(6)} %select_n.59, ...), kind=kLoop, calls=%fused_computation.3 | loop fusion | bytes 786440 | tf_op jit(solution)/shard_map/stack | solution.py:440
  17.4 0.0 copy-start
  17.4 1.1 %copy-done = bf16[16,192,128]{2,1,0:T(8,128)(2,1)S(1)} copy-done((bf16[16,192,128]{2,1,0:T(8,128)(2,1)S(1)}, bf16[16,192,128]{2,1,0:T(8,128)(2,1)}, u32[]{:S(2)}) %copy-start) | copy-done | bytes 786456
  18.5 0.0 copy-start.1
  18.5 1.1 %copy-done.1 = bf16[16,192,128]{2,1,0:T(8,128)(2,1)S(1)} copy-done((bf16[16,192,128]{2,1,0:T(8,128)(2,1)S(1)}, bf16[16,192,128]{2,1,0:T(8,128)(2,1)}, u32[]{:S(2)}) %copy-start.1) | copy-done | bytes 786456
  19.6 0.1 shard_map.68
  19.8 0.1 pad.7.clone
  19.8 0.0 collective-permute-done.2
  19.8 0.0 collective-permute-done.1
  19.9 0.1 pad_maximum_fusion.2.tail_ref
  20.0 0.9 %collective-permute-start.3 = (bf16[2,2,208,128]{3,2,1,0:T(8,128)(2,1)S(1)}, bf16[2,2,208,128]{3,2,1,0:T(8,128)(2,1)S(1)}, u32[]{:S(2)}, u32[]{:S(2)}) collective-permute-start(bf16[2,2,208,128]{3,2,1,0:T(8,128)(2,1)S(1)} %pad_maximum_fusion), channel_id=1, source_target_pairs={{0,16},{32,48},{64,80},{96,112},{16,0},{48,32},{80,64},{112,96},{1... | collective-permute-start | bytes 638984 | tf_op jit(solution)/shard_map/ppermute | solution.py:25
  20.9 5.6 %collective-permute-start.4 = (bf16[2,2,208,128]{3,2,1,0:T(8,128)(2,1)S(1)}, bf16[2,2,208,128]{3,2,1,0:T(8,128)(2,1)S(1)}, u32[]{:S(2)}, u32[]{:S(2)}) collective-permute-start(bf16[2,2,208,128]{3,2,1,0:T(8,128)(2,1)S(1)} %pad_maximum_fusion.1), channel_id=1, source_target_pairs={{16,32},{48,64},{80,96},{32,16},{64,48},{96,80},{17,33},{49,65},{8... | collective-permute-start | bytes 638984 | tf_op jit(solution)/shard_map/ppermute | solution.py:25
  26.6 0.0 all-to-all-done
  26.6 0.1 collective-permute-start
  26.7 2.0 %shard_map.69 = (bf16[2,8,208,768]{3,2,1,0:T(8,128)(2,1)S(1)}, bf16[2,2,768,1152]{3,2,1,0:T(8,128)(2,1)S(1)}) custom-call(bf16[16,192,128]{2,1,0:T(8,128)(2,1)S(1)} %get-tuple-element.16.feat_ref, bf16[16,192,128]{2,1,0:T(8,128)(2,1)S(1)} %get-tuple-element.17.cot_ref, bf16[2,16,16,128]{3,2,1,0:T(8,128)(2,1)S(1)} %pad_maximum_fusion.2.tail_ref), custom_call_target="tpu_custom_call" | custom-call | flops 4294967296 | bytes 16777216 | tf_op jit(solution)/shard_map/pallas_call | solution.py:168
  28.7 0.0 collective-permute-done.3.even_ref
  28.7 4.1 %collective-permute-done.4.odd_ref = bf16[2,2,208,128]{3,2,1,0:T(8,128)(2,1)S(1)} collective-permute-done((bf16[2,2,208,128]{3,2,1,0:T(8,128)(2,1)S(1)}, bf16[2,2,208,128]{3,2,1,0:T(8,128)(2,1)S(1)}, u32[]{:S(2)}, u32[]{:S(2)}) %collective-permute-start.4) | collective-permute-done | bytes 213024 | tf_op jit(solution)/shard_map/ppermute | solution.py:25
  32.8 0.7 %shard_map.70 = (bf16[2,2,208,768]{3,2,1,0:T(8,128)(2,1)S(1)}, bf16[2,2,768,384]{3,2,1,0:T(8,128)(2,1)S(1)}) custom-call(bf16[2,2,208,128]{3,2,1,0:T(8,128)(2,1)S(1)} %collective-permute-done.3.even_ref, bf16[2,2,208,128]{3,2,1,0:T(8,128)(2,1)S(1)} %collective-permute-done.4.odd_ref, bf16[2,8,208,768]{3,2,1,0:T(8,128)(2,1)S(1)} %get-tuple-element.19.near_ref.inner_taps_ref), custom_call_target="tpu_custom_call" | custom-call | flops 1073741824 | bytes 4194304 | tf_op jit(solution)/shard_map/pallas_call | solution.py:212
  33.5 0.0 collective-permute-done.other_ref
  33.5 0.0 copy-start.2
  33.5 6.1 %shard_map.71 = (f32[1152,128]{1,0:T(8,128)S(1)}, f32[1152,128]{1,0:T(8,128)S(1)}, bf16[9,208,256]{2,1,0:T(8,128)(2,1)S(1)}, bf16[1152,128]{1,0:T(8,128)(2,1)S(1)}) custom-call(bf16[1152,128]{1,0:T(8,128)(2,1)S(1)} %bitcast.26, bf16[1152,128]{1,0:T(8,128)(2,1)S(1)} %collective-permute-done.other_ref, ...), custom_call_target="tpu_custom_call" | custom-call | tf_op jit(solution)/shard_map/pallas_call | solution.py:367
  39.6 0.1 collective-permute-start.5
  39.7 2.0 %collective-permute-done.5.got_ref = f32[1152,128]{1,0:T(8,128)S(1)} collective-permute-done((f32[1152,128]{1,0:T(8,128)S(1)}, f32[1152,128]{1,0:T(8,128)S(1)}, u32[]{:S(2)}, u32[]{:S(2)}) %collective-permute-start.5) | collective-permute-done | bytes 589856 | tf_op jit(solution)/shard_map/ppermute | solution.py:80
  41.7 0.9 %shard_map.73 = f32[1152,128]{1,0:T(8,128)} custom-call(f32[1152,128]{1,0:T(8,128)S(1)} %get-tuple-element.25.keep_ref, f32[1152,128]{1,0:T(8,128)S(1)} %collective-permute-done.5.got_ref), custom_call_target="tpu_custom_call" | custom-call | tf_op jit(solution)/shard_map/pallas_call | solution.py:93
  42.6 8.6 %all-to-all-start.1 = ((f32[64,9,2,128]{3,2,1,0:T(2,128)}), f32[64,9,2,128]{3,2,1,0:T(2,128)S(1)}, u32[]{:S(2)}, u32[]{:S(2)}) async-start(f32[64,9,2,128]{3,2,1,0:T(2,128)} %bitcast.10), calls=%async_computation.1 | async-start | bytes 1179648 | tf_op jit(solution)/shard_map/all_to_all | solution.py:83
  51.2 0.0 copy-done.2
  51.2 2.4 %shard_map.72 = bf16[16,192,128]{2,1,0:T(8,128)(2,1)} custom-call(bf16[1152,128]{1,0:T(8,128)(2,1)S(1)} %get-tuple-element.23.one_ref, bf16[9,208,256]{2,1,0:T(8,128)(2,1)S(1)} %get-tuple-element.24.back_ref, bf16[16,192,128]{2,1,0:T(8,128)(2,1)S(1)} %copy-done.2), custom_call_target="tpu_custom_call" | custom-call | flops 4294967296 | bytes 8388608 | tf_op jit(solution)/shard_map/pallas_call | solution.py:415
  53.6 10.4 %all-to-all-done.1 = f32[64,9,2,128]{3,2,1,0:T(2,128)S(1)} async-done(((f32[64,9,2,128]{3,2,1,0:T(2,128)}), f32[64,9,2,128]{3,2,1,0:T(2,128)S(1)}, u32[]{:S(2)}, u32[]{:S(2)}) %all-to-all-start.1) | async-done | bytes 589856 | tf_op jit(solution)/shard_map/all_to_all | solution.py:83
  64.0 0.6 shard_map.74
  (7 shorter events, 0.1 us)
Async XLA Ops:
  1.5 18.3 %collective-permute-start.2 = (bf16[2,16,2,128]{3,2,1,0:T(2,128)(2,1)S(1)}, bf16[2,16,2,128]{3,2,1,0:T(2,128)(2,1)S(1)}, u32[]{:S(2)}, u32[]{:S(2)}) collective-permute-start(bf16[2,16,2,128]{3,2,1,0:T(2,128)(2,1)S(1)} %pad_maximum_fusion.4), channel_id=1, source_target_pairs={{0,1},{2,3},{4,5},{6,7},{8,9},{10,11},{12,13},{14,15},{1,0},{3,2},... | collective-permute-start | bytes 49160 | tf_op jit(solution)/shard_map/ppermute | solution.py:25
  1.7 18.2 %collective-permute-start.1 = (bf16[2,16,2,128]{3,2,1,0:T(2,128)(2,1)S(1)}, bf16[2,16,2,128]{3,2,1,0:T(2,128)(2,1)S(1)}, u32[]{:S(2)}, u32[]{:S(2)}) collective-permute-start(bf16[2,16,2,128]{3,2,1,0:T(2,128)(2,1)S(1)} %pad_maximum_fusion.3), channel_id=1, source_target_pairs={{1,2},{3,4},{5,6},{7,8},{9,10},{11,12},{13,14},{15,0},{2,1},{4,3},... | collective-permute-start | bytes 49160 | tf_op jit(solution)/shard_map/ppermute | solution.py:25
  7.7 18.9 %all-to-all-start = ((bf16[64,9,2,128]{3,2,1,0:T(2,128)(2,1)}), bf16[64,9,2,128]{3,2,1,0:T(2,128)(2,1)S(1)}, u32[]{:S(2)}, u32[]{:S(2)}) async-start(bf16[64,9,2,128]{3,2,1,0:T(2,128)(2,1)} %bitcast.27), calls=%async_computation | async-start | bytes 589824 | tf_op jit(solution)/shard_map/all_to_all | solution.py:71
  17.4 1.1 %copy-start = (bf16[16,192,128]{2,1,0:T(8,128)(2,1)S(1)}, bf16[16,192,128]{2,1,0:T(8,128)(2,1)}, u32[]{:S(2)}) copy-start(bf16[16,192,128]{2,1,0:T(8,128)(2,1)} %feat_ref.1) | copy-start | bytes 2359300
  18.5 1.1 %copy-start.1 = (bf16[16,192,128]{2,1,0:T(8,128)(2,1)S(1)}, bf16[16,192,128]{2,1,0:T(8,128)(2,1)}, u32[]{:S(2)}) copy-start(bf16[16,192,128]{2,1,0:T(8,128)(2,1)} %cot_ref.3) | copy-start | bytes 2359300
  20.0 8.7 %collective-permute-start.3 = (bf16[2,2,208,128]{3,2,1,0:T(8,128)(2,1)S(1)}, bf16[2,2,208,128]{3,2,1,0:T(8,128)(2,1)S(1)}, u32[]{:S(2)}, u32[]{:S(2)}) collective-permute-start(bf16[2,2,208,128]{3,2,1,0:T(8,128)(2,1)S(1)} %pad_maximum_fusion), channel_id=1, source_target_pairs={{0,16},{32,48},{64,80},{96,112},{16,0},{48,32},{80,64},{112,96},{1... | collective-permute-start | bytes 638984 | tf_op jit(solution)/shard_map/ppermute | solution.py:25
  20.9 11.8 %collective-permute-start.4 = (bf16[2,2,208,128]{3,2,1,0:T(8,128)(2,1)S(1)}, bf16[2,2,208,128]{3,2,1,0:T(8,128)(2,1)S(1)}, u32[]{:S(2)}, u32[]{:S(2)}) collective-permute-start(bf16[2,2,208,128]{3,2,1,0:T(8,128)(2,1)S(1)} %pad_maximum_fusion.1), channel_id=1, source_target_pairs={{16,32},{48,64},{80,96},{32,16},{64,48},{96,80},{17,33},{49,65},{8... | collective-permute-start | bytes 638984 | tf_op jit(solution)/shard_map/ppermute | solution.py:25
  26.6 6.9 %collective-permute-start = (bf16[1152,128]{1,0:T(8,128)(2,1)S(1)}, bf16[1152,128]{1,0:T(8,128)(2,1)S(1)}, u32[]{:S(2)}, u32[]{:S(2)}) collective-permute-start(bf16[1152,128]{1,0:T(8,128)(2,1)S(1)} %bitcast.25), channel_id=1, source_target_pairs={{0,1},{1,0},{2,3},{3,2},{4,5},{5,4},{6,7},{7,6},{8,9},{9,8},{10,11... | collective-permute-start | bytes 884744 | tf_op jit(solution)/shard_map/ppermute | solution.py:73
  33.5 17.7 %copy-start.2 = (bf16[16,192,128]{2,1,0:T(8,128)(2,1)S(1)}, bf16[16,192,128]{2,1,0:T(8,128)(2,1)}, u32[]{:S(2)}) copy-start(bf16[16,192,128]{2,1,0:T(8,128)(2,1)} %cot_ref.3) | copy-start | bytes 2359300
  39.6 2.1 %collective-permute-start.5 = (f32[1152,128]{1,0:T(8,128)S(1)}, f32[1152,128]{1,0:T(8,128)S(1)}, u32[]{:S(2)}, u32[]{:S(2)}) collective-permute-start(f32[1152,128]{1,0:T(8,128)S(1)} %get-tuple-element.26), channel_id=1, source_target_pairs={{0,1},{1,0},{2,3},{3,2},{4,5},{5,4},{6,7},{7,6},{8,9},{9,8},{10,11... | collective-permute-start | bytes 1769480 | tf_op jit(solution)/shard_map/ppermute | solution.py:80
  42.6 21.4 %all-to-all-start.1 = ((f32[64,9,2,128]{3,2,1,0:T(2,128)}), f32[64,9,2,128]{3,2,1,0:T(2,128)S(1)}, u32[]{:S(2)}, u32[]{:S(2)}) async-start(f32[64,9,2,128]{3,2,1,0:T(2,128)} %bitcast.10), calls=%async_computation.1 | async-start | bytes 1179648 | tf_op jit(solution)/shard_map/all_to_all | solution.py:83
